TPU v7x, 32 devices: a whole 2x2x4 slice. The times are simulated.
32 devices in a mesh: outer: 4 (over y, core), atoms: 8 (over z, x).
Axes of the slice: x: 2, y: 2, z: 4, core: 2. Of those that a mesh axis runs over, the one named last changes fastest.
Arguments:
- features: float32 [32768, 128], P(('outer', 'atoms')), may hold values from -6 to 6
- positions: int32 [3, 32768], P(None, ('outer', 'atoms')), may hold values from 0 to 262143
- wavevectors: int32 [3, 768], replicated, may hold values from -6 to 6
- w_value: float32 [2, 128, 128], replicated, may hold values from -0.5 to 0.5
- freq_filter: float32 [2, 768, 128], replicated, may hold values from 0.05 to 1
- norm_gain: float32 [2, 128], replicated, may hold values from 0.1 to 1.9
- w_hidden: float32 [2, 128, 128], replicated, may hold values from -0.5 to 0.5
- b_hidden: float32 [2, 128], replicated, may hold values from -4 to 4
- w_output: float32 [2, 128, 128], replicated, may hold values from -0.5 to 0.5
Outputs:
- updated: float32 [32768, 128], P(('outer', 'atoms'))
All inputs are finite; a program needn't handle non-finite values.
Results may differ from a plain program's by a relative error of at most 0.0003.
Values sent between devices are 32-bit elements; how exact they have to be, the bound alone decides.
No kernel may reach another device: no remote copies, remote signals or barrier semaphores. Data moves between devices by JAX's collectives and lax.ppermute only.
A program may use at most 64 MiB of HBM per device.

v0:
```python
import jax
import jax.numpy as jnp
from jax import lax
from jax.experimental import pallas as pl
from jax.experimental.pallas import tpu as pltpu
from jax.sharding import PartitionSpec as P

axes = ("outer", "atoms")
first_limit, table_limit, block_limit = 10 * 2**20, 8 * 2**20, 10 * 2**20
turn_bits = 18
half_sin = (0.10982699, -0.84611289, 3.60635441, -7.3082457, 4.44288292)
half_cos = (0.31069819, -1.88356299, 5.73946117, -6.97885099, 1.4142135)
to_integer = 1.5 * 2.0**23
f32, bf16 = jnp.float32, jnp.bfloat16


class Layout:
    def __init__(self, mesh):
        self.outer, self.atoms = mesh.shape["outer"], mesh.shape["atoms"]
        self.pair = 2 if self.outer % 2 == 0 else 1
        self.high = self.outer // self.pair
        self.low = 2 if self.atoms % 2 == 0 else 1
        self.line = self.atoms // self.low
        self.square = self.high * self.low
        self.chunks = self.pair * self.square

    def split(self, index):
        outer, atoms = index // self.atoms, index % self.atoms
        return outer // self.pair, outer % self.pair, atoms // self.low, atoms % self.low

    def join(self, high, pair, line, low):
        return (high * self.pair + pair) * self.atoms + line * self.low + low

    def moved(self, index, d_high, d_pair, d_line, d_low):
        high, pair, line, low = self.split(index)
        return self.join(
            (high + d_high) % self.high,
            (pair + d_pair) % self.pair,
            (line + d_line) % self.line,
            (low + d_low) % self.low,
        )

    def send(self, value, **steps):
        d = dict(d_high=0, d_pair=0, d_line=0, d_low=0) | steps
        count = self.outer * self.atoms
        return lax.ppermute(value, axes, [(i, self.moved(i, **d)) for i in range(count)])

    def exchange(self, value, bits):
        count = self.outer * self.atoms
        pairs = []
        for i in range(count):
            high, pair, line, low = self.split(i)
            pairs.append((i, self.join(high, pair, line ^ bits, low)))
        return lax.ppermute(value, axes, pairs)

    def owned(self):
        outer, atoms = lax.axis_index("outer"), lax.axis_index("atoms")
        return outer % self.pair, outer // self.pair, atoms % self.low

    def chunk_of(self, d_pair, d_high, d_low):
        pair, high, low = self.owned()
        pair = (pair + d_pair) % self.pair
        high = (high + d_high) % self.high
        low = (low + d_low) % self.low
        return (pair * self.high + high) * self.low + low

    def offsets(self):
        return [(p, h, w) for p in range(self.pair) for h in range(self.high) for w in range(self.low)]


def total(layout, parts, scale):
    squares = [(h, w) for h in range(layout.high) for w in range(layout.low)]
    held = {}
    for h, w in squares[1:] + squares[:1]:
        value = parts[0, h, w]
        for p in range(1, layout.pair):
            value = value + layout.send(parts[p, h, w], d_pair=p)
        held[h, w] = value
    own = held[0, 0]
    for h, w in squares[1:]:
        own = own + layout.send(held[h, w], d_high=h, d_low=w)
    summed = own
    if layout.line <= 4 and layout.line & (layout.line - 1) == 0:
        for d in range(layout.line - 1, 0, -1):
            summed = summed + layout.exchange(own, d)
    elif layout.line & (layout.line - 1) == 0:
        span = 1
        while span < layout.line:
            summed = summed + layout.exchange(summed, span)
            span *= 2
    else:
        for d in range(1, layout.line):
            summed = summed + layout.send(own, d_line=d)
    own = summed * scale
    out = {}
    for h, w in squares:
        value = own
        if (h, w) != (0, 0):
            value = layout.send(own, d_high=-h, d_low=-w)
        out[0, h, w] = value
        for p in range(1, layout.pair):
            out[p, h, w] = layout.send(value, d_pair=-p)
    return out


def halves(value):
    high = value.astype(bf16)
    return high, (value - high.astype(f32)).astype(bf16)


def matmul(left, right):
    return jnp.dot(left, right, preferred_element_type=f32)


def paired(value):
    high, low = halves(value)
    return jnp.concatenate([high, low], axis=1)


def product(left, right):
    width = right.shape[1]
    left_high, left_low = halves(left)
    pair = paired(right)
    both = matmul(left_high, pair)
    return both[:, :width] + both[:, width:] + matmul(left_low, pair[:, :width])


def digits(position):
    return (
        (position >> 12).astype(f32) * 2.0**-6,
        ((position >> 6) & 63).astype(f32) * 2.0**-12,
        (position & 63).astype(f32) * 2.0**-turn_bits,
    )


def operands(waves_ref, positions_ref, wave_rows, digit_rows):
    wave_rows[...] = jnp.zeros_like(wave_rows)
    digit_rows[...] = jnp.zeros_like(digit_rows)
    waves = waves_ref[...].astype(f32)
    for n, digit in enumerate(digits(positions_ref[...])):
        wave_rows[3 * n : 3 * n + 3, :] = waves
        digit_rows[3 * n : 3 * n + 3, :] = digit


def contract_rows(left, right):
    return lax.dot_general(
        left.astype(bf16), right.astype(bf16), (((0,), (0,)), ((), ())), preferred_element_type=f32
    )


def horner(coefficients, u):
    value = coefficients[0] * u + coefficients[1]
    for c in coefficients[2:]:
        value = value * u + c
    return value


def fill_tables(turns_ref, cos_high, cos_low, sin_high, sin_low):
    rows, columns = turns_ref.shape
    step, width = 32, 256

    def body(n, carry):
        here = pl.ds(pl.multiple_of(n * step, step), step)
        for at in range(0, columns, width):
            lanes = slice(at, at + width)
            turns = turns_ref[here, lanes]
            t = turns - ((turns + to_integer) - to_integer)
            u = t * t
            s = horner(half_sin, u) * t
            c = horner(half_cos, u)
            cos_high[here, lanes], cos_low[here, lanes] = halves(1.0 - s * s)
            sin_high[here, lanes], sin_low[here, lanes] = halves(s * c)
        return carry

    lax.fori_loop(0, rows // step, body, 0)


def project(layout, tables, pair, chunk_refs, rows):
    width = pair.shape[1] // 2
    for offset, chunk_ref in zip(layout.offsets(), chunk_refs):
        here = pl.ds(pl.multiple_of(layout.chunk_of(*offset) * rows, rows), rows)
        for n in range(2):
            both = matmul(tables[2 * n][here, :], pair)
            rest = matmul(tables[2 * n + 1][here, :], pair[:, :width])
            chunk_ref[n * rows : (n + 1) * rows, :] = both[:, :width] + both[:, width:] + rest


def first_kernel(layout, rows, *refs):
    sources, refs = refs[:4], refs[4:]
    tables, chunks = refs[:4], refs[4 : 4 + layout.chunks]
    wave_rows, digit_rows, turns, waves, positions, features, w_value, arrived = refs[4 + layout.chunks :]
    copies = [
        pltpu.make_async_copy(source, target, arrived.at[n])
        for n, (source, target) in enumerate(zip(sources, (waves, positions, features, w_value)))
    ]
    for copy in copies:
        copy.start()
    copies[0].wait()
    copies[1].wait()
    operands(waves, positions, wave_rows, digit_rows)
    turns[...] = contract_rows(wave_rows[...], digit_rows[...])
    fill_tables(turns, *tables)
    copies[2].wait()
    copies[3].wait()
    pair = paired(product(features[...], w_value[0]))
    project(layout, tables, pair, chunks, rows)


def atom_table_kernel(layout, rows, waves, positions, freq_filter, *refs):
    tables, scales = refs[:4], refs[4:-3]
    wave_rows, digit_rows, turns = refs[-3:]
    here = pl.ds(pl.multiple_of(layout.chunk_of(0, 0, 0) * rows, rows), rows)
    for block, scale in enumerate(scales):
        scale[:rows, :] = freq_filter[block, here, :]
        scale[rows:, :] = freq_filter[block, here, :]
    operands(waves, positions, wave_rows, digit_rows)
    turns[...] = contract_rows(digit_rows[...], wave_rows[...])
    fill_tables(turns, *tables)


def block_kernel(layout, rows, block, last, *refs):
    chunks_in, refs = refs[: layout.chunks], refs[layout.chunks :]
    atom_tables, refs = refs[:4], refs[4:]
    current_ref, gain, w_hidden, b_hidden, w_output = refs[:5]
    refs = refs[5:]
    if not last:
        w_value, tables, refs = refs[0], refs[1:5], refs[5:]
    current_out, refs = refs[0], refs[1:]
    cos_pair, sin_pair = refs[-2:]
    width = current_ref.shape[1]
    for offset, chunk in zip(layout.offsets(), chunks_in):
        here = pl.ds(pl.multiple_of(layout.chunk_of(*offset) * rows, rows), rows)
        cos_pair[here, :] = paired(chunk[:rows, :])
        sin_pair[here, :] = paired(chunk[rows:, :])
    atoms = current_ref.shape[0]
    step = min(256, atoms)
    for at in range(0, atoms, step):
        here = slice(at, at + step)
        both = matmul(atom_tables[0][here, :], cos_pair[...])
        both = both + matmul(atom_tables[2][here, :], sin_pair[...])
        messages = both[:, :width] + both[:, width:]
        messages = messages + matmul(atom_tables[1][here, :], cos_pair[:, :width])
        messages = messages + matmul(atom_tables[3][here, :], sin_pair[:, :width])
        mean = jnp.mean(messages * messages, axis=1, keepdims=True)
        normed = messages * lax.rsqrt(mean + 1e-06) * gain[block : block + 1, :]
        hidden = product(normed, w_hidden[block]) + b_hidden[block : block + 1, :]
        hidden = hidden / (1.0 + jnp.exp(-hidden))
        current_out[here, :] = current_ref[here, :] + product(hidden, w_output[block])
    if not last:
        pair = paired(product(current_out[...], w_value[block + 1]))
        project(layout, tables, pair, refs[: layout.chunks], rows)


def call(kernel, outputs, scratch, limit, flops, *inputs, space=pltpu.VMEM):
    return pl.pallas_call(
        kernel,
        in_specs=[pl.BlockSpec(memory_space=space)] * len(inputs),
        out_specs=[pl.BlockSpec(memory_space=pltpu.VMEM)] * len(outputs),
        out_shape=outputs,
        scratch_shapes=scratch,
        compiler_params=pltpu.CompilerParams(vmem_limit_bytes=limit),
        cost_estimate=pl.CostEstimate(flops=flops, bytes_accessed=flops // 200, transcendentals=0),
    )(*inputs)


def local(
    layout, features, positions, wavevectors, w_value, freq_filter, norm_gain, w_hidden, b_hidden, w_output
):
    waves, channels = wavevectors.shape[1], features.shape[1]
    atoms, blocks = features.shape[0], w_value.shape[0]
    rows = waves // layout.chunks
    shape = jax.ShapeDtypeStruct
    chunk = shape((2 * rows, channels), f32)
    index_scratch = [pltpu.VMEM((16, waves), f32), pltpu.VMEM((16, atoms), f32)]
    flops = 12 * waves * atoms * channels
    early = [wavevectors, positions, features, w_value]
    outs = call(
        lambda *refs: first_kernel(layout, rows, *refs),
        [shape((waves, atoms), bf16)] * 4 + [chunk] * layout.chunks,
        index_scratch
        + [pltpu.VMEM((waves, atoms), f32)]
        + [pltpu.VMEM(array.shape, array.dtype) for array in early]
        + [pltpu.SemaphoreType.DMA((len(early),))],
        first_limit,
        flops,
        *early,
        space=pltpu.HBM,
    )
    tables, chunks = outs[:4], outs[4:]
    outs = call(
        lambda *refs: atom_table_kernel(layout, rows, *refs),
        [shape((atoms, waves), bf16)] * 4 + [chunk] * blocks,
        index_scratch + [pltpu.VMEM((atoms, waves), f32)],
        table_limit,
        flops,
        wavevectors,
        positions,
        freq_filter,
    )
    atom_tables, scales = outs[:4], outs[4:]
    current = features
    offsets = layout.offsets()
    for block in range(blocks):
        last = block == blocks - 1
        gathered = total(layout, dict(zip(offsets, chunks)), scales[block])
        inputs = [gathered[o] for o in offsets] + list(atom_tables)
        inputs += [current, norm_gain, w_hidden, b_hidden, w_output]
        if not last:
            inputs += [w_value] + list(tables)
        outs = call(
            lambda *refs, block=block, last=last: block_kernel(layout, rows, block, last, *refs),
            [shape((atoms, channels), f32)] + ([] if last else [chunk] * layout.chunks),
            [pltpu.VMEM((waves, 2 * channels), bf16)] * 2,
            block_limit,
            flops,
            *inputs,
        )
        current, chunks = outs[0], outs[1:]
    return current


def solution(mesh):
    placed = (
        P(("outer", "atoms"), None),
        P(None, ("outer", "atoms")),
        P(),
        P(),
        P(),
        P(),
        P(),
        P(),
        P(),
    )
    layout = Layout(mesh)

    def body(*arguments):
        return local(layout, *arguments)

    return jax.shard_map(
        body, mesh=mesh, in_specs=placed, out_specs=P(("outer", "atoms"), None), check_vma=False
    )
```

profile of v0, /device:TPU:0, one launch (start us, length us, event | category | flops | bytes accessed | tf_op | source)
XLA Modules:
  0.0 80.0 jit_solution(12147503840709162029)
XLA Ops:
  0.0 1.0 %copy-done.2 = f32[1024,128]{1,0:T(8,128)S(1)} copy-done((f32[1024,128]{1,0:T(8,128)S(1)}, f32[1024,128]{1,0:T(8,128)}, u32[]{:S(2)}) %copy-start.2) | copy-done | bytes 524312
  1.0 0.9 %copy-done.4 = f32[2,128,128]{2,1,0:T(8,128)S(1)} copy-done((f32[2,128,128]{2,1,0:T(8,128)S(1)}, f32[2,128,128]{2,1,0:T(8,128)}, u32[]{:S(2)}) %copy-start.4) | copy-done | bytes 131096
  1.9 0.7 copy-done.9
  2.7 0.7 copy-done.11
  3.4 6.9 %shard_map.91 = (bf16[768,1024]{1,0:T(8,128)(2,1)S(1)}, bf16[768,1024]{1,0:T(8,128)(2,1)S(1)}, bf16[768,1024]{1,0:T(8,128)(2,1)S(1)}, bf16[768,1024]{1,0:T(8,128...) custom-call(s32[3,768]{1,0:T(4,128)S(1)} %copy-done.11, ...), custom_call_target="tpu_custom_call" | custom-call | flops 1207959552 | bytes 6039797 | tf_op jit(solution)/shard_map/pallas_call | solution.py:255
  10.3 0.6 collective-permute-start.1
  10.9 0.4 collective-permute-start.5
  11.4 0.4 collective-permute-done.1
  11.8 2.9 %collective-permute-start.2 = (f32[192,128]{1,0:T(8,128)S(1)}, f32[192,128]{1,0:T(8,128)S(1)}, u32[]{:S(2)}, u32[]{:S(2)}) collective-permute-start(f32[192,128]{1,0:T(8,128)S(1)} %add.61), channel_id=1, source_target_pairs={{0,1},{1,0},{2,3},{3,2},{4,5},{5,4},{6,7},{7,6},{8,9},{9,8},{10,11... | collective-permute-start | bytes 294920 | tf_op jit(solution)/shard_map/ppermute | solution.py:46
  14.7 1.6 %collective-permute-start.4 = (f32[192,128]{1,0:T(8,128)S(1)}, f32[192,128]{1,0:T(8,128)S(1)}, u32[]{:S(2)}, u32[]{:S(2)}) collective-permute-start(f32[192,128]{1,0:T(8,128)S(1)} %add.63), channel_id=1, source_target_pairs={{0,16},{1,17},{2,18},{3,19},{4,20},{5,21},{6,22},{7,23},{8,24},{9,... | collective-permute-start | bytes 294920 | tf_op jit(solution)/shard_map/ppermute | solution.py:46
  16.4 1.4 %collective-permute-done.2 = f32[192,128]{1,0:T(8,128)S(1)} collective-permute-done((f32[192,128]{1,0:T(8,128)S(1)}, f32[192,128]{1,0:T(8,128)S(1)}, u32[]{:S(2)}, u32[]{:S(2)}) %collective-permute-start.2) | collective-permute-done | bytes 98336 | tf_op jit(solution)/shard_map/ppermute | solution.py:46
  17.8 2.7 %collective-permute-done.4 = f32[192,128]{1,0:T(8,128)S(1)} collective-permute-done((f32[192,128]{1,0:T(8,128)S(1)}, f32[192,128]{1,0:T(8,128)S(1)}, u32[]{:S(2)}, u32[]{:S(2)}) %collective-permute-start.4) | collective-permute-done | bytes 98336 | tf_op jit(solution)/shard_map/ppermute | solution.py:46
  20.5 1.4 %collective-permute-done.6 = f32[192,128]{1,0:T(8,128)S(1)} collective-permute-done((f32[192,128]{1,0:T(8,128)S(1)}, f32[192,128]{1,0:T(8,128)S(1)}, u32[]{:S(2)}, u32[]{:S(2)}) %collective-permute-start.6) | collective-permute-done | bytes 98336 | tf_op jit(solution)/shard_map/ppermute | solution.py:46
  22.0 1.6 %collective-permute-start.9 = (f32[192,128]{1,0:T(8,128)S(1)}, f32[192,128]{1,0:T(8,128)S(1)}, u32[]{:S(2)}, u32[]{:S(2)}) collective-permute-start(f32[192,128]{1,0:T(8,128)S(1)} %add_add_fusion.1), channel_id=1, source_target_pairs={{0,2},{1,3},{2,0},{3,1},{4,6},{5,7},{6,4},{7,5},{8,10},{9,11},{10,... | collective-permute-start | bytes 294920 | tf_op jit(solution)/shard_map/ppermute | solution.py:54
  23.6 2.6 %collective-permute-start.8 = (f32[192,128]{1,0:T(8,128)S(1)}, f32[192,128]{1,0:T(8,128)S(1)}, u32[]{:S(2)}, u32[]{:S(2)}) collective-permute-start(f32[192,128]{1,0:T(8,128)S(1)} %add_add_fusion.1), channel_id=1, source_target_pairs={{0,4},{1,5},{2,6},{3,7},{4,0},{5,1},{6,2},{7,3},{8,12},{9,13},{10,... | collective-permute-start | bytes 294920 | tf_op jit(solution)/shard_map/ppermute | solution.py:54
  26.5 4.3 %shard_map.92 = (bf16[1024,768]{1,0:T(8,128)(2,1)S(1)}, bf16[1024,768]{1,0:T(8,128)(2,1)S(1)}, bf16[1024,768]{1,0:T(8,128)(2,1)S(1)}, bf16[1024,768]{1,0:T(8,128...) custom-call(s32[3,768]{1,0:T(4,128)S(1)} %copy-done.12, s32[3,1024]{1,0:T(4,128)S(1)} %copy-done.10, ...), custom_call_target="tpu_custom_call" | custom-call | flops 1207959552 | bytes 6039797 | tf_op jit(solution)/shard_map/pallas_call | solution.py:255
  30.8 0.9 %collective-permute-done.8 = f32[192,128]{1,0:T(8,128)S(1)} collective-permute-done((f32[192,128]{1,0:T(8,128)S(1)}, f32[192,128]{1,0:T(8,128)S(1)}, u32[]{:S(2)}, u32[]{:S(2)}) %collective-permute-start.8) | collective-permute-done | bytes 98336 | tf_op jit(solution)/shard_map/ppermute | solution.py:54
  31.6 1.1 %collective-permute-done.7 = f32[192,128]{1,0:T(8,128)S(1)} collective-permute-done((f32[192,128]{1,0:T(8,128)S(1)}, f32[192,128]{1,0:T(8,128)S(1)}, u32[]{:S(2)}, u32[]{:S(2)}) %collective-permute-start.7) | collective-permute-done | bytes 98336 | tf_op jit(solution)/shard_map/ppermute | solution.py:54
  32.8 1.4 %collective-permute-start.12 = (f32[192,128]{1,0:T(8,128)S(1)}, f32[192,128]{1,0:T(8,128)S(1)}, u32[]{:S(2)}, u32[]{:S(2)}) collective-permute-start(f32[192,128]{1,0:T(8,128)S(1)} %add_multiply_fusion.1.refs_0_), channel_id=1, source_target_pairs={{0,17},{1,16},{2,19},{3,18},{4,21},{5,20},{6,23},{7,22},{8,25},{9,... | collective-permute-start | bytes 294920 | tf_op jit(solution)/shard_map/ppermute | solution.py:46
  34.2 1.5 %collective-permute-start.11 = (f32[192,128]{1,0:T(8,128)S(1)}, f32[192,128]{1,0:T(8,128)S(1)}, u32[]{:S(2)}, u32[]{:S(2)}) collective-permute-start(f32[192,128]{1,0:T(8,128)S(1)} %add_multiply_fusion.1.refs_0_), channel_id=1, source_target_pairs={{0,16},{1,17},{2,18},{3,19},{4,20},{5,21},{6,22},{7,23},{8,24},{9,... | collective-permute-start | bytes 294920 | tf_op jit(solution)/shard_map/ppermute | solution.py:46
  35.7 0.6 collective-permute-start.10
  36.3 2.1 %collective-permute-done.12.refs_3_ = f32[192,128]{1,0:T(8,128)S(1)} collective-permute-done((f32[192,128]{1,0:T(8,128)S(1)}, f32[192,128]{1,0:T(8,128)S(1)}, u32[]{:S(2)}, u32[]{:S(2)}) %collective-permute-start.12) | collective-permute-done | bytes 98336 | tf_op jit(solution)/shard_map/ppermute | solution.py:46
  38.4 1.0 %collective-permute-done.11.refs_2_ = f32[192,128]{1,0:T(8,128)S(1)} collective-permute-done((f32[192,128]{1,0:T(8,128)S(1)}, f32[192,128]{1,0:T(8,128)S(1)}, u32[]{:S(2)}, u32[]{:S(2)}) %collective-permute-start.11) | collective-permute-done | bytes 98336 | tf_op jit(solution)/shard_map/ppermute | solution.py:46
  39.4 0.9 %collective-permute-done.10.refs_1_ = f32[192,128]{1,0:T(8,128)S(1)} collective-permute-done((f32[192,128]{1,0:T(8,128)S(1)}, f32[192,128]{1,0:T(8,128)S(1)}, u32[]{:S(2)}, u32[]{:S(2)}) %collective-permute-start.10) | collective-permute-done | bytes 98336 | tf_op jit(solution)/shard_map/ppermute | solution.py:46
  40.4 0.4 collective-permute-done.15.refs_6_
  40.7 0.9 %collective-permute-done.14.refs_5_ = f32[192,128]{1,0:T(8,128)S(1)} collective-permute-done((f32[192,128]{1,0:T(8,128)S(1)}, f32[192,128]{1,0:T(8,128)S(1)}, u32[]{:S(2)}, u32[]{:S(2)}) %collective-permute-start.14) | collective-permute-done | bytes 98336 | tf_op jit(solution)/shard_map/ppermute | solution.py:46
  41.7 5.8 %shard_map.93 = (f32[1024,128]{1,0:T(8,128)S(1)}, f32[192,128]{1,0:T(8,128)S(1)}, f32[192,128]{1,0:T(8,128)S(1)}, f32[192,128]{1,0:T(8,128)S(1)}, f32[192,128]{1...) custom-call(f32[192,128]{1,0:T(8,128)S(1)} %add_multiply_fusion.1.re, ...), custom_call_target="tpu_custom_call" | custom-call | flops 1207959552 | bytes 6039797 | tf_op jit(solution)/shard_map/pallas_call | solution.py:255
  47.7 0.4 collective-permute-start.20
  48.2 0.4 collective-permute-start.17
  48.6 0.3 collective-permute-done.18
  48.8 0.7 collective-permute-start.19
  49.6 1.1 %collective-permute-start.21 = (f32[192,128]{1,0:T(8,128)S(1)}, f32[192,128]{1,0:T(8,128)S(1)}, u32[]{:S(2)}, u32[]{:S(2)}) collective-permute-start(f32[192,128]{1,0:T(8,128)S(1)} %add.73), channel_id=1, source_target_pairs={{0,16},{1,17},{2,18},{3,19},{4,20},{5,21},{6,22},{7,23},{8,24},{9,... | collective-permute-start | bytes 294920 | tf_op jit(solution)/shard_map/ppermute | solution.py:46
  50.7 1.8 %collective-permute-start.23 = (f32[192,128]{1,0:T(8,128)S(1)}, f32[192,128]{1,0:T(8,128)S(1)}, u32[]{:S(2)}, u32[]{:S(2)}) collective-permute-start(f32[192,128]{1,0:T(8,128)S(1)} %add.75), channel_id=1, source_target_pairs={{0,17},{1,16},{2,19},{3,18},{4,21},{5,20},{6,23},{7,22},{8,25},{9,... | collective-permute-start | bytes 294920 | tf_op jit(solution)/shard_map/ppermute | solution.py:46
  52.6 1.4 %collective-permute-done.19 = f32[192,128]{1,0:T(8,128)S(1)} collective-permute-done((f32[192,128]{1,0:T(8,128)S(1)}, f32[192,128]{1,0:T(8,128)S(1)}, u32[]{:S(2)}, u32[]{:S(2)}) %collective-permute-start.19) | collective-permute-done | bytes 98336 | tf_op jit(solution)/shard_map/ppermute | solution.py:46
  53.9 2.6 %collective-permute-done.21 = f32[192,128]{1,0:T(8,128)S(1)} collective-permute-done((f32[192,128]{1,0:T(8,128)S(1)}, f32[192,128]{1,0:T(8,128)S(1)}, u32[]{:S(2)}, u32[]{:S(2)}) %collective-permute-start.21) | collective-permute-done | bytes 98336 | tf_op jit(solution)/shard_map/ppermute | solution.py:46
  56.6 1.5 %collective-permute-start.26 = (f32[192,128]{1,0:T(8,128)S(1)}, f32[192,128]{1,0:T(8,128)S(1)}, u32[]{:S(2)}, u32[]{:S(2)}) collective-permute-start(f32[192,128]{1,0:T(8,128)S(1)} %add_add_fusion), channel_id=1, source_target_pairs={{0,2},{1,3},{2,0},{3,1},{4,6},{5,7},{6,4},{7,5},{8,10},{9,11},{10,... | collective-permute-start | bytes 294920 | tf_op jit(solution)/shard_map/ppermute | solution.py:54
  58.0 1.4 %collective-permute-start.25 = (f32[192,128]{1,0:T(8,128)S(1)}, f32[192,128]{1,0:T(8,128)S(1)}, u32[]{:S(2)}, u32[]{:S(2)}) collective-permute-start(f32[192,128]{1,0:T(8,128)S(1)} %add_add_fusion), channel_id=1, source_target_pairs={{0,4},{1,5},{2,6},{3,7},{4,0},{5,1},{6,2},{7,3},{8,12},{9,13},{10,... | collective-permute-start | bytes 294920 | tf_op jit(solution)/shard_map/ppermute | solution.py:54
  59.4 1.6 %collective-permute-start.24 = (f32[192,128]{1,0:T(8,128)S(1)}, f32[192,128]{1,0:T(8,128)S(1)}, u32[]{:S(2)}, u32[]{:S(2)}) collective-permute-start(f32[192,128]{1,0:T(8,128)S(1)} %add_add_fusion), channel_id=1, source_target_pairs={{0,6},{1,7},{2,4},{3,5},{4,2},{5,3},{6,0},{7,1},{8,14},{9,15},{10,... | collective-permute-start | bytes 294920 | tf_op jit(solution)/shard_map/ppermute | solution.py:54
  61.0 1.1 %collective-permute-done.26 = f32[192,128]{1,0:T(8,128)S(1)} collective-permute-done((f32[192,128]{1,0:T(8,128)S(1)}, f32[192,128]{1,0:T(8,128)S(1)}, u32[]{:S(2)}, u32[]{:S(2)}) %collective-permute-start.26) | collective-permute-done | bytes 98336 | tf_op jit(solution)/shard_map/ppermute | solution.py:54
  62.2 5.4 %collective-permute-done.25 = f32[192,128]{1,0:T(8,128)S(1)} collective-permute-done((f32[192,128]{1,0:T(8,128)S(1)}, f32[192,128]{1,0:T(8,128)S(1)}, u32[]{:S(2)}, u32[]{:S(2)}) %collective-permute-start.25) | collective-permute-done | bytes 98336 | tf_op jit(solution)/shard_map/ppermute | solution.py:54
  67.6 1.4 %collective-permute-start.29 = (f32[192,128]{1,0:T(8,128)S(1)}, f32[192,128]{1,0:T(8,128)S(1)}, u32[]{:S(2)}, u32[]{:S(2)}) collective-permute-start(f32[192,128]{1,0:T(8,128)S(1)} %add_multiply_fusion.refs_0_), channel_id=1, source_target_pairs={{0,17},{1,16},{2,19},{3,18},{4,21},{5,20},{6,23},{7,22},{8,25},{9,... | collective-permute-start | bytes 294920 | tf_op jit(solution)/shard_map/ppermute | solution.py:46
  69.0 0.7 collective-permute-start.28
  69.8 1.4 %collective-permute-start.27 = (f32[192,128]{1,0:T(8,128)S(1)}, f32[192,128]{1,0:T(8,128)S(1)}, u32[]{:S(2)}, u32[]{:S(2)}) collective-permute-start(f32[192,128]{1,0:T(8,128)S(1)} %add_multiply_fusion.refs_0_), channel_id=1, source_target_pairs={{0,1},{1,0},{2,3},{3,2},{4,5},{5,4},{6,7},{7,6},{8,9},{9,8},{10,11... | collective-permute-start | bytes 294920 | tf_op jit(solution)/shard_map/ppermute | solution.py:46
  71.2 2.1 %collective-permute-done.29.refs_3_ = f32[192,128]{1,0:T(8,128)S(1)} collective-permute-done((f32[192,128]{1,0:T(8,128)S(1)}, f32[192,128]{1,0:T(8,128)S(1)}, u32[]{:S(2)}, u32[]{:S(2)}) %collective-permute-start.29) | collective-permute-done | bytes 98336 | tf_op jit(solution)/shard_map/ppermute | solution.py:46
  73.3 1.0 %collective-permute-done.28.refs_2_ = f32[192,128]{1,0:T(8,128)S(1)} collective-permute-done((f32[192,128]{1,0:T(8,128)S(1)}, f32[192,128]{1,0:T(8,128)S(1)}, u32[]{:S(2)}, u32[]{:S(2)}) %collective-permute-start.28) | collective-permute-done | bytes 98336 | tf_op jit(solution)/shard_map/ppermute | solution.py:46
  74.4 0.4 collective-permute-start.31
  74.8 0.8 collective-permute-done.32.refs_6_
  75.7 4.2 %shard_map.94 = f32[1024,128]{1,0:T(8,128)} custom-call(f32[192,128]{1,0:T(8,128)S(1)} %add_multiply_fusion.refs_0_, f32[192,128]{1,0:T(8,128)S(1)} %collective-permute-done.27.refs_1_, f32[192,128]{1,0:T(8,128)S(1)} %collective-permute-done.28.refs_2_, f32[192,128]{1,0:T(8,128)S(1)} %collective-permute-done.29.refs_3_, ...), custom_call_target="tpu_custom_call" | custom-call | flops 1207959552 | bytes 6039797 | tf_op jit(solution)/shard_map/pallas_call | solution.py:255
  (60 shorter events, 1.4 us)
Async XLA Ops:
  0.0 1.0 %copy-start.2 = (f32[1024,128]{1,0:T(8,128)S(1)}, f32[1024,128]{1,0:T(8,128)}, u32[]{:S(2)}) copy-start(f32[1024,128]{1,0:T(8,128)} %refs_12_.1) | copy-start | bytes 1572868
  1.0 0.9 %copy-start.4 = (f32[2,128,128]{2,1,0:T(8,128)S(1)}, f32[2,128,128]{2,1,0:T(8,128)}, u32[]{:S(2)}) copy-start(f32[2,128,128]{2,1,0:T(8,128)} %refs_17_.1) | copy-start | bytes 393220
  1.9 0.7 copy-start.9
  2.7 0.7 copy-start.11
  3.4 23.1 %copy-start.8 = (f32[2,768,128]{2,1,0:T(8,128)S(1)}, f32[2,768,128]{2,1,0:T(8,128)}, u32[]{:S(2)}) copy-start(f32[2,768,128]{2,1,0:T(8,128)} %refs_2_.3) | copy-start | bytes 2359300
  3.4 23.1 %copy-start.10 = (s32[3,1024]{1,0:T(4,128)S(1)}, s32[3,1024]{1,0:T(4,128)}, u32[]{:S(2)}) copy-start(s32[3,1024]{1,0:T(4,128)} %refs_1_.3) | copy-start | bytes 36868
  3.4 23.1 %copy-start.12 = (s32[3,768]{1,0:T(4,128)S(1)}, s32[3,768]{1,0:T(4,128)}, u32[]{:S(2)}) copy-start(s32[3,768]{1,0:T(4,128)} %refs_0_.3) | copy-start | bytes 27652
  10.3 1.5 %collective-permute-start.1 = (f32[192,128]{1,0:T(8,128)S(1)}, f32[192,128]{1,0:T(8,128)S(1)}, u32[]{:S(2)}, u32[]{:S(2)}) collective-permute-start(f32[192,128]{1,0:T(8,128)S(1)} %get-tuple-element.35), channel_id=1, source_target_pairs={{0,8},{1,9},{2,10},{3,11},{4,12},{5,13},{6,14},{7,15},{8,0},{9,1},... | collective-permute-start | bytes 294920 | tf_op jit(solution)/shard_map/ppermute | solution.py:46
  10.8 3.9 %collective-permute-start.3 = (f32[192,128]{1,0:T(8,128)S(1)}, f32[192,128]{1,0:T(8,128)S(1)}, u32[]{:S(2)}, u32[]{:S(2)}) collective-permute-start(f32[192,128]{1,0:T(8,128)S(1)} %get-tuple-element.37), channel_id=1, source_target_pairs={{0,8},{1,9},{2,10},{3,11},{4,12},{5,13},{6,14},{7,15},{8,0},{9,1},... | collective-permute-start | bytes 294920 | tf_op jit(solution)/shard_map/ppermute | solution.py:46
  10.9 5.4 %collective-permute-start.5 = (f32[192,128]{1,0:T(8,128)S(1)}, f32[192,128]{1,0:T(8,128)S(1)}, u32[]{:S(2)}, u32[]{:S(2)}) collective-permute-start(f32[192,128]{1,0:T(8,128)S(1)} %get-tuple-element.39), channel_id=1, source_target_pairs={{0,8},{1,9},{2,10},{3,11},{4,12},{5,13},{6,14},{7,15},{8,0},{9,1},... | collective-permute-start | bytes 294920 | tf_op jit(solution)/shard_map/ppermute | solution.py:46
  11.3 5.1 %collective-permute-start = (f32[192,128]{1,0:T(8,128)S(1)}, f32[192,128]{1,0:T(8,128)S(1)}, u32[]{:S(2)}, u32[]{:S(2)}) collective-permute-start(f32[192,128]{1,0:T(8,128)S(1)} %get-tuple-element.33), channel_id=1, source_target_pairs={{0,8},{1,9},{2,10},{3,11},{4,12},{5,13},{6,14},{7,15},{8,0},{9,1},... | collective-permute-start | bytes 294920 | tf_op jit(solution)/shard_map/ppermute | solution.py:46
  11.8 6.0 %collective-permute-start.2 = (f32[192,128]{1,0:T(8,128)S(1)}, f32[192,128]{1,0:T(8,128)S(1)}, u32[]{:S(2)}, u32[]{:S(2)}) collective-permute-start(f32[192,128]{1,0:T(8,128)S(1)} %add.61), channel_id=1, source_target_pairs={{0,1},{1,0},{2,3},{3,2},{4,5},{5,4},{6,7},{7,6},{8,9},{9,8},{10,11... | collective-permute-start | bytes 294920 | tf_op jit(solution)/shard_map/ppermute | solution.py:46
  14.7 5.8 %collective-permute-start.4 = (f32[192,128]{1,0:T(8,128)S(1)}, f32[192,128]{1,0:T(8,128)S(1)}, u32[]{:S(2)}, u32[]{:S(2)}) collective-permute-start(f32[192,128]{1,0:T(8,128)S(1)} %add.63), channel_id=1, source_target_pairs={{0,16},{1,17},{2,18},{3,19},{4,20},{5,21},{6,22},{7,23},{8,24},{9,... | collective-permute-start | bytes 294920 | tf_op jit(solution)/shard_map/ppermute | solution.py:46
  16.3 5.6 %collective-permute-start.6 = (f32[192,128]{1,0:T(8,128)S(1)}, f32[192,128]{1,0:T(8,128)S(1)}, u32[]{:S(2)}, u32[]{:S(2)}) collective-permute-start(f32[192,128]{1,0:T(8,128)S(1)} %add.65), channel_id=1, source_target_pairs={{0,17},{1,16},{2,19},{3,18},{4,21},{5,20},{6,23},{7,22},{8,25},{9,... | collective-permute-start | bytes 294920 | tf_op jit(solution)/shard_map/ppermute | solution.py:46
  21.9 19.7 %copy-start = (f32[2,128,128]{2,1,0:T(8,128)S(1)}, f32[2,128,128]{2,1,0:T(8,128)}, u32[]{:S(2)}) copy-start(f32[2,128,128]{2,1,0:T(8,128)} %refs_14_.3) | copy-start | bytes 393220
  21.9 19.7 %copy-start.1 = (f32[2,128,128]{2,1,0:T(8,128)S(1)}, f32[2,128,128]{2,1,0:T(8,128)}, u32[]{:S(2)}) copy-start(f32[2,128,128]{2,1,0:T(8,128)} %refs_16_.3) | copy-start | bytes 393220
  22.0 19.7 %copy-start.3 = (f32[1024,128]{1,0:T(8,128)S(1)}, f32[1024,128]{1,0:T(8,128)}, u32[]{:S(2)}) copy-start(f32[1024,128]{1,0:T(8,128)} %refs_12_.1) | copy-start | bytes 1572868
  22.0 19.7 %copy-start.5 = (f32[2,128,128]{2,1,0:T(8,128)S(1)}, f32[2,128,128]{2,1,0:T(8,128)}, u32[]{:S(2)}) copy-start(f32[2,128,128]{2,1,0:T(8,128)} %refs_17_.1) | copy-start | bytes 393220
  22.0 19.7 %copy-start.6 = (f32[2,128]{1,0:T(2,128)S(1)}, f32[2,128]{1,0:T(2,128)}, u32[]{:S(2)}) copy-start(f32[2,128]{1,0:T(2,128)} %refs_13_.3) | copy-start | bytes 3076
  22.0 19.7 %copy-start.7 = (f32[2,128]{1,0:T(2,128)S(1)}, f32[2,128]{1,0:T(2,128)}, u32[]{:S(2)}) copy-start(f32[2,128]{1,0:T(2,128)} %refs_15_.3) | copy-start | bytes 3076
  22.0 8.7 %collective-permute-start.9 = (f32[192,128]{1,0:T(8,128)S(1)}, f32[192,128]{1,0:T(8,128)S(1)}, u32[]{:S(2)}, u32[]{:S(2)}) collective-permute-start(f32[192,128]{1,0:T(8,128)S(1)} %add_add_fusion.1), channel_id=1, source_target_pairs={{0,2},{1,3},{2,0},{3,1},{4,6},{5,7},{6,4},{7,5},{8,10},{9,11},{10,... | collective-permute-start | bytes 294920 | tf_op jit(solution)/shard_map/ppermute | solution.py:54
  23.6 8.0 %collective-permute-start.8 = (f32[192,128]{1,0:T(8,128)S(1)}, f32[192,128]{1,0:T(8,128)S(1)}, u32[]{:S(2)}, u32[]{:S(2)}) collective-permute-start(f32[192,128]{1,0:T(8,128)S(1)} %add_add_fusion.1), channel_id=1, source_target_pairs={{0,4},{1,5},{2,6},{3,7},{4,0},{5,1},{6,2},{7,3},{8,12},{9,13},{10,... | collective-permute-start | bytes 294920 | tf_op jit(solution)/shard_map/ppermute | solution.py:54
  26.2 6.5 %collective-permute-start.7 = (f32[192,128]{1,0:T(8,128)S(1)}, f32[192,128]{1,0:T(8,128)S(1)}, u32[]{:S(2)}, u32[]{:S(2)}) collective-permute-start(f32[192,128]{1,0:T(8,128)S(1)} %add_add_fusion.1), channel_id=1, source_target_pairs={{0,6},{1,7},{2,4},{3,5},{4,2},{5,3},{6,0},{7,1},{8,14},{9,15},{10,... | collective-permute-start | bytes 294920 | tf_op jit(solution)/shard_map/ppermute | solution.py:54
  32.8 5.6 %collective-permute-start.12 = (f32[192,128]{1,0:T(8,128)S(1)}, f32[192,128]{1,0:T(8,128)S(1)}, u32[]{:S(2)}, u32[]{:S(2)}) collective-permute-start(f32[192,128]{1,0:T(8,128)S(1)} %add_multiply_fusion.1.refs_0_), channel_id=1, source_target_pairs={{0,17},{1,16},{2,19},{3,18},{4,21},{5,20},{6,23},{7,22},{8,25},{9,... | collective-permute-start | bytes 294920 | tf_op jit(solution)/shard_map/ppermute | solution.py:46
  34.2 5.2 %collective-permute-start.11 = (f32[192,128]{1,0:T(8,128)S(1)}, f32[192,128]{1,0:T(8,128)S(1)}, u32[]{:S(2)}, u32[]{:S(2)}) collective-permute-start(f32[192,128]{1,0:T(8,128)S(1)} %add_multiply_fusion.1.refs_0_), channel_id=1, source_target_pairs={{0,16},{1,17},{2,18},{3,19},{4,20},{5,21},{6,22},{7,23},{8,24},{9,... | collective-permute-start | bytes 294920 | tf_op jit(solution)/shard_map/ppermute | solution.py:46
  35.7 4.6 %collective-permute-start.10 = (f32[192,128]{1,0:T(8,128)S(1)}, f32[192,128]{1,0:T(8,128)S(1)}, u32[]{:S(2)}, u32[]{:S(2)}) collective-permute-start(f32[192,128]{1,0:T(8,128)S(1)} %add_multiply_fusion.1.refs_0_), channel_id=1, source_target_pairs={{0,1},{1,0},{2,3},{3,2},{4,5},{5,4},{6,7},{7,6},{8,9},{9,8},{10,11... | collective-permute-start | bytes 294920 | tf_op jit(solution)/shard_map/ppermute | solution.py:46
  36.3 4.0 %collective-permute-start.13 = (f32[192,128]{1,0:T(8,128)S(1)}, f32[192,128]{1,0:T(8,128)S(1)}, u32[]{:S(2)}, u32[]{:S(2)}) collective-permute-start(f32[192,128]{1,0:T(8,128)S(1)} %add_multiply_fusion.1.refs_0_), channel_id=1, source_target_pairs={{0,8},{1,9},{2,10},{3,11},{4,12},{5,13},{6,14},{7,15},{8,0},{9,1},... | collective-permute-start | bytes 294920 | tf_op jit(solution)/shard_map/ppermute | solution.py:46
  38.4 1.9 %collective-permute-start.16 = (f32[192,128]{1,0:T(8,128)S(1)}, f32[192,128]{1,0:T(8,128)S(1)}, u32[]{:S(2)}, u32[]{:S(2)}) collective-permute-start(f32[192,128]{1,0:T(8,128)S(1)} %collective-permute-done.12.refs_3_), channel_id=1, source_target_pairs={{0,8},{1,9},{2,10},{3,11},{4,12},{5,13},{6,14},{7,15},{8,0},{9,1},... | collective-permute-start | bytes 294920 | tf_op jit(solution)/shard_map/ppermute | solution.py:46
  39.4 1.3 %collective-permute-start.15 = (f32[192,128]{1,0:T(8,128)S(1)}, f32[192,128]{1,0:T(8,128)S(1)}, u32[]{:S(2)}, u32[]{:S(2)}) collective-permute-start(f32[192,128]{1,0:T(8,128)S(1)} %collective-permute-done.11.refs_2_), channel_id=1, source_target_pairs={{0,8},{1,9},{2,10},{3,11},{4,12},{5,13},{6,14},{7,15},{8,0},{9,1},... | collective-permute-start | bytes 294920 | tf_op jit(solution)/shard_map/ppermute | solution.py:46
  40.4 1.3 %collective-permute-start.14 = (f32[192,128]{1,0:T(8,128)S(1)}, f32[192,128]{1,0:T(8,128)S(1)}, u32[]{:S(2)}, u32[]{:S(2)}) collective-permute-start(f32[192,128]{1,0:T(8,128)S(1)} %collective-permute-done.10.refs_1_), channel_id=1, source_target_pairs={{0,8},{1,9},{2,10},{3,11},{4,12},{5,13},{6,14},{7,15},{8,0},{9,1},... | collective-permute-start | bytes 294920 | tf_op jit(solution)/shard_map/ppermute | solution.py:46
  47.5 1.4 %collective-permute-start.18 = (f32[192,128]{1,0:T(8,128)S(1)}, f32[192,128]{1,0:T(8,128)S(1)}, u32[]{:S(2)}, u32[]{:S(2)}) collective-permute-start(f32[192,128]{1,0:T(8,128)S(1)} %get-tuple-element.52), channel_id=1, source_target_pairs={{0,8},{1,9},{2,10},{3,11},{4,12},{5,13},{6,14},{7,15},{8,0},{9,1},... | collective-permute-start | bytes 294920 | tf_op jit(solution)/shard_map/ppermute | solution.py:46
  47.7 1.9 %collective-permute-start.20 = (f32[192,128]{1,0:T(8,128)S(1)}, f32[192,128]{1,0:T(8,128)S(1)}, u32[]{:S(2)}, u32[]{:S(2)}) collective-permute-start(f32[192,128]{1,0:T(8,128)S(1)} %get-tuple-element.54), channel_id=1, source_target_pairs={{0,8},{1,9},{2,10},{3,11},{4,12},{5,13},{6,14},{7,15},{8,0},{9,1},... | collective-permute-start | bytes 294920 | tf_op jit(solution)/shard_map/ppermute | solution.py:46
  48.0 2.7 %collective-permute-start.22 = (f32[192,128]{1,0:T(8,128)S(1)}, f32[192,128]{1,0:T(8,128)S(1)}, u32[]{:S(2)}, u32[]{:S(2)}) collective-permute-start(f32[192,128]{1,0:T(8,128)S(1)} %get-tuple-element.56), channel_id=1, source_target_pairs={{0,8},{1,9},{2,10},{3,11},{4,12},{5,13},{6,14},{7,15},{8,0},{9,1},... | collective-permute-start | bytes 294920 | tf_op jit(solution)/shard_map/ppermute | solution.py:46
  48.2 4.4 %collective-permute-start.17 = (f32[192,128]{1,0:T(8,128)S(1)}, f32[192,128]{1,0:T(8,128)S(1)}, u32[]{:S(2)}, u32[]{:S(2)}) collective-permute-start(f32[192,128]{1,0:T(8,128)S(1)} %get-tuple-element.50), channel_id=1, source_target_pairs={{0,8},{1,9},{2,10},{3,11},{4,12},{5,13},{6,14},{7,15},{8,0},{9,1},... | collective-permute-start | bytes 294920 | tf_op jit(solution)/shard_map/ppermute | solution.py:46
  48.8 5.1 %collective-permute-start.19 = (f32[192,128]{1,0:T(8,128)S(1)}, f32[192,128]{1,0:T(8,128)S(1)}, u32[]{:S(2)}, u32[]{:S(2)}) collective-permute-start(f32[192,128]{1,0:T(8,128)S(1)} %add.71), channel_id=1, source_target_pairs={{0,1},{1,0},{2,3},{3,2},{4,5},{5,4},{6,7},{7,6},{8,9},{9,8},{10,11... | collective-permute-start | bytes 294920 | tf_op jit(solution)/shard_map/ppermute | solution.py:46
  49.6 6.9 %collective-permute-start.21 = (f32[192,128]{1,0:T(8,128)S(1)}, f32[192,128]{1,0:T(8,128)S(1)}, u32[]{:S(2)}, u32[]{:S(2)}) collective-permute-start(f32[192,128]{1,0:T(8,128)S(1)} %add.73), channel_id=1, source_target_pairs={{0,16},{1,17},{2,18},{3,19},{4,20},{5,21},{6,22},{7,23},{8,24},{9,... | collective-permute-start | bytes 294920 | tf_op jit(solution)/shard_map/ppermute | solution.py:46
  50.7 5.8 %collective-permute-start.23 = (f32[192,128]{1,0:T(8,128)S(1)}, f32[192,128]{1,0:T(8,128)S(1)}, u32[]{:S(2)}, u32[]{:S(2)}) collective-permute-start(f32[192,128]{1,0:T(8,128)S(1)} %add.75), channel_id=1, source_target_pairs={{0,17},{1,16},{2,19},{3,18},{4,21},{5,20},{6,23},{7,22},{8,25},{9,... | collective-permute-start | bytes 294920 | tf_op jit(solution)/shard_map/ppermute | solution.py:46
  56.6 5.6 %collective-permute-start.26 = (f32[192,128]{1,0:T(8,128)S(1)}, f32[192,128]{1,0:T(8,128)S(1)}, u32[]{:S(2)}, u32[]{:S(2)}) collective-permute-start(f32[192,128]{1,0:T(8,128)S(1)} %add_add_fusion), channel_id=1, source_target_pairs={{0,2},{1,3},{2,0},{3,1},{4,6},{5,7},{6,4},{7,5},{8,10},{9,11},{10,... | collective-permute-start | bytes 294920 | tf_op jit(solution)/shard_map/ppermute | solution.py:54
  58.0 9.6 %collective-permute-start.25 = (f32[192,128]{1,0:T(8,128)S(1)}, f32[192,128]{1,0:T(8,128)S(1)}, u32[]{:S(2)}, u32[]{:S(2)}) collective-permute-start(f32[192,128]{1,0:T(8,128)S(1)} %add_add_fusion), channel_id=1, source_target_pairs={{0,4},{1,5},{2,6},{3,7},{4,0},{5,1},{6,2},{7,3},{8,12},{9,13},{10,... | collective-permute-start | bytes 294920 | tf_op jit(solution)/shard_map/ppermute | solution.py:54
  59.4 8.2 %collective-permute-start.24 = (f32[192,128]{1,0:T(8,128)S(1)}, f32[192,128]{1,0:T(8,128)S(1)}, u32[]{:S(2)}, u32[]{:S(2)}) collective-permute-start(f32[192,128]{1,0:T(8,128)S(1)} %add_add_fusion), channel_id=1, source_target_pairs={{0,6},{1,7},{2,4},{3,5},{4,2},{5,3},{6,0},{7,1},{8,14},{9,15},{10,... | collective-permute-start | bytes 294920 | tf_op jit(solution)/shard_map/ppermute | solution.py:54
  67.6 5.6 %collective-permute-start.29 = (f32[192,128]{1,0:T(8,128)S(1)}, f32[192,128]{1,0:T(8,128)S(1)}, u32[]{:S(2)}, u32[]{:S(2)}) collective-permute-start(f32[192,128]{1,0:T(8,128)S(1)} %add_multiply_fusion.refs_0_), channel_id=1, source_target_pairs={{0,17},{1,16},{2,19},{3,18},{4,21},{5,20},{6,23},{7,22},{8,25},{9,... | collective-permute-start | bytes 294920 | tf_op jit(solution)/shard_map/ppermute | solution.py:46
  69.0 5.3 %collective-permute-start.28 = (f32[192,128]{1,0:T(8,128)S(1)}, f32[192,128]{1,0:T(8,128)S(1)}, u32[]{:S(2)}, u32[]{:S(2)}) collective-permute-start(f32[192,128]{1,0:T(8,128)S(1)} %add_multiply_fusion.refs_0_), channel_id=1, source_target_pairs={{0,16},{1,17},{2,18},{3,19},{4,20},{5,21},{6,22},{7,23},{8,24},{9,... | collective-permute-start | bytes 294920 | tf_op jit(solution)/shard_map/ppermute | solution.py:46
  69.8 4.6 %collective-permute-start.27 = (f32[192,128]{1,0:T(8,128)S(1)}, f32[192,128]{1,0:T(8,128)S(1)}, u32[]{:S(2)}, u32[]{:S(2)}) collective-permute-start(f32[192,128]{1,0:T(8,128)S(1)} %add_multiply_fusion.refs_0_), channel_id=1, source_target_pairs={{0,1},{1,0},{2,3},{3,2},{4,5},{5,4},{6,7},{7,6},{8,9},{9,8},{10,11... | collective-permute-start | bytes 294920 | tf_op jit(solution)/shard_map/ppermute | solution.py:46
  71.2 3.6 %collective-permute-start.30 = (f32[192,128]{1,0:T(8,128)S(1)}, f32[192,128]{1,0:T(8,128)S(1)}, u32[]{:S(2)}, u32[]{:S(2)}) collective-permute-start(f32[192,128]{1,0:T(8,128)S(1)} %add_multiply_fusion.refs_0_), channel_id=1, source_target_pairs={{0,8},{1,9},{2,10},{3,11},{4,12},{5,13},{6,14},{7,15},{8,0},{9,1},... | collective-permute-start | bytes 294920 | tf_op jit(solution)/shard_map/ppermute | solution.py:46
  73.3 1.5 %collective-permute-start.33 = (f32[192,128]{1,0:T(8,128)S(1)}, f32[192,128]{1,0:T(8,128)S(1)}, u32[]{:S(2)}, u32[]{:S(2)}) collective-permute-start(f32[192,128]{1,0:T(8,128)S(1)} %collective-permute-done.29.refs_3_), channel_id=1, source_target_pairs={{0,8},{1,9},{2,10},{3,11},{4,12},{5,13},{6,14},{7,15},{8,0},{9,1},... | collective-permute-start | bytes 294920 | tf_op jit(solution)/shard_map/ppermute | solution.py:46
  74.3 1.3 %collective-permute-start.32 = (f32[192,128]{1,0:T(8,128)S(1)}, f32[192,128]{1,0:T(8,128)S(1)}, u32[]{:S(2)}, u32[]{:S(2)}) collective-permute-start(f32[192,128]{1,0:T(8,128)S(1)} %collective-permute-done.28.refs_2_), channel_id=1, source_target_pairs={{0,8},{1,9},{2,10},{3,11},{4,12},{5,13},{6,14},{7,15},{8,0},{9,1},... | collective-permute-start | bytes 294920 | tf_op jit(solution)/shard_map/ppermute | solution.py:46
  74.4 1.4 %collective-permute-start.31 = (f32[192,128]{1,0:T(8,128)S(1)}, f32[192,128]{1,0:T(8,128)S(1)}, u32[]{:S(2)}, u32[]{:S(2)}) collective-permute-start(f32[192,128]{1,0:T(8,128)S(1)} %collective-permute-done.27.refs_1_), channel_id=1, source_target_pairs={{0,8},{1,9},{2,10},{3,11},{4,12},{5,13},{6,14},{7,15},{8,0},{9,1},... | collective-permute-start | bytes 294920 | tf_op jit(solution)/shard_map/ppermute | solution.py:46
where the time goes:
time: 80.3 us; the launch traced here: 80 us
  waiting for transfers between devices  28.1 us (35%)
  starting transfers between devices  26.9 us (33%)
  Pallas kernels  21.1 us (26%)
  local copies, waits for them, and re-layouts  3.42 us (4%)
    pallas_call x4, Pallas kernels, call(): pl.pallas_call(kernel, in_specs=[pl.BlockSpec(memory_space=space)] * len(...  21.1 us
    ppermute x28, waiting for transfers between devices, send(): lax.ppermute(value, axes, [(i, self.moved(i, **d)) for i in range(count)])  19.5 us
    ppermute x28, starting transfers between devices, send(): lax.ppermute(value, axes, [(i, self.moved(i, **d)) for i in range(count)])  18 us
    ppermute x6, starting transfers between devices, exchange(): return lax.ppermute(value, axes, pairs)  8.9 us
    ppermute x6, waiting for transfers between devices, exchange(): return lax.ppermute(value, axes, pairs)  8.58 us
    unnamed x26, local copies, waits for them, and re-layouts  3.42 us
  transfers between devices with their start and end apart: 34, of which 21 were waited for; matrix products, arithmetic and copies ran while one was open for 0% of the time, Pallas kernels for 5%

commit v1 on v0

--- a/solution.py
+++ b/solution.py
@@ -6,7 +6,7 @@
 from jax.sharding import PartitionSpec as P
 
 axes = ("outer", "atoms")
-first_limit, table_limit, block_limit = 10 * 2**20, 8 * 2**20, 10 * 2**20
+first_limit, near_limit, table_limit, block_limit = (n * 2**20 for n in (10, 4, 8, 12))
 turn_bits = 18
 half_sin = (0.10982699, -0.84611289, 3.60635441, -7.3082457, 4.44288292)
 half_cos = (0.31069819, -1.88356299, 5.73946117, -6.97885099, 1.4142135)
@@ -117,12 +117,20 @@
     return jnp.concatenate([high, low], axis=1)
 
 
-def product(left, right):
-    width = right.shape[1]
-    left_high, left_low = halves(left)
-    pair = paired(right)
-    both = matmul(left_high, pair)
-    return both[:, :width] + both[:, width:] + matmul(left_low, pair[:, :width])
+def folded(value):
+    width = value.shape[1] // 2
+    return value[:, :width] + value[:, width:]
+
+
+def stacked(weight):
+    pair = paired(weight)
+    width = weight.shape[1]
+    again = jnp.concatenate([pair[:, :width], jnp.zeros_like(pair[:, width:])], axis=1)
+    return jnp.concatenate([pair, again], axis=0)
+
+
+def product(left, stack):
+    return folded(matmul(paired(left), stack))
 
 
 def digits(position):
@@ -155,40 +163,43 @@
     return value
 
 
-def fill_tables(turns_ref, cos_high, cos_low, sin_high, sin_low):
-    rows, columns = turns_ref.shape
+def fill_tables(turns_ref, here, lanes, targets):
+    turns = turns_ref[here, lanes]
+    t = turns - ((turns + to_integer) - to_integer)
+    u = t * t
+    s = horner(half_sin, u) * t
+    c = horner(half_cos, u)
+    cos_high, cos_low = halves(1.0 - s * s)
+    sin_high, sin_low = halves(s * c)
+    for (ref, index), value in zip(targets, (cos_high, sin_high, cos_low, sin_low)):
+        ref[index] = value
+
+
+def fill_chunk(turns_ref, first_row, rows, table_ref, n):
     step, width = 32, 256
-
-    def body(n, carry):
-        here = pl.ds(pl.multiple_of(n * step, step), step)
-        for at in range(0, columns, width):
+    for row in range(0, rows, step):
+        here = pl.ds(pl.multiple_of(first_row + row, step), step)
+        for at in range(0, turns_ref.shape[1], width):
             lanes = slice(at, at + width)
-            turns = turns_ref[here, lanes]
-            t = turns - ((turns + to_integer) - to_integer)
-            u = t * t
-            s = horner(half_sin, u) * t
-            c = horner(half_cos, u)
-            cos_high[here, lanes], cos_low[here, lanes] = halves(1.0 - s * s)
-            sin_high[here, lanes], sin_low[here, lanes] = halves(s * c)
-        return carry
-
-    lax.fori_loop(0, rows // step, body, 0)
-
-
-def project(layout, tables, pair, chunk_refs, rows):
+            targets = [
+                (table_ref, (n, slice(kind * rows + row, kind * rows + row + step), lanes)) for kind in range(4)
+            ]
+            fill_tables(turns_ref, here, lanes, targets)
+
+
+def project(table, pair, chunk_ref, rows):
     width = pair.shape[1] // 2
-    for offset, chunk_ref in zip(layout.offsets(), chunk_refs):
-        here = pl.ds(pl.multiple_of(layout.chunk_of(*offset) * rows, rows), rows)
-        for n in range(2):
-            both = matmul(tables[2 * n][here, :], pair)
-            rest = matmul(tables[2 * n + 1][here, :], pair[:, :width])
-            chunk_ref[n * rows : (n + 1) * rows, :] = both[:, :width] + both[:, width:] + rest
+    both = matmul(table, pair)
+    chunk_ref[...] = folded(both[: 2 * rows, :]) + both[2 * rows :, :width]
 
 
 def first_kernel(layout, rows, *refs):
     sources, refs = refs[:4], refs[4:]
-    tables, chunks = refs[:4], refs[4 : 4 + layout.chunks]
-    wave_rows, digit_rows, turns, waves, positions, features, w_value, arrived = refs[4 + layout.chunks :]
+    far = [o for o in layout.offsets() if o[1:] != (0, 0)]
+    near = [o for o in layout.offsets() if o[1:] == (0, 0)]
+    table, pair_out, near_turns = refs[:3]
+    chunks = refs[3 : 3 + len(far)]
+    wave_rows, digit_rows, turns, waves, positions, features, w_value, arrived = refs[3 + len(far) :]
     copies = [
         pltpu.make_async_copy(source, target, arrived.at[n])
         for n, (source, target) in enumerate(zip(sources, (waves, positions, features, w_value)))
@@ -199,56 +210,97 @@
     copies[1].wait()
     operands(waves, positions, wave_rows, digit_rows)
     turns[...] = contract_rows(wave_rows[...], digit_rows[...])
-    fill_tables(turns, *tables)
     copies[2].wait()
     copies[3].wait()
-    pair = paired(product(features[...], w_value[0]))
-    project(layout, tables, pair, chunks, rows)
-
-
-def atom_table_kernel(layout, rows, waves, positions, freq_filter, *refs):
-    tables, scales = refs[:4], refs[4:-3]
+    pair_out[...] = paired(product(features[...], stacked(w_value[0])))
+    for n, offset in enumerate(near):
+        here = pl.ds(pl.multiple_of(layout.chunk_of(*offset) * rows, rows), rows)
+        near_turns[n * rows : (n + 1) * rows, :] = turns[here, :]
+    for n, offset in enumerate(far):
+        fill_chunk(turns, layout.chunk_of(*offset) * rows, rows, table, n)
+        if n:
+            project(table[n - 1], pair_out[...], chunks[n - 1], rows)
+    project(table[len(far) - 1], pair_out[...], chunks[len(far) - 1], rows)
+
+
+def near_kernel(rows, turns, pair, table, *chunks):
+    for n in range(len(chunks)):
+        fill_chunk(turns, n * rows, rows, table, n)
+        if n:
+            project(table[n - 1], pair[...], chunks[n - 1], rows)
+    project(table[len(chunks) - 1], pair[...], chunks[-1], rows)
+
+
+def atom_table_kernel(layout, rows, waves, positions, freq_filter, table, *refs):
+    scales = refs[:-3]
     wave_rows, digit_rows, turns = refs[-3:]
-    here = pl.ds(pl.multiple_of(layout.chunk_of(0, 0, 0) * rows, rows), rows)
+    own = pl.ds(pl.multiple_of(layout.chunk_of(0, 0, 0) * rows, rows), rows)
     for block, scale in enumerate(scales):
-        scale[:rows, :] = freq_filter[block, here, :]
-        scale[rows:, :] = freq_filter[block, here, :]
+        scale[:rows, :] = freq_filter[block, own, :]
+        scale[rows:, :] = freq_filter[block, own, :]
     operands(waves, positions, wave_rows, digit_rows)
     turns[...] = contract_rows(digit_rows[...], wave_rows[...])
-    fill_tables(turns, *tables)
+    atoms, count = turns.shape
+    step, width = 32, 256
+    half = table.shape[1] // 2
+    per_group = half // step
+
+    def body(m, carry):
+        here = pl.ds(pl.multiple_of(m * step, step), step)
+        group, row = m // per_group, pl.multiple_of((m % per_group) * step, step)
+        for at in range(0, count, width):
+            targets = [
+                (table, (group, pl.ds(row + low * half, step), pl.ds(kind * count + at, width)))
+                for low in range(2)
+                for kind in range(2)
+            ]
+            fill_tables(turns, here, slice(at, at + width), targets)
+        return carry
+
+    lax.fori_loop(0, atoms // step, body, 0)
 
 
 def block_kernel(layout, rows, block, last, *refs):
     chunks_in, refs = refs[: layout.chunks], refs[layout.chunks :]
-    atom_tables, refs = refs[:4], refs[4:]
-    current_ref, gain, w_hidden, b_hidden, w_output = refs[:5]
-    refs = refs[5:]
+    atom_table, current_ref, gain, w_hidden, b_hidden, w_output = refs[:6]
+    refs = refs[6:]
     if not last:
-        w_value, tables, refs = refs[0], refs[1:5], refs[5:]
-    current_out, refs = refs[0], refs[1:]
-    cos_pair, sin_pair = refs[-2:]
+        w_value, far_table, near_table, refs = refs[0], refs[1], refs[2], refs[3:]
+    current_out, chunks_out, factor = refs[0], refs[1:-1], refs[-1]
+    waves = rows * layout.chunks
     width = current_ref.shape[1]
     for offset, chunk in zip(layout.offsets(), chunks_in):
-        here = pl.ds(pl.multiple_of(layout.chunk_of(*offset) * rows, rows), rows)
-        cos_pair[here, :] = paired(chunk[:rows, :])
-        sin_pair[here, :] = paired(chunk[rows:, :])
-    atoms = current_ref.shape[0]
-    step = min(256, atoms)
-    for at in range(0, atoms, step):
-        here = slice(at, at + step)
-        both = matmul(atom_tables[0][here, :], cos_pair[...])
-        both = both + matmul(atom_tables[2][here, :], sin_pair[...])
-        messages = both[:, :width] + both[:, width:]
-        messages = messages + matmul(atom_tables[1][here, :], cos_pair[:, :width])
-        messages = messages + matmul(atom_tables[3][here, :], sin_pair[:, :width])
+        row = pl.multiple_of(layout.chunk_of(*offset) * rows, rows)
+        factor[pl.ds(row, rows), :] = paired(chunk[:rows, :])
+        factor[pl.ds(waves + row, rows), :] = paired(chunk[rows:, :])
+    hidden_stack, output_stack = stacked(w_hidden[block]), stacked(w_output[block])
+    groups = atom_table.shape[0]
+    step = atom_table.shape[1] // 2
+
+    def back(n):
+        both = matmul(atom_table[n], factor[...])
+        return folded(both[:step, :]) + both[step:, :width]
+
+    def update(n, messages):
+        here = slice(n * step, (n + 1) * step)
         mean = jnp.mean(messages * messages, axis=1, keepdims=True)
         normed = messages * lax.rsqrt(mean + 1e-06) * gain[block : block + 1, :]
-        hidden = product(normed, w_hidden[block]) + b_hidden[block : block + 1, :]
+        hidden = product(normed, hidden_stack) + b_hidden[block : block + 1, :]
         hidden = hidden / (1.0 + jnp.exp(-hidden))
-        current_out[here, :] = current_ref[here, :] + product(hidden, w_output[block])
+        current_out[here, :] = current_ref[here, :] + product(hidden, output_stack)
+
+    messages = back(0)
+    for n in range(groups):
+        coming = back(n + 1) if n + 1 < groups else None
+        update(n, messages)
+        messages = coming
     if not last:
-        pair = paired(product(current_out[...], w_value[block + 1]))
-        project(layout, tables, pair, refs[: layout.chunks], rows)
+        pair = paired(product(current_out[...], stacked(w_value[block + 1])))
+        far = [n for n, o in enumerate(layout.offsets()) if o[1:] != (0, 0)]
+        near = [n for n, o in enumerate(layout.offsets()) if o[1:] == (0, 0)]
+        for table, members in ((far_table, far), (near_table, near)):
+            for at, n in enumerate(members):
+                project(table[at], pair, chunks_out[n], rows)
 
 
 def call(kernel, outputs, scratch, limit, flops, *inputs, space=pltpu.VMEM):
@@ -274,22 +326,43 @@
     index_scratch = [pltpu.VMEM((16, waves), f32), pltpu.VMEM((16, atoms), f32)]
     flops = 12 * waves * atoms * channels
     early = [wavevectors, positions, features, w_value]
+    offsets = layout.offsets()
+    far = [o for o in offsets if o[1:] != (0, 0)]
+    near = [o for o in offsets if o[1:] == (0, 0)]
+    group = min(256, atoms)
     outs = call(
         lambda *refs: first_kernel(layout, rows, *refs),
-        [shape((waves, atoms), bf16)] * 4 + [chunk] * layout.chunks,
+        [
+            shape((len(far), 4 * rows, atoms), bf16),
+            shape((atoms, 2 * channels), bf16),
+            shape((len(near) * rows, atoms), f32),
+        ]
+        + [chunk] * len(far),
         index_scratch
         + [pltpu.VMEM((waves, atoms), f32)]
         + [pltpu.VMEM(array.shape, array.dtype) for array in early]
         + [pltpu.SemaphoreType.DMA((len(early),))],
         first_limit,
         flops,
-        *early,
+        *[pltpu.with_memory_space_constraint(array, pltpu.HBM) for array in early],
         space=pltpu.HBM,
     )
-    tables, chunks = outs[:4], outs[4:]
+    far_table, pair, near_turns = outs[:3]
+    parts = dict(zip(far, outs[3:]))
+    outs = call(
+        lambda *refs: near_kernel(rows, *refs),
+        [shape((len(near), 4 * rows, atoms), bf16)] + [chunk] * len(near),
+        [],
+        near_limit,
+        flops // 4,
+        near_turns,
+        pair,
+    )
+    near_table = outs[0]
+    parts |= dict(zip(near, outs[1:]))
     outs = call(
         lambda *refs: atom_table_kernel(layout, rows, *refs),
-        [shape((atoms, waves), bf16)] * 4 + [chunk] * blocks,
+        [shape((atoms // group, 2 * group, 2 * waves), bf16)] + [chunk] * blocks,
         index_scratch + [pltpu.VMEM((atoms, waves), f32)],
         table_limit,
         flops,
@@ -297,25 +370,25 @@
         positions,
         freq_filter,
     )
-    atom_tables, scales = outs[:4], outs[4:]
+    atom_table, scales = outs[0], outs[1:]
     current = features
-    offsets = layout.offsets()
     for block in range(blocks):
         last = block == blocks - 1
-        gathered = total(layout, dict(zip(offsets, chunks)), scales[block])
-        inputs = [gathered[o] for o in offsets] + list(atom_tables)
-        inputs += [current, norm_gain, w_hidden, b_hidden, w_output]
+        gathered = total(layout, parts, scales[block])
+        inputs = [gathered[o] for o in offsets]
+        inputs += [atom_table, current, norm_gain, w_hidden, b_hidden, w_output]
         if not last:
-            inputs += [w_value] + list(tables)
+            inputs += [w_value, far_table, near_table]
         outs = call(
             lambda *refs, block=block, last=last: block_kernel(layout, rows, block, last, *refs),
             [shape((atoms, channels), f32)] + ([] if last else [chunk] * layout.chunks),
-            [pltpu.VMEM((waves, 2 * channels), bf16)] * 2,
+            [pltpu.VMEM((2 * waves, 2 * channels), bf16)],
             block_limit,
             flops,
             *inputs,
         )
-        current, chunks = outs[0], outs[1:]
+        current = outs[0]
+        parts = dict(zip(offsets, outs[1:]))
     return current
 
 

time: 80.3 us -> 73.4 us (0.914)
  local copies, waits for them, and re-layouts: 3.42 us -> 0.05 us
  Pallas kernels: 21.1 us -> 18.2 us
    unnamed x26 -> x18, local copies, waits for them, and re-layouts: 3.42 us -> 0.05 us
    pallas_call x4 -> x5, Pallas kernels: 21.1 us -> 18.2 us  [call(): pl.pallas_call(kernel, in_specs=[pl.BlockSpec(memory_space=space)] * len(...]
  transfers between devices with their start and end apart: 34 -> 34, of which waited for: 21 -> 20; matrix products, arithmetic and copies ran while one was open for 0% -> 0% of each run, Pallas kernels for 5% -> 7%
where the time goes in v1:
time: 73.4 us; the launch traced here: 73.3 us
  waiting for transfers between devices  27.6 us (38%)
  starting transfers between devices  27 us (37%)
  Pallas kernels  18.2 us (25%)
    ppermute x28, waiting for transfers between devices, send(): lax.ppermute(value, axes, [(i, self.moved(i, **d)) for i in range(count)])  19 us
    pallas_call x5, Pallas kernels, call(): pl.pallas_call(kernel, in_specs=[pl.BlockSpec(memory_space=space)] * len(...  18.2 us
    ppermute x28, starting transfers between devices, send(): lax.ppermute(value, axes, [(i, self.moved(i, **d)) for i in range(count)])  18.1 us
    ppermute x6, starting transfers between devices, exchange(): return lax.ppermute(value, axes, pairs)  8.9 us
    ppermute x6, waiting for transfers between devices, exchange(): return lax.ppermute(value, axes, pairs)  8.61 us
  transfers between devices with their start and end apart: 34, of which 20 were waited for; matrix products, arithmetic and copies ran while one was open for 0% of the time, Pallas kernels for 7%

profile of v1, /device:TPU:0, one launch (start us, length us, event | category | flops | bytes accessed | tf_op | source)
XLA Modules:
  0.0 73.3 jit_solution(8162324129621185868)
XLA Ops:
  0.0 4.7 %shard_map.91 = (bf16[6,384,1024]{2,1,0:T(8,128)(2,1)S(1)}, bf16[1024,256]{1,0:T(8,128)(2,1)S(1)}, f32[192,1024]{1,0:T(8,128)S(1)}, f32[192,128]{1,0:T(8,128)S(1...) custom-call(s32[3,768]{1,0:T(4,128)} %refs_0_.3, ...), custom_call_target="tpu_custom_call" | custom-call | flops 1207959552 | bytes 6039797 | tf_op jit(solution)/shard_map/pallas_call | solution.py:307
  4.8 0.6 collective-permute-start.1
  5.4 0.4 collective-permute-start.5
  5.9 1.0 %shard_map.92 = (bf16[2,384,1024]{2,1,0:T(8,128)(2,1)S(1)}, f32[192,128]{1,0:T(8,128)S(1)}, f32[192,128]{1,0:T(8,128)S(1)}) custom-call(f32[192,1024]{1,0:T(8,128)S(1)} %get-tuple-element.29.refs_0_, bf16[1024,256]{1,0:T(8,128)(2,1)S(1)} %get-tuple-element.30.refs_1_), custom_call_target="tpu_custom_call" | custom-call | flops 301989888 | bytes 1509949 | tf_op jit(solution)/shard_map/pallas_call | solution.py:307
  6.9 0.1 collective-permute-start
  7.1 3.0 %collective-permute-start.2 = (f32[192,128]{1,0:T(8,128)S(1)}, f32[192,128]{1,0:T(8,128)S(1)}, u32[]{:S(2)}, u32[]{:S(2)}) collective-permute-start(f32[192,128]{1,0:T(8,128)S(1)} %add.61), channel_id=1, source_target_pairs={{0,1},{1,0},{2,3},{3,2},{4,5},{5,4},{6,7},{7,6},{8,9},{9,8},{10,11... | collective-permute-start | bytes 294920 | tf_op jit(solution)/shard_map/ppermute | solution.py:46
  10.1 1.6 %collective-permute-start.4 = (f32[192,128]{1,0:T(8,128)S(1)}, f32[192,128]{1,0:T(8,128)S(1)}, u32[]{:S(2)}, u32[]{:S(2)}) collective-permute-start(f32[192,128]{1,0:T(8,128)S(1)} %add.63), channel_id=1, source_target_pairs={{0,16},{1,17},{2,18},{3,19},{4,20},{5,21},{6,22},{7,23},{8,24},{9,... | collective-permute-start | bytes 294920 | tf_op jit(solution)/shard_map/ppermute | solution.py:46
  11.8 1.3 %collective-permute-done.2 = f32[192,128]{1,0:T(8,128)S(1)} collective-permute-done((f32[192,128]{1,0:T(8,128)S(1)}, f32[192,128]{1,0:T(8,128)S(1)}, u32[]{:S(2)}, u32[]{:S(2)}) %collective-permute-start.2) | collective-permute-done | bytes 98336 | tf_op jit(solution)/shard_map/ppermute | solution.py:46
  13.1 2.8 %collective-permute-done.4 = f32[192,128]{1,0:T(8,128)S(1)} collective-permute-done((f32[192,128]{1,0:T(8,128)S(1)}, f32[192,128]{1,0:T(8,128)S(1)}, u32[]{:S(2)}, u32[]{:S(2)}) %collective-permute-start.4) | collective-permute-done | bytes 98336 | tf_op jit(solution)/shard_map/ppermute | solution.py:46
  15.9 1.3 %collective-permute-done.6 = f32[192,128]{1,0:T(8,128)S(1)} collective-permute-done((f32[192,128]{1,0:T(8,128)S(1)}, f32[192,128]{1,0:T(8,128)S(1)}, u32[]{:S(2)}, u32[]{:S(2)}) %collective-permute-start.6) | collective-permute-done | bytes 98336 | tf_op jit(solution)/shard_map/ppermute | solution.py:46
  17.3 1.6 %collective-permute-start.9 = (f32[192,128]{1,0:T(8,128)S(1)}, f32[192,128]{1,0:T(8,128)S(1)}, u32[]{:S(2)}, u32[]{:S(2)}) collective-permute-start(f32[192,128]{1,0:T(8,128)S(1)} %add_add_fusion.1), channel_id=1, source_target_pairs={{0,2},{1,3},{2,0},{3,1},{4,6},{5,7},{6,4},{7,5},{8,10},{9,11},{10,... | collective-permute-start | bytes 294920 | tf_op jit(solution)/shard_map/ppermute | solution.py:54
  18.9 2.6 %collective-permute-start.8 = (f32[192,128]{1,0:T(8,128)S(1)}, f32[192,128]{1,0:T(8,128)S(1)}, u32[]{:S(2)}, u32[]{:S(2)}) collective-permute-start(f32[192,128]{1,0:T(8,128)S(1)} %add_add_fusion.1), channel_id=1, source_target_pairs={{0,4},{1,5},{2,6},{3,7},{4,0},{5,1},{6,2},{7,3},{8,12},{9,13},{10,... | collective-permute-start | bytes 294920 | tf_op jit(solution)/shard_map/ppermute | solution.py:54
  21.5 0.2 collective-permute-start.7
  21.7 4.2 %shard_map.93 = (bf16[4,512,1536]{2,1,0:T(8,128)(2,1)S(1)}, f32[192,128]{1,0:T(8,128)S(1)}, f32[192,128]{1,0:T(8,128)S(1)}) custom-call(s32[3,768]{1,0:T(4,128)S(1)} %copy-done.8, s32[3,1024]{1,0:T(4,128)S(1)} %copy-done.7, f32[2,768,128]{2,1,0:T(8,128)S(1)} %copy-done.6), custom_call_target="tpu_custom_call" | custom-call | flops 1207959552 | bytes 6039797 | tf_op jit(solution)/shard_map/pallas_call | solution.py:307
  26.0 0.8 %collective-permute-done.8 = f32[192,128]{1,0:T(8,128)S(1)} collective-permute-done((f32[192,128]{1,0:T(8,128)S(1)}, f32[192,128]{1,0:T(8,128)S(1)}, u32[]{:S(2)}, u32[]{:S(2)}) %collective-permute-start.8) | collective-permute-done | bytes 98336 | tf_op jit(solution)/shard_map/ppermute | solution.py:54
  26.8 1.2 %collective-permute-done.7 = f32[192,128]{1,0:T(8,128)S(1)} collective-permute-done((f32[192,128]{1,0:T(8,128)S(1)}, f32[192,128]{1,0:T(8,128)S(1)}, u32[]{:S(2)}, u32[]{:S(2)}) %collective-permute-start.7) | collective-permute-done | bytes 98336 | tf_op jit(solution)/shard_map/ppermute | solution.py:54
  28.1 1.3 %collective-permute-start.12 = (f32[192,128]{1,0:T(8,128)S(1)}, f32[192,128]{1,0:T(8,128)S(1)}, u32[]{:S(2)}, u32[]{:S(2)}) collective-permute-start(f32[192,128]{1,0:T(8,128)S(1)} %add_multiply_fusion.1.refs_0_), channel_id=1, source_target_pairs={{0,17},{1,16},{2,19},{3,18},{4,21},{5,20},{6,23},{7,22},{8,25},{9,... | collective-permute-start | bytes 294920 | tf_op jit(solution)/shard_map/ppermute | solution.py:46
  29.4 1.5 %collective-permute-start.11 = (f32[192,128]{1,0:T(8,128)S(1)}, f32[192,128]{1,0:T(8,128)S(1)}, u32[]{:S(2)}, u32[]{:S(2)}) collective-permute-start(f32[192,128]{1,0:T(8,128)S(1)} %add_multiply_fusion.1.refs_0_), channel_id=1, source_target_pairs={{0,16},{1,17},{2,18},{3,19},{4,20},{5,21},{6,22},{7,23},{8,24},{9,... | collective-permute-start | bytes 294920 | tf_op jit(solution)/shard_map/ppermute | solution.py:46
  30.9 0.8 %collective-permute-start.10 = (f32[192,128]{1,0:T(8,128)S(1)}, f32[192,128]{1,0:T(8,128)S(1)}, u32[]{:S(2)}, u32[]{:S(2)}) collective-permute-start(f32[192,128]{1,0:T(8,128)S(1)} %add_multiply_fusion.1.refs_0_), channel_id=1, source_target_pairs={{0,1},{1,0},{2,3},{3,2},{4,5},{5,4},{6,7},{7,6},{8,9},{9,8},{10,11... | collective-permute-start | bytes 294920 | tf_op jit(solution)/shard_map/ppermute | solution.py:46
  31.6 2.1 %collective-permute-done.12.refs_3_ = f32[192,128]{1,0:T(8,128)S(1)} collective-permute-done((f32[192,128]{1,0:T(8,128)S(1)}, f32[192,128]{1,0:T(8,128)S(1)}, u32[]{:S(2)}, u32[]{:S(2)}) %collective-permute-start.12) | collective-permute-done | bytes 98336 | tf_op jit(solution)/shard_map/ppermute | solution.py:46
  33.7 1.0 %collective-permute-done.11.refs_2_ = f32[192,128]{1,0:T(8,128)S(1)} collective-permute-done((f32[192,128]{1,0:T(8,128)S(1)}, f32[192,128]{1,0:T(8,128)S(1)}, u32[]{:S(2)}, u32[]{:S(2)}) %collective-permute-start.11) | collective-permute-done | bytes 98336 | tf_op jit(solution)/shard_map/ppermute | solution.py:46
  34.7 0.8 %collective-permute-done.10.refs_1_ = f32[192,128]{1,0:T(8,128)S(1)} collective-permute-done((f32[192,128]{1,0:T(8,128)S(1)}, f32[192,128]{1,0:T(8,128)S(1)}, u32[]{:S(2)}, u32[]{:S(2)}) %collective-permute-start.10) | collective-permute-done | bytes 98336 | tf_op jit(solution)/shard_map/ppermute | solution.py:46
  35.5 0.5 collective-permute-done.15.refs_6_
  36.0 0.8 %collective-permute-done.14.refs_5_ = f32[192,128]{1,0:T(8,128)S(1)} collective-permute-done((f32[192,128]{1,0:T(8,128)S(1)}, f32[192,128]{1,0:T(8,128)S(1)}, u32[]{:S(2)}, u32[]{:S(2)}) %collective-permute-start.14) | collective-permute-done | bytes 98336 | tf_op jit(solution)/shard_map/ppermute | solution.py:46
  36.8 4.6 %shard_map.94 = (f32[1024,128]{1,0:T(8,128)S(1)}, f32[192,128]{1,0:T(8,128)S(1)}, f32[192,128]{1,0:T(8,128)S(1)}, f32[192,128]{1,0:T(8,128)S(1)}, f32[192,128]{1...) custom-call(f32[192,128]{1,0:T(8,128)S(1)} %add_multiply_fusion.1.re, ...), custom_call_target="tpu_custom_call" | custom-call | flops 1207959552 | bytes 6039797 | tf_op jit(solution)/shard_map/pallas_call | solution.py:307
  41.4 0.2 collective-permute-start.18
  41.6 0.4 collective-permute-start.20
  42.1 0.4 collective-permute-start.17
  42.5 0.3 collective-permute-done.18
  42.8 0.8 %collective-permute-start.19 = (f32[192,128]{1,0:T(8,128)S(1)}, f32[192,128]{1,0:T(8,128)S(1)}, u32[]{:S(2)}, u32[]{:S(2)}) collective-permute-start(f32[192,128]{1,0:T(8,128)S(1)} %add.71), channel_id=1, source_target_pairs={{0,1},{1,0},{2,3},{3,2},{4,5},{5,4},{6,7},{7,6},{8,9},{9,8},{10,11... | collective-permute-start | bytes 294920 | tf_op jit(solution)/shard_map/ppermute | solution.py:46
  43.6 1.2 %collective-permute-start.21 = (f32[192,128]{1,0:T(8,128)S(1)}, f32[192,128]{1,0:T(8,128)S(1)}, u32[]{:S(2)}, u32[]{:S(2)}) collective-permute-start(f32[192,128]{1,0:T(8,128)S(1)} %add.73), channel_id=1, source_target_pairs={{0,16},{1,17},{2,18},{3,19},{4,20},{5,21},{6,22},{7,23},{8,24},{9,... | collective-permute-start | bytes 294920 | tf_op jit(solution)/shard_map/ppermute | solution.py:46
  44.8 1.7 %collective-permute-start.23 = (f32[192,128]{1,0:T(8,128)S(1)}, f32[192,128]{1,0:T(8,128)S(1)}, u32[]{:S(2)}, u32[]{:S(2)}) collective-permute-start(f32[192,128]{1,0:T(8,128)S(1)} %add.75), channel_id=1, source_target_pairs={{0,17},{1,16},{2,19},{3,18},{4,21},{5,20},{6,23},{7,22},{8,25},{9,... | collective-permute-start | bytes 294920 | tf_op jit(solution)/shard_map/ppermute | solution.py:46
  46.5 1.4 %collective-permute-done.19 = f32[192,128]{1,0:T(8,128)S(1)} collective-permute-done((f32[192,128]{1,0:T(8,128)S(1)}, f32[192,128]{1,0:T(8,128)S(1)}, u32[]{:S(2)}, u32[]{:S(2)}) %collective-permute-start.19) | collective-permute-done | bytes 98336 | tf_op jit(solution)/shard_map/ppermute | solution.py:46
  47.9 2.6 %collective-permute-done.21 = f32[192,128]{1,0:T(8,128)S(1)} collective-permute-done((f32[192,128]{1,0:T(8,128)S(1)}, f32[192,128]{1,0:T(8,128)S(1)}, u32[]{:S(2)}, u32[]{:S(2)}) %collective-permute-start.21) | collective-permute-done | bytes 98336 | tf_op jit(solution)/shard_map/ppermute | solution.py:46
  50.5 1.6 %collective-permute-start.26 = (f32[192,128]{1,0:T(8,128)S(1)}, f32[192,128]{1,0:T(8,128)S(1)}, u32[]{:S(2)}, u32[]{:S(2)}) collective-permute-start(f32[192,128]{1,0:T(8,128)S(1)} %add_add_fusion), channel_id=1, source_target_pairs={{0,2},{1,3},{2,0},{3,1},{4,6},{5,7},{6,4},{7,5},{8,10},{9,11},{10,... | collective-permute-start | bytes 294920 | tf_op jit(solution)/shard_map/ppermute | solution.py:54
  52.1 1.3 %collective-permute-start.25 = (f32[192,128]{1,0:T(8,128)S(1)}, f32[192,128]{1,0:T(8,128)S(1)}, u32[]{:S(2)}, u32[]{:S(2)}) collective-permute-start(f32[192,128]{1,0:T(8,128)S(1)} %add_add_fusion), channel_id=1, source_target_pairs={{0,4},{1,5},{2,6},{3,7},{4,0},{5,1},{6,2},{7,3},{8,12},{9,13},{10,... | collective-permute-start | bytes 294920 | tf_op jit(solution)/shard_map/ppermute | solution.py:54
  53.4 1.5 %collective-permute-start.24 = (f32[192,128]{1,0:T(8,128)S(1)}, f32[192,128]{1,0:T(8,128)S(1)}, u32[]{:S(2)}, u32[]{:S(2)}) collective-permute-start(f32[192,128]{1,0:T(8,128)S(1)} %add_add_fusion), channel_id=1, source_target_pairs={{0,6},{1,7},{2,4},{3,5},{4,2},{5,3},{6,0},{7,1},{8,14},{9,15},{10,... | collective-permute-start | bytes 294920 | tf_op jit(solution)/shard_map/ppermute | solution.py:54
  54.9 1.1 %collective-permute-done.26 = f32[192,128]{1,0:T(8,128)S(1)} collective-permute-done((f32[192,128]{1,0:T(8,128)S(1)}, f32[192,128]{1,0:T(8,128)S(1)}, u32[]{:S(2)}, u32[]{:S(2)}) %collective-permute-start.26) | collective-permute-done | bytes 98336 | tf_op jit(solution)/shard_map/ppermute | solution.py:54
  56.0 5.5 %collective-permute-done.25 = f32[192,128]{1,0:T(8,128)S(1)} collective-permute-done((f32[192,128]{1,0:T(8,128)S(1)}, f32[192,128]{1,0:T(8,128)S(1)}, u32[]{:S(2)}, u32[]{:S(2)}) %collective-permute-start.25) | collective-permute-done | bytes 98336 | tf_op jit(solution)/shard_map/ppermute | solution.py:54
  61.6 1.4 %collective-permute-start.29 = (f32[192,128]{1,0:T(8,128)S(1)}, f32[192,128]{1,0:T(8,128)S(1)}, u32[]{:S(2)}, u32[]{:S(2)}) collective-permute-start(f32[192,128]{1,0:T(8,128)S(1)} %add_multiply_fusion.refs_0_), channel_id=1, source_target_pairs={{0,17},{1,16},{2,19},{3,18},{4,21},{5,20},{6,23},{7,22},{8,25},{9,... | collective-permute-start | bytes 294920 | tf_op jit(solution)/shard_map/ppermute | solution.py:46
  63.0 0.8 %collective-permute-start.28 = (f32[192,128]{1,0:T(8,128)S(1)}, f32[192,128]{1,0:T(8,128)S(1)}, u32[]{:S(2)}, u32[]{:S(2)}) collective-permute-start(f32[192,128]{1,0:T(8,128)S(1)} %add_multiply_fusion.refs_0_), channel_id=1, source_target_pairs={{0,16},{1,17},{2,18},{3,19},{4,20},{5,21},{6,22},{7,23},{8,24},{9,... | collective-permute-start | bytes 294920 | tf_op jit(solution)/shard_map/ppermute | solution.py:46
  63.7 1.4 %collective-permute-start.27 = (f32[192,128]{1,0:T(8,128)S(1)}, f32[192,128]{1,0:T(8,128)S(1)}, u32[]{:S(2)}, u32[]{:S(2)}) collective-permute-start(f32[192,128]{1,0:T(8,128)S(1)} %add_multiply_fusion.refs_0_), channel_id=1, source_target_pairs={{0,1},{1,0},{2,3},{3,2},{4,5},{5,4},{6,7},{7,6},{8,9},{9,8},{10,11... | collective-permute-start | bytes 294920 | tf_op jit(solution)/shard_map/ppermute | solution.py:46
  65.1 2.1 %collective-permute-done.29.refs_3_ = f32[192,128]{1,0:T(8,128)S(1)} collective-permute-done((f32[192,128]{1,0:T(8,128)S(1)}, f32[192,128]{1,0:T(8,128)S(1)}, u32[]{:S(2)}, u32[]{:S(2)}) %collective-permute-start.29) | collective-permute-done | bytes 98336 | tf_op jit(solution)/shard_map/ppermute | solution.py:46
  67.2 1.0 %collective-permute-done.28.refs_2_ = f32[192,128]{1,0:T(8,128)S(1)} collective-permute-done((f32[192,128]{1,0:T(8,128)S(1)}, f32[192,128]{1,0:T(8,128)S(1)}, u32[]{:S(2)}, u32[]{:S(2)}) %collective-permute-start.28) | collective-permute-done | bytes 98336 | tf_op jit(solution)/shard_map/ppermute | solution.py:46
  68.3 0.4 collective-permute-start.31
  68.7 0.8 %collective-permute-done.32.refs_6_ = f32[192,128]{1,0:T(8,128)S(1)} collective-permute-done((f32[192,128]{1,0:T(8,128)S(1)}, f32[192,128]{1,0:T(8,128)S(1)}, u32[]{:S(2)}, u32[]{:S(2)}) %collective-permute-start.32) | collective-permute-done | bytes 98336 | tf_op jit(solution)/shard_map/ppermute | solution.py:46
  69.5 0.2 collective-permute-done.31.refs_5_
  69.7 3.6 %shard_map.95 = f32[1024,128]{1,0:T(8,128)} custom-call(f32[192,128]{1,0:T(8,128)S(1)} %add_multiply_fusion.refs_0_, f32[192,128]{1,0:T(8,128)S(1)} %collective-permute-done.27.refs_1_, f32[192,128]{1,0:T(8,128)S(1)} %collective-permute-done.28.refs_2_, f32[192,128]{1,0:T(8,128)S(1)} %collective-permute-done.29.refs_3_, ...), custom_call_target="tpu_custom_call" | custom-call | flops 1207959552 | bytes 6039797 | tf_op jit(solution)/shard_map/pallas_call | solution.py:307
  (53 shorter events, 0.7 us)
Async XLA Ops:
  0.0 21.7 %copy-start.8 = (s32[3,768]{1,0:T(4,128)S(1)}, s32[3,768]{1,0:T(4,128)}, u32[]{:S(2)}) copy-start(s32[3,768]{1,0:T(4,128)} %refs_0_.3) | copy-start | bytes 27652
  0.0 21.7 %copy-start.7 = (s32[3,1024]{1,0:T(4,128)S(1)}, s32[3,1024]{1,0:T(4,128)}, u32[]{:S(2)}) copy-start(s32[3,1024]{1,0:T(4,128)} %refs_1_.3) | copy-start | bytes 36868
  0.0 21.7 %copy-start.6 = (f32[2,768,128]{2,1,0:T(8,128)S(1)}, f32[2,768,128]{2,1,0:T(8,128)}, u32[]{:S(2)}) copy-start(f32[2,768,128]{2,1,0:T(8,128)} %refs_2_.3) | copy-start | bytes 2359300
  4.7 32.1 %copy-start = (f32[2,128,128]{2,1,0:T(8,128)S(1)}, f32[2,128,128]{2,1,0:T(8,128)}, u32[]{:S(2)}) copy-start(f32[2,128,128]{2,1,0:T(8,128)} %refs_11_.3) | copy-start | bytes 393220
  4.7 32.1 %copy-start.1 = (f32[2,128,128]{2,1,0:T(8,128)S(1)}, f32[2,128,128]{2,1,0:T(8,128)}, u32[]{:S(2)}) copy-start(f32[2,128,128]{2,1,0:T(8,128)} %refs_13_.3) | copy-start | bytes 393220
  4.7 32.1 %copy-start.2 = (f32[1024,128]{1,0:T(8,128)S(1)}, f32[1024,128]{1,0:T(8,128)}, u32[]{:S(2)}) copy-start(f32[1024,128]{1,0:T(8,128)} %refs_9_.1) | copy-start | bytes 1572868
  4.8 32.0 %copy-start.3 = (f32[2,128,128]{2,1,0:T(8,128)S(1)}, f32[2,128,128]{2,1,0:T(8,128)}, u32[]{:S(2)}) copy-start(f32[2,128,128]{2,1,0:T(8,128)} %refs_14_.1) | copy-start | bytes 393220
  4.8 32.0 %copy-start.4 = (f32[2,128]{1,0:T(2,128)S(1)}, f32[2,128]{1,0:T(2,128)}, u32[]{:S(2)}) copy-start(f32[2,128]{1,0:T(2,128)} %refs_10_.3) | copy-start | bytes 3076
  4.8 32.0 %copy-start.5 = (f32[2,128]{1,0:T(2,128)S(1)}, f32[2,128]{1,0:T(2,128)}, u32[]{:S(2)}) copy-start(f32[2,128]{1,0:T(2,128)} %refs_12_.3) | copy-start | bytes 3076
  4.8 2.3 %collective-permute-start.1 = (f32[192,128]{1,0:T(8,128)S(1)}, f32[192,128]{1,0:T(8,128)S(1)}, u32[]{:S(2)}, u32[]{:S(2)}) collective-permute-start(f32[192,128]{1,0:T(8,128)S(1)} %get-tuple-element.34), channel_id=1, source_target_pairs={{0,8},{1,9},{2,10},{3,11},{4,12},{5,13},{6,14},{7,15},{8,0},{9,1},... | collective-permute-start | bytes 294920 | tf_op jit(solution)/shard_map/ppermute | solution.py:46
  5.4 4.7 %collective-permute-start.3 = (f32[192,128]{1,0:T(8,128)S(1)}, f32[192,128]{1,0:T(8,128)S(1)}, u32[]{:S(2)}, u32[]{:S(2)}) collective-permute-start(f32[192,128]{1,0:T(8,128)S(1)} %get-tuple-element.36), channel_id=1, source_target_pairs={{0,8},{1,9},{2,10},{3,11},{4,12},{5,13},{6,14},{7,15},{8,0},{9,1},... | collective-permute-start | bytes 294920 | tf_op jit(solution)/shard_map/ppermute | solution.py:46
  5.4 6.2 %collective-permute-start.5 = (f32[192,128]{1,0:T(8,128)S(1)}, f32[192,128]{1,0:T(8,128)S(1)}, u32[]{:S(2)}, u32[]{:S(2)}) collective-permute-start(f32[192,128]{1,0:T(8,128)S(1)} %get-tuple-element.38), channel_id=1, source_target_pairs={{0,8},{1,9},{2,10},{3,11},{4,12},{5,13},{6,14},{7,15},{8,0},{9,1},... | collective-permute-start | bytes 294920 | tf_op jit(solution)/shard_map/ppermute | solution.py:46
  6.9 4.8 %collective-permute-start = (f32[192,128]{1,0:T(8,128)S(1)}, f32[192,128]{1,0:T(8,128)S(1)}, u32[]{:S(2)}, u32[]{:S(2)}) collective-permute-start(f32[192,128]{1,0:T(8,128)S(1)} %get-tuple-element.32), channel_id=1, source_target_pairs={{0,8},{1,9},{2,10},{3,11},{4,12},{5,13},{6,14},{7,15},{8,0},{9,1},... | collective-permute-start | bytes 294920 | tf_op jit(solution)/shard_map/ppermute | solution.py:46
  7.1 6.0 %collective-permute-start.2 = (f32[192,128]{1,0:T(8,128)S(1)}, f32[192,128]{1,0:T(8,128)S(1)}, u32[]{:S(2)}, u32[]{:S(2)}) collective-permute-start(f32[192,128]{1,0:T(8,128)S(1)} %add.61), channel_id=1, source_target_pairs={{0,1},{1,0},{2,3},{3,2},{4,5},{5,4},{6,7},{7,6},{8,9},{9,8},{10,11... | collective-permute-start | bytes 294920 | tf_op jit(solution)/shard_map/ppermute | solution.py:46
  10.1 5.9 %collective-permute-start.4 = (f32[192,128]{1,0:T(8,128)S(1)}, f32[192,128]{1,0:T(8,128)S(1)}, u32[]{:S(2)}, u32[]{:S(2)}) collective-permute-start(f32[192,128]{1,0:T(8,128)S(1)} %add.63), channel_id=1, source_target_pairs={{0,16},{1,17},{2,18},{3,19},{4,20},{5,21},{6,22},{7,23},{8,24},{9,... | collective-permute-start | bytes 294920 | tf_op jit(solution)/shard_map/ppermute | solution.py:46
  11.7 5.6 %collective-permute-start.6 = (f32[192,128]{1,0:T(8,128)S(1)}, f32[192,128]{1,0:T(8,128)S(1)}, u32[]{:S(2)}, u32[]{:S(2)}) collective-permute-start(f32[192,128]{1,0:T(8,128)S(1)} %add.65), channel_id=1, source_target_pairs={{0,17},{1,16},{2,19},{3,18},{4,21},{5,20},{6,23},{7,22},{8,25},{9,... | collective-permute-start | bytes 294920 | tf_op jit(solution)/shard_map/ppermute | solution.py:46
  17.3 8.7 %collective-permute-start.9 = (f32[192,128]{1,0:T(8,128)S(1)}, f32[192,128]{1,0:T(8,128)S(1)}, u32[]{:S(2)}, u32[]{:S(2)}) collective-permute-start(f32[192,128]{1,0:T(8,128)S(1)} %add_add_fusion.1), channel_id=1, source_target_pairs={{0,2},{1,3},{2,0},{3,1},{4,6},{5,7},{6,4},{7,5},{8,10},{9,11},{10,... | collective-permute-start | bytes 294920 | tf_op jit(solution)/shard_map/ppermute | solution.py:54
  18.9 7.9 %collective-permute-start.8 = (f32[192,128]{1,0:T(8,128)S(1)}, f32[192,128]{1,0:T(8,128)S(1)}, u32[]{:S(2)}, u32[]{:S(2)}) collective-permute-start(f32[192,128]{1,0:T(8,128)S(1)} %add_add_fusion.1), channel_id=1, source_target_pairs={{0,4},{1,5},{2,6},{3,7},{4,0},{5,1},{6,2},{7,3},{8,12},{9,13},{10,... | collective-permute-start | bytes 294920 | tf_op jit(solution)/shard_map/ppermute | solution.py:54
  21.5 6.5 %collective-permute-start.7 = (f32[192,128]{1,0:T(8,128)S(1)}, f32[192,128]{1,0:T(8,128)S(1)}, u32[]{:S(2)}, u32[]{:S(2)}) collective-permute-start(f32[192,128]{1,0:T(8,128)S(1)} %add_add_fusion.1), channel_id=1, source_target_pairs={{0,6},{1,7},{2,4},{3,5},{4,2},{5,3},{6,0},{7,1},{8,14},{9,15},{10,... | collective-permute-start | bytes 294920 | tf_op jit(solution)/shard_map/ppermute | solution.py:54
  28.1 5.7 %collective-permute-start.12 = (f32[192,128]{1,0:T(8,128)S(1)}, f32[192,128]{1,0:T(8,128)S(1)}, u32[]{:S(2)}, u32[]{:S(2)}) collective-permute-start(f32[192,128]{1,0:T(8,128)S(1)} %add_multiply_fusion.1.refs_0_), channel_id=1, source_target_pairs={{0,17},{1,16},{2,19},{3,18},{4,21},{5,20},{6,23},{7,22},{8,25},{9,... | collective-permute-start | bytes 294920 | tf_op jit(solution)/shard_map/ppermute | solution.py:46
  29.4 5.4 %collective-permute-start.11 = (f32[192,128]{1,0:T(8,128)S(1)}, f32[192,128]{1,0:T(8,128)S(1)}, u32[]{:S(2)}, u32[]{:S(2)}) collective-permute-start(f32[192,128]{1,0:T(8,128)S(1)} %add_multiply_fusion.1.refs_0_), channel_id=1, source_target_pairs={{0,16},{1,17},{2,18},{3,19},{4,20},{5,21},{6,22},{7,23},{8,24},{9,... | collective-permute-start | bytes 294920 | tf_op jit(solution)/shard_map/ppermute | solution.py:46
  30.9 4.6 %collective-permute-start.10 = (f32[192,128]{1,0:T(8,128)S(1)}, f32[192,128]{1,0:T(8,128)S(1)}, u32[]{:S(2)}, u32[]{:S(2)}) collective-permute-start(f32[192,128]{1,0:T(8,128)S(1)} %add_multiply_fusion.1.refs_0_), channel_id=1, source_target_pairs={{0,1},{1,0},{2,3},{3,2},{4,5},{5,4},{6,7},{7,6},{8,9},{9,8},{10,11... | collective-permute-start | bytes 294920 | tf_op jit(solution)/shard_map/ppermute | solution.py:46
  31.6 3.9 %collective-permute-start.13 = (f32[192,128]{1,0:T(8,128)S(1)}, f32[192,128]{1,0:T(8,128)S(1)}, u32[]{:S(2)}, u32[]{:S(2)}) collective-permute-start(f32[192,128]{1,0:T(8,128)S(1)} %add_multiply_fusion.1.refs_0_), channel_id=1, source_target_pairs={{0,8},{1,9},{2,10},{3,11},{4,12},{5,13},{6,14},{7,15},{8,0},{9,1},... | collective-permute-start | bytes 294920 | tf_op jit(solution)/shard_map/ppermute | solution.py:46
  33.7 1.8 %collective-permute-start.16 = (f32[192,128]{1,0:T(8,128)S(1)}, f32[192,128]{1,0:T(8,128)S(1)}, u32[]{:S(2)}, u32[]{:S(2)}) collective-permute-start(f32[192,128]{1,0:T(8,128)S(1)} %collective-permute-done.12.refs_3_), channel_id=1, source_target_pairs={{0,8},{1,9},{2,10},{3,11},{4,12},{5,13},{6,14},{7,15},{8,0},{9,1},... | collective-permute-start | bytes 294920 | tf_op jit(solution)/shard_map/ppermute | solution.py:46
  34.7 1.3 %collective-permute-start.15 = (f32[192,128]{1,0:T(8,128)S(1)}, f32[192,128]{1,0:T(8,128)S(1)}, u32[]{:S(2)}, u32[]{:S(2)}) collective-permute-start(f32[192,128]{1,0:T(8,128)S(1)} %collective-permute-done.11.refs_2_), channel_id=1, source_target_pairs={{0,8},{1,9},{2,10},{3,11},{4,12},{5,13},{6,14},{7,15},{8,0},{9,1},... | collective-permute-start | bytes 294920 | tf_op jit(solution)/shard_map/ppermute | solution.py:46
  35.5 1.3 %collective-permute-start.14 = (f32[192,128]{1,0:T(8,128)S(1)}, f32[192,128]{1,0:T(8,128)S(1)}, u32[]{:S(2)}, u32[]{:S(2)}) collective-permute-start(f32[192,128]{1,0:T(8,128)S(1)} %collective-permute-done.10.refs_1_), channel_id=1, source_target_pairs={{0,8},{1,9},{2,10},{3,11},{4,12},{5,13},{6,14},{7,15},{8,0},{9,1},... | collective-permute-start | bytes 294920 | tf_op jit(solution)/shard_map/ppermute | solution.py:46
  41.4 1.4 %collective-permute-start.18 = (f32[192,128]{1,0:T(8,128)S(1)}, f32[192,128]{1,0:T(8,128)S(1)}, u32[]{:S(2)}, u32[]{:S(2)}) collective-permute-start(f32[192,128]{1,0:T(8,128)S(1)} %get-tuple-element.46), channel_id=1, source_target_pairs={{0,8},{1,9},{2,10},{3,11},{4,12},{5,13},{6,14},{7,15},{8,0},{9,1},... | collective-permute-start | bytes 294920 | tf_op jit(solution)/shard_map/ppermute | solution.py:46
  41.6 2.0 %collective-permute-start.20 = (f32[192,128]{1,0:T(8,128)S(1)}, f32[192,128]{1,0:T(8,128)S(1)}, u32[]{:S(2)}, u32[]{:S(2)}) collective-permute-start(f32[192,128]{1,0:T(8,128)S(1)} %get-tuple-element.48), channel_id=1, source_target_pairs={{0,8},{1,9},{2,10},{3,11},{4,12},{5,13},{6,14},{7,15},{8,0},{9,1},... | collective-permute-start | bytes 294920 | tf_op jit(solution)/shard_map/ppermute | solution.py:46
  42.0 2.8 %collective-permute-start.22 = (f32[192,128]{1,0:T(8,128)S(1)}, f32[192,128]{1,0:T(8,128)S(1)}, u32[]{:S(2)}, u32[]{:S(2)}) collective-permute-start(f32[192,128]{1,0:T(8,128)S(1)} %get-tuple-element.50), channel_id=1, source_target_pairs={{0,8},{1,9},{2,10},{3,11},{4,12},{5,13},{6,14},{7,15},{8,0},{9,1},... | collective-permute-start | bytes 294920 | tf_op jit(solution)/shard_map/ppermute | solution.py:46
  42.1 4.4 %collective-permute-start.17 = (f32[192,128]{1,0:T(8,128)S(1)}, f32[192,128]{1,0:T(8,128)S(1)}, u32[]{:S(2)}, u32[]{:S(2)}) collective-permute-start(f32[192,128]{1,0:T(8,128)S(1)} %get-tuple-element.44), channel_id=1, source_target_pairs={{0,8},{1,9},{2,10},{3,11},{4,12},{5,13},{6,14},{7,15},{8,0},{9,1},... | collective-permute-start | bytes 294920 | tf_op jit(solution)/shard_map/ppermute | solution.py:46
  42.8 5.1 %collective-permute-start.19 = (f32[192,128]{1,0:T(8,128)S(1)}, f32[192,128]{1,0:T(8,128)S(1)}, u32[]{:S(2)}, u32[]{:S(2)}) collective-permute-start(f32[192,128]{1,0:T(8,128)S(1)} %add.71), channel_id=1, source_target_pairs={{0,1},{1,0},{2,3},{3,2},{4,5},{5,4},{6,7},{7,6},{8,9},{9,8},{10,11... | collective-permute-start | bytes 294920 | tf_op jit(solution)/shard_map/ppermute | solution.py:46
  43.6 6.8 %collective-permute-start.21 = (f32[192,128]{1,0:T(8,128)S(1)}, f32[192,128]{1,0:T(8,128)S(1)}, u32[]{:S(2)}, u32[]{:S(2)}) collective-permute-start(f32[192,128]{1,0:T(8,128)S(1)} %add.73), channel_id=1, source_target_pairs={{0,16},{1,17},{2,18},{3,19},{4,20},{5,21},{6,22},{7,23},{8,24},{9,... | collective-permute-start | bytes 294920 | tf_op jit(solution)/shard_map/ppermute | solution.py:46
  44.8 5.6 %collective-permute-start.23 = (f32[192,128]{1,0:T(8,128)S(1)}, f32[192,128]{1,0:T(8,128)S(1)}, u32[]{:S(2)}, u32[]{:S(2)}) collective-permute-start(f32[192,128]{1,0:T(8,128)S(1)} %add.75), channel_id=1, source_target_pairs={{0,17},{1,16},{2,19},{3,18},{4,21},{5,20},{6,23},{7,22},{8,25},{9,... | collective-permute-start | bytes 294920 | tf_op jit(solution)/shard_map/ppermute | solution.py:46
  50.5 5.5 %collective-permute-start.26 = (f32[192,128]{1,0:T(8,128)S(1)}, f32[192,128]{1,0:T(8,128)S(1)}, u32[]{:S(2)}, u32[]{:S(2)}) collective-permute-start(f32[192,128]{1,0:T(8,128)S(1)} %add_add_fusion), channel_id=1, source_target_pairs={{0,2},{1,3},{2,0},{3,1},{4,6},{5,7},{6,4},{7,5},{8,10},{9,11},{10,... | collective-permute-start | bytes 294920 | tf_op jit(solution)/shard_map/ppermute | solution.py:54
  52.1 9.5 %collective-permute-start.25 = (f32[192,128]{1,0:T(8,128)S(1)}, f32[192,128]{1,0:T(8,128)S(1)}, u32[]{:S(2)}, u32[]{:S(2)}) collective-permute-start(f32[192,128]{1,0:T(8,128)S(1)} %add_add_fusion), channel_id=1, source_target_pairs={{0,4},{1,5},{2,6},{3,7},{4,0},{5,1},{6,2},{7,3},{8,12},{9,13},{10,... | collective-permute-start | bytes 294920 | tf_op jit(solution)/shard_map/ppermute | solution.py:54
  53.4 8.1 %collective-permute-start.24 = (f32[192,128]{1,0:T(8,128)S(1)}, f32[192,128]{1,0:T(8,128)S(1)}, u32[]{:S(2)}, u32[]{:S(2)}) collective-permute-start(f32[192,128]{1,0:T(8,128)S(1)} %add_add_fusion), channel_id=1, source_target_pairs={{0,6},{1,7},{2,4},{3,5},{4,2},{5,3},{6,0},{7,1},{8,14},{9,15},{10,... | collective-permute-start | bytes 294920 | tf_op jit(solution)/shard_map/ppermute | solution.py:54
  61.6 5.6 %collective-permute-start.29 = (f32[192,128]{1,0:T(8,128)S(1)}, f32[192,128]{1,0:T(8,128)S(1)}, u32[]{:S(2)}, u32[]{:S(2)}) collective-permute-start(f32[192,128]{1,0:T(8,128)S(1)} %add_multiply_fusion.refs_0_), channel_id=1, source_target_pairs={{0,17},{1,16},{2,19},{3,18},{4,21},{5,20},{6,23},{7,22},{8,25},{9,... | collective-permute-start | bytes 294920 | tf_op jit(solution)/shard_map/ppermute | solution.py:46
  63.0 5.2 %collective-permute-start.28 = (f32[192,128]{1,0:T(8,128)S(1)}, f32[192,128]{1,0:T(8,128)S(1)}, u32[]{:S(2)}, u32[]{:S(2)}) collective-permute-start(f32[192,128]{1,0:T(8,128)S(1)} %add_multiply_fusion.refs_0_), channel_id=1, source_target_pairs={{0,16},{1,17},{2,18},{3,19},{4,20},{5,21},{6,22},{7,23},{8,24},{9,... | collective-permute-start | bytes 294920 | tf_op jit(solution)/shard_map/ppermute | solution.py:46
  63.7 4.6 %collective-permute-start.27 = (f32[192,128]{1,0:T(8,128)S(1)}, f32[192,128]{1,0:T(8,128)S(1)}, u32[]{:S(2)}, u32[]{:S(2)}) collective-permute-start(f32[192,128]{1,0:T(8,128)S(1)} %add_multiply_fusion.refs_0_), channel_id=1, source_target_pairs={{0,1},{1,0},{2,3},{3,2},{4,5},{5,4},{6,7},{7,6},{8,9},{9,8},{10,11... | collective-permute-start | bytes 294920 | tf_op jit(solution)/shard_map/ppermute | solution.py:46
  65.1 3.6 %collective-permute-start.30 = (f32[192,128]{1,0:T(8,128)S(1)}, f32[192,128]{1,0:T(8,128)S(1)}, u32[]{:S(2)}, u32[]{:S(2)}) collective-permute-start(f32[192,128]{1,0:T(8,128)S(1)} %add_multiply_fusion.refs_0_), channel_id=1, source_target_pairs={{0,8},{1,9},{2,10},{3,11},{4,12},{5,13},{6,14},{7,15},{8,0},{9,1},... | collective-permute-start | bytes 294920 | tf_op jit(solution)/shard_map/ppermute | solution.py:46
  67.2 1.5 %collective-permute-start.33 = (f32[192,128]{1,0:T(8,128)S(1)}, f32[192,128]{1,0:T(8,128)S(1)}, u32[]{:S(2)}, u32[]{:S(2)}) collective-permute-start(f32[192,128]{1,0:T(8,128)S(1)} %collective-permute-done.29.refs_3_), channel_id=1, source_target_pairs={{0,8},{1,9},{2,10},{3,11},{4,12},{5,13},{6,14},{7,15},{8,0},{9,1},... | collective-permute-start | bytes 294920 | tf_op jit(solution)/shard_map/ppermute | solution.py:46
  68.2 1.3 %collective-permute-start.32 = (f32[192,128]{1,0:T(8,128)S(1)}, f32[192,128]{1,0:T(8,128)S(1)}, u32[]{:S(2)}, u32[]{:S(2)}) collective-permute-start(f32[192,128]{1,0:T(8,128)S(1)} %collective-permute-done.28.refs_2_), channel_id=1, source_target_pairs={{0,8},{1,9},{2,10},{3,11},{4,12},{5,13},{6,14},{7,15},{8,0},{9,1},... | collective-permute-start | bytes 294920 | tf_op jit(solution)/shard_map/ppermute | solution.py:46
  68.3 1.3 %collective-permute-start.31 = (f32[192,128]{1,0:T(8,128)S(1)}, f32[192,128]{1,0:T(8,128)S(1)}, u32[]{:S(2)}, u32[]{:S(2)}) collective-permute-start(f32[192,128]{1,0:T(8,128)S(1)} %collective-permute-done.27.refs_1_), channel_id=1, source_target_pairs={{0,8},{1,9},{2,10},{3,11},{4,12},{5,13},{6,14},{7,15},{8,0},{9,1},... | collective-permute-start | bytes 294920 | tf_op jit(solution)/shard_map/ppermute | solution.py:46

commit v2 on v1

--- a/solution.py
+++ b/solution.py
@@ -6,7 +6,7 @@
 from jax.sharding import PartitionSpec as P
 
 axes = ("outer", "atoms")
-first_limit, near_limit, table_limit, block_limit = (n * 2**20 for n in (10, 4, 8, 12))
+first_limit, near_limit, table_limit, block_limit = (n * 2**20 for n in (8, 6, 8, 12))
 turn_bits = 18
 half_sin = (0.10982699, -0.84611289, 3.60635441, -7.3082457, 4.44288292)
 half_cos = (0.31069819, -1.88356299, 5.73946117, -6.97885099, 1.4142135)
@@ -163,8 +163,8 @@
     return value
 
 
-def fill_tables(turns_ref, here, lanes, targets):
-    turns = turns_ref[here, lanes]
+def fill_tables(turns_ref, index, targets):
+    turns = turns_ref[index]
     t = turns - ((turns + to_integer) - to_integer)
     u = t * t
     s = horner(half_sin, u) * t
@@ -175,16 +175,17 @@
         ref[index] = value
 
 
-def fill_chunk(turns_ref, first_row, rows, table_ref, n):
+def fill_chunk(wave_columns, digit_rows, turns_ref, first_row, rows, table_ref, n):
+    chunk = wave_columns[pl.ds(pl.multiple_of(first_row, rows), rows), :]
+    turns_ref[n] = matmul(chunk, digit_rows[...])
     step, width = 32, 256
     for row in range(0, rows, step):
-        here = pl.ds(pl.multiple_of(first_row + row, step), step)
-        for at in range(0, turns_ref.shape[1], width):
+        for at in range(0, digit_rows.shape[1], width):
             lanes = slice(at, at + width)
             targets = [
                 (table_ref, (n, slice(kind * rows + row, kind * rows + row + step), lanes)) for kind in range(4)
             ]
-            fill_tables(turns_ref, here, lanes, targets)
+            fill_tables(turns_ref, (n, slice(row, row + step), lanes), targets)
 
 
 def project(table, pair, chunk_ref, rows):
@@ -193,13 +194,20 @@
     chunk_ref[...] = folded(both[: 2 * rows, :]) + both[2 * rows :, :width]
 
 
-def first_kernel(layout, rows, *refs):
+def fill_group(layout, rows, group, wave_columns, digit_rows, pair, table, chunks, turns):
+    for n, offset in enumerate(group):
+        row = layout.chunk_of(*offset) * rows
+        fill_chunk(wave_columns, digit_rows, turns, row, rows, table, n)
+        if n:
+            project(table[n - 1], pair[...], chunks[n - 1], rows)
+    project(table[len(group) - 1], pair[...], chunks[-1], rows)
+
+
+def first_kernel(layout, rows, group, *refs):
     sources, refs = refs[:4], refs[4:]
-    far = [o for o in layout.offsets() if o[1:] != (0, 0)]
-    near = [o for o in layout.offsets() if o[1:] == (0, 0)]
-    table, pair_out, near_turns = refs[:3]
-    chunks = refs[3 : 3 + len(far)]
-    wave_rows, digit_rows, turns, waves, positions, features, w_value, arrived = refs[3 + len(far) :]
+    wave_columns, digits_out, pair, table = refs[:4]
+    chunks = refs[4 : 4 + len(group)]
+    wave_rows, digit_rows, turns, waves, positions, features, w_value, arrived = refs[4 + len(group) :]
     copies = [
         pltpu.make_async_copy(source, target, arrived.at[n])
         for n, (source, target) in enumerate(zip(sources, (waves, positions, features, w_value)))
@@ -209,26 +217,24 @@
     copies[0].wait()
     copies[1].wait()
     operands(waves, positions, wave_rows, digit_rows)
-    turns[...] = contract_rows(wave_rows[...], digit_rows[...])
+    count = wave_rows.shape[0]
+    row, column = (lax.broadcasted_iota(jnp.int32, (count, count), axis) for axis in range(2))
+    unit = (row == column).astype(f32)
+    wave_columns[...] = contract_rows(wave_rows[...], unit).astype(bf16)
+    digits_out[...] = digit_rows[...].astype(bf16)
     copies[2].wait()
     copies[3].wait()
-    pair_out[...] = paired(product(features[...], stacked(w_value[0])))
-    for n, offset in enumerate(near):
-        here = pl.ds(pl.multiple_of(layout.chunk_of(*offset) * rows, rows), rows)
-        near_turns[n * rows : (n + 1) * rows, :] = turns[here, :]
-    for n, offset in enumerate(far):
-        fill_chunk(turns, layout.chunk_of(*offset) * rows, rows, table, n)
-        if n:
-            project(table[n - 1], pair_out[...], chunks[n - 1], rows)
-    project(table[len(far) - 1], pair_out[...], chunks[len(far) - 1], rows)
-
-
-def near_kernel(rows, turns, pair, table, *chunks):
-    for n in range(len(chunks)):
-        fill_chunk(turns, n * rows, rows, table, n)
-        if n:
-            project(table[n - 1], pair[...], chunks[n - 1], rows)
-    project(table[len(chunks) - 1], pair[...], chunks[-1], rows)
+    pair[...] = paired(product(features[...], stacked(w_value[0])))
+    fill_group(layout, rows, group, wave_columns, digits_out, pair, table, chunks, turns)
+
+
+def fill_kernel(layout, rows, group, wave_columns, digit_rows, pair, table, *refs):
+    fill_group(layout, rows, group, wave_columns, digit_rows, pair, table, refs[:-1], refs[-1])
+
+
+def project_kernel(rows, table, pair, *chunks):
+    for n, chunk in enumerate(chunks):
+        project(table[n], pair[...], chunk, rows)
 
 
 def atom_table_kernel(layout, rows, waves, positions, freq_filter, table, *refs):
@@ -254,7 +260,7 @@
                 for low in range(2)
                 for kind in range(2)
             ]
-            fill_tables(turns, here, slice(at, at + width), targets)
+            fill_tables(turns, (here, slice(at, at + width)), targets)
         return carry
 
     lax.fori_loop(0, atoms // step, body, 0)
@@ -265,8 +271,11 @@
     atom_table, current_ref, gain, w_hidden, b_hidden, w_output = refs[:6]
     refs = refs[6:]
     if not last:
-        w_value, far_table, near_table, refs = refs[0], refs[1], refs[2], refs[3:]
-    current_out, chunks_out, factor = refs[0], refs[1:-1], refs[-1]
+        w_value, table, refs = refs[0], refs[1], refs[2:]
+        pair_out, refs = refs[1], refs[:1] + refs[2:]
+        current_out, chunks_out, factor = refs[0], refs[1:-1], refs[-1]
+    else:
+        result, factor, current_out, sent = refs
     waves = rows * layout.chunks
     width = current_ref.shape[1]
     for offset, chunk in zip(layout.offsets(), chunks_in):
@@ -289,25 +298,27 @@
         hidden = hidden / (1.0 + jnp.exp(-hidden))
         current_out[here, :] = current_ref[here, :] + product(hidden, output_stack)
 
-    messages = back(0)
+    messages, copies = back(0), []
     for n in range(groups):
         coming = back(n + 1) if n + 1 < groups else None
         update(n, messages)
         messages = coming
+        if last:
+            here = pl.ds(n * step, step)
+            copies.append(pltpu.make_async_copy(current_out.at[here], result.at[here], sent.at[n]))
+            copies[-1].start()
     if not last:
-        pair = paired(product(current_out[...], stacked(w_value[block + 1])))
-        far = [n for n, o in enumerate(layout.offsets()) if o[1:] != (0, 0)]
-        near = [n for n, o in enumerate(layout.offsets()) if o[1:] == (0, 0)]
-        for table, members in ((far_table, far), (near_table, near)):
-            for at, n in enumerate(members):
-                project(table[at], pair, chunks_out[n], rows)
-
-
-def call(kernel, outputs, scratch, limit, flops, *inputs, space=pltpu.VMEM):
+        pair_out[...] = paired(product(current_out[...], stacked(w_value[block + 1])))
+        project_kernel(rows, table, pair_out, *chunks_out)
+    for copy in copies:
+        copy.wait()
+
+
+def call(kernel, outputs, scratch, limit, flops, *inputs, space=pltpu.VMEM, out_space=pltpu.VMEM):
     return pl.pallas_call(
         kernel,
         in_specs=[pl.BlockSpec(memory_space=space)] * len(inputs),
-        out_specs=[pl.BlockSpec(memory_space=pltpu.VMEM)] * len(outputs),
+        out_specs=[pl.BlockSpec(memory_space=out_space)] * len(outputs),
         out_shape=outputs,
         scratch_shapes=scratch,
         compiler_params=pltpu.CompilerParams(vmem_limit_bytes=limit),
@@ -327,19 +338,19 @@
     flops = 12 * waves * atoms * channels
     early = [wavevectors, positions, features, w_value]
     offsets = layout.offsets()
-    far = [o for o in offsets if o[1:] != (0, 0)]
-    near = [o for o in offsets if o[1:] == (0, 0)]
-    group = min(256, atoms)
+    squares = sorted({o[1:] for o in offsets})
+    members = {"far": squares[-1:], "mid": squares[1:-1], "near": squares[:1]}
+    groups = {name: [o for o in offsets if o[1:] in some] for name, some in members.items()}
+    table_of = lambda name: shape((len(groups[name]), 4 * rows, atoms), bf16)
+    chunks_of = lambda name: [chunk] * len(groups[name])
+    turns_of = lambda name: pltpu.VMEM((len(groups[name]), rows, atoms), f32)
+    pair_shape = shape((atoms, 2 * channels), bf16)
+    step = min(256, atoms)
     outs = call(
-        lambda *refs: first_kernel(layout, rows, *refs),
-        [
-            shape((len(far), 4 * rows, atoms), bf16),
-            shape((atoms, 2 * channels), bf16),
-            shape((len(near) * rows, atoms), f32),
-        ]
-        + [chunk] * len(far),
+        lambda *refs: first_kernel(layout, rows, groups["far"], *refs),
+        [shape((waves, 16), bf16), shape((16, atoms), bf16), pair_shape, table_of("far")] + chunks_of("far"),
         index_scratch
-        + [pltpu.VMEM((waves, atoms), f32)]
+        + [turns_of("far")]
         + [pltpu.VMEM(array.shape, array.dtype) for array in early]
         + [pltpu.SemaphoreType.DMA((len(early),))],
         first_limit,
@@ -347,22 +358,25 @@
         *[pltpu.with_memory_space_constraint(array, pltpu.HBM) for array in early],
         space=pltpu.HBM,
     )
-    far_table, pair, near_turns = outs[:3]
-    parts = dict(zip(far, outs[3:]))
-    outs = call(
-        lambda *refs: near_kernel(rows, *refs),
-        [shape((len(near), 4 * rows, atoms), bf16)] + [chunk] * len(near),
-        [],
-        near_limit,
-        flops // 4,
-        near_turns,
-        pair,
-    )
-    near_table = outs[0]
-    parts |= dict(zip(near, outs[1:]))
+    wave_columns, digit_rows, pair = outs[:3]
+    tables = {"far": outs[3]}
+    parts = dict(zip(groups["far"], outs[4:]))
+    for name in ("mid", "near"):
+        outs = call(
+            lambda *refs, name=name: fill_kernel(layout, rows, groups[name], *refs),
+            [table_of(name)] + chunks_of(name),
+            [turns_of(name)],
+            near_limit,
+            flops // 4,
+            wave_columns,
+            digit_rows,
+            pair,
+        )
+        tables[name] = outs[0]
+        parts |= dict(zip(groups[name], outs[1:]))
     outs = call(
         lambda *refs: atom_table_kernel(layout, rows, *refs),
-        [shape((atoms // group, 2 * group, 2 * waves), bf16)] + [chunk] * blocks,
+        [shape((atoms // step, 2 * step, 2 * waves), bf16)] + [chunk] * blocks,
         index_scratch + [pltpu.VMEM((atoms, waves), f32)],
         table_limit,
         flops,
@@ -377,19 +391,37 @@
         gathered = total(layout, parts, scales[block])
         inputs = [gathered[o] for o in offsets]
         inputs += [atom_table, current, norm_gain, w_hidden, b_hidden, w_output]
-        if not last:
-            inputs += [w_value, far_table, near_table]
+        outputs = [shape((atoms, channels), f32)]
+        scratch = [pltpu.VMEM((2 * waves, 2 * channels), bf16)]
+        if last:
+            scratch += [pltpu.VMEM((atoms, channels), f32), pltpu.SemaphoreType.DMA((atoms // step,))]
+        else:
+            inputs += [w_value, tables["far"]]
+            outputs += [pair_shape] + chunks_of("far")
         outs = call(
             lambda *refs, block=block, last=last: block_kernel(layout, rows, block, last, *refs),
-            [shape((atoms, channels), f32)] + ([] if last else [chunk] * layout.chunks),
-            [pltpu.VMEM((2 * waves, 2 * channels), bf16)],
+            outputs,
+            scratch,
             block_limit,
             flops,
             *inputs,
+            out_space=pltpu.HBM if last else pltpu.VMEM,
         )
         current = outs[0]
-        parts = dict(zip(offsets, outs[1:]))
-    return current
+        if last:
+            return current
+        pair, parts = outs[1], dict(zip(groups["far"], outs[2:]))
+        for name in ("mid", "near"):
+            outs = call(
+                lambda *refs: project_kernel(rows, *refs),
+                chunks_of(name),
+                [],
+                near_limit,
+                flops // 4,
+                tables[name],
+                pair,
+            )
+            parts |= dict(zip(groups[name], outs))
 
 
 def solution(mesh):
@@ -409,6 +441,4 @@
     def body(*arguments):
         return local(layout, *arguments)
 
-    return jax.shard_map(
-        body, mesh=mesh, in_specs=placed, out_specs=P(("outer", "atoms"), None), check_vma=False
-    )
+    return jax.shard_map(body, mesh=mesh, in_specs=placed, out_specs=P(("outer", "atoms"), None), check_vma=False)

time: 73.4 us -> 76.7 us (1.045)
  waiting for transfers between devices: 27.6 us -> 29.6 us
  Pallas kernels: 18.2 us -> 19.4 us
    ppermute x6, waiting for transfers between devices: 8.61 us -> 10 us  [exchange(): return lax.ppermute(value, axes, pairs)]
    pallas_call x5 -> x8, Pallas kernels: 18.2 us -> 19.4 us  [call(): pl.pallas_call(kernel, in_specs=[pl.BlockSpec(memory_space=space)] * len(...]
  transfers between devices with their start and end apart: 34 -> 34, of which waited for: 20 -> 18; matrix products, arithmetic and copies ran while one was open for 0% -> 0% of each run, Pallas kernels for 7% -> 13%
where the time goes in v2:
time: 76.7 us; the launch traced here: 76.6 us
  waiting for transfers between devices  29.6 us (39%)
  starting transfers between devices  27 us (35%)
  Pallas kernels  19.4 us (25%)
    ppermute x28, waiting for transfers between devices, send(): lax.ppermute(value, axes, [(i, self.moved(i, **d)) for i in range(count)])  19.6 us
    pallas_call x8, Pallas kernels, call(): pl.pallas_call(kernel, in_specs=[pl.BlockSpec(memory_space=space)] * len(...  19.4 us
    ppermute x28, starting transfers between devices, send(): lax.ppermute(value, axes, [(i, self.moved(i, **d)) for i in range(count)])  18.1 us
    ppermute x6, waiting for transfers between devices, exchange(): return lax.ppermute(value, axes, pairs)  10 us
    ppermute x6, starting transfers between devices, exchange(): return lax.ppermute(value, axes, pairs)  8.9 us
  transfers between devices with their start and end apart: 34, of which 18 were waited for; matrix products, arithmetic and copies ran while one was open for 0% of the time, Pallas kernels for 13%

profile of v2, /device:TPU:0, one launch (start us, length us, event | category | flops | bytes accessed | tf_op | source)
XLA Modules:
  0.0 76.6 jit_solution(13634951566414992577)
XLA Ops:
  0.0 2.7 %shard_map.91 = (bf16[768,16]{1,0:T(8,128)(2,1)S(1)}, bf16[16,1024]{1,0:T(8,128)(2,1)S(1)}, bf16[1024,256]{1,0:T(8,128)(2,1)S(1)}, bf16[2,384,1024]{2,1,0:T(8,12...) custom-call(s32[3,768]{1,0:T(4,128)} %refs_0_.3, s32[3,1024]{1,0:T(4,128)} %refs_1_.3, f32[1024,128]{1,0:T(8,128)} %refs_9_.1, ...), custom_call_target="tpu_custom_call" | custom-call | flops 1207959552 | bytes 6039797 | tf_op jit(solution)/shard_map/pallas_call | solution.py:318
  2.7 0.6 collective-permute-start.5
  3.3 2.5 %shard_map.93 = (bf16[4,384,1024]{2,1,0:T(8,128)(2,1)S(1)}, f32[192,128]{1,0:T(8,128)S(1)}, f32[192,128]{1,0:T(8,128)S(1)}, f32[192,128]{1,0:T(8,128)S(1)}, f32[192,128]{1,0:T(8,128)S(1)}) custom-call(bf16[768,16]{1,0:T(8,128)(2,1)S(1)} %get-tuple-element.32.refs_0_, bf16[16,1024]{1,0:T(8,128)(2,1)S(1)} %get-tuple-element.33.refs_1_, ...), custom_call_target="tpu_custom_call" | custom-call | flops 301989888 | bytes 1509949 | tf_op jit(solution)/shard_map/pallas_call | solution.py:318
  5.9 0.5 collective-permute-start.3
  6.4 1.4 %shard_map.92 = (bf16[2,384,1024]{2,1,0:T(8,128)(2,1)S(1)}, f32[192,128]{1,0:T(8,128)S(1)}, f32[192,128]{1,0:T(8,128)S(1)}) custom-call(bf16[768,16]{1,0:T(8,128)(2,1)S(1)} %get-tuple-element.32.refs_0_, bf16[16,1024]{1,0:T(8,128)(2,1)S(1)} %get-tuple-element.33.refs_1_, bf16[1024,256]{1,0:T(8,128)(2,1)S(1)} %get-tuple-element.34.refs_2_), custom_call_target="tpu_custom_call" | custom-call | flops 301989888 | bytes 1509949 | tf_op jit(solution)/shard_map/pallas_call | solution.py:318
  7.9 0.1 collective-permute-start
  8.1 3.9 %collective-permute-start.6 = (f32[192,128]{1,0:T(8,128)S(1)}, f32[192,128]{1,0:T(8,128)S(1)}, u32[]{:S(2)}, u32[]{:S(2)}) collective-permute-start(f32[192,128]{1,0:T(8,128)S(1)} %add.65), channel_id=1, source_target_pairs={{0,17},{1,16},{2,19},{3,18},{4,21},{5,20},{6,23},{7,22},{8,25},{9,... | collective-permute-start | bytes 294920 | tf_op jit(solution)/shard_map/ppermute | solution.py:46
  12.0 0.6 collective-permute-start.2
  12.8 2.9 %collective-permute-done.6 = f32[192,128]{1,0:T(8,128)S(1)} collective-permute-done((f32[192,128]{1,0:T(8,128)S(1)}, f32[192,128]{1,0:T(8,128)S(1)}, u32[]{:S(2)}, u32[]{:S(2)}) %collective-permute-start.6) | collective-permute-done | bytes 98336 | tf_op jit(solution)/shard_map/ppermute | solution.py:46
  15.7 1.7 %collective-permute-done.2 = f32[192,128]{1,0:T(8,128)S(1)} collective-permute-done((f32[192,128]{1,0:T(8,128)S(1)}, f32[192,128]{1,0:T(8,128)S(1)}, u32[]{:S(2)}, u32[]{:S(2)}) %collective-permute-start.2) | collective-permute-done | bytes 98336 | tf_op jit(solution)/shard_map/ppermute | solution.py:46
  17.4 1.8 %collective-permute-start.9 = (f32[192,128]{1,0:T(8,128)S(1)}, f32[192,128]{1,0:T(8,128)S(1)}, u32[]{:S(2)}, u32[]{:S(2)}) collective-permute-start(f32[192,128]{1,0:T(8,128)S(1)} %add_add_fusion.1), channel_id=1, source_target_pairs={{0,2},{1,3},{2,0},{3,1},{4,6},{5,7},{6,4},{7,5},{8,10},{9,11},{10,... | collective-permute-start | bytes 294920 | tf_op jit(solution)/shard_map/ppermute | solution.py:54
  19.2 2.6 %collective-permute-start.8 = (f32[192,128]{1,0:T(8,128)S(1)}, f32[192,128]{1,0:T(8,128)S(1)}, u32[]{:S(2)}, u32[]{:S(2)}) collective-permute-start(f32[192,128]{1,0:T(8,128)S(1)} %add_add_fusion.1), channel_id=1, source_target_pairs={{0,4},{1,5},{2,6},{3,7},{4,0},{5,1},{6,2},{7,3},{8,12},{9,13},{10,... | collective-permute-start | bytes 294920 | tf_op jit(solution)/shard_map/ppermute | solution.py:54
  21.9 4.2 %shard_map.94 = (bf16[4,512,1536]{2,1,0:T(8,128)(2,1)S(1)}, f32[192,128]{1,0:T(8,128)S(1)}, f32[192,128]{1,0:T(8,128)S(1)}) custom-call(s32[3,768]{1,0:T(4,128)S(1)} %copy-done.8, s32[3,1024]{1,0:T(4,128)S(1)} %copy-done.7, f32[2,768,128]{2,1,0:T(8,128)S(1)} %copy-done.6), custom_call_target="tpu_custom_call" | custom-call | flops 1207959552 | bytes 6039797 | tf_op jit(solution)/shard_map/pallas_call | solution.py:318
  26.2 2.9 %collective-permute-done.8 = f32[192,128]{1,0:T(8,128)S(1)} collective-permute-done((f32[192,128]{1,0:T(8,128)S(1)}, f32[192,128]{1,0:T(8,128)S(1)}, u32[]{:S(2)}, u32[]{:S(2)}) %collective-permute-start.8) | collective-permute-done | bytes 98336 | tf_op jit(solution)/shard_map/ppermute | solution.py:54
  29.1 2.7 %collective-permute-start.12 = (f32[192,128]{1,0:T(8,128)S(1)}, f32[192,128]{1,0:T(8,128)S(1)}, u32[]{:S(2)}, u32[]{:S(2)}) collective-permute-start(f32[192,128]{1,0:T(8,128)S(1)} %add_multiply_fusion.1.refs_0_), channel_id=1, source_target_pairs={{0,17},{1,16},{2,19},{3,18},{4,21},{5,20},{6,23},{7,22},{8,25},{9,... | collective-permute-start | bytes 294920 | tf_op jit(solution)/shard_map/ppermute | solution.py:46
  31.8 0.4 collective-permute-start.11
  32.2 0.4 collective-permute-start.10
  32.7 2.6 %collective-permute-done.12.refs_3_ = f32[192,128]{1,0:T(8,128)S(1)} collective-permute-done((f32[192,128]{1,0:T(8,128)S(1)}, f32[192,128]{1,0:T(8,128)S(1)}, u32[]{:S(2)}, u32[]{:S(2)}) %collective-permute-start.12) | collective-permute-done | bytes 98336 | tf_op jit(solution)/shard_map/ppermute | solution.py:46
  35.3 1.2 %collective-permute-done.11.refs_2_ = f32[192,128]{1,0:T(8,128)S(1)} collective-permute-done((f32[192,128]{1,0:T(8,128)S(1)}, f32[192,128]{1,0:T(8,128)S(1)}, u32[]{:S(2)}, u32[]{:S(2)}) %collective-permute-start.11) | collective-permute-done | bytes 98336 | tf_op jit(solution)/shard_map/ppermute | solution.py:46
  36.4 0.4 collective-permute-done.10.refs_1_
  37.0 0.8 %collective-permute-done.15.refs_6_ = f32[192,128]{1,0:T(8,128)S(1)} collective-permute-done((f32[192,128]{1,0:T(8,128)S(1)}, f32[192,128]{1,0:T(8,128)S(1)}, u32[]{:S(2)}, u32[]{:S(2)}) %collective-permute-start.15) | collective-permute-done | bytes 98336 | tf_op jit(solution)/shard_map/ppermute | solution.py:46
  37.7 0.4 collective-permute-done.14.refs_5_
  38.2 3.3 %shard_map.95 = (f32[1024,128]{1,0:T(8,128)S(1)}, bf16[1024,256]{1,0:T(8,128)(2,1)S(1)}, f32[192,128]{1,0:T(8,128)S(1)}, f32[192,128]{1,0:T(8,128)S(1)}) custom-call(f32[192,128]{1,0:T(8,128)S(1)} %add_multiply_fusion.1.refs_0_, f32[192,128]{1,0:T(8,128)S(1)} %collective-permute-done.10.refs_1_, f32[192,128]{1,0:T(8,128)S(1)} %collective-permute-done.11.refs_2_, ...), custom_call_target="tpu_custom_call" | custom-call | flops 1207959552 | bytes 6039797 | tf_op jit(solution)/shard_map/pallas_call | solution.py:318
  41.5 0.2 collective-permute-start.22
  41.7 1.0 %shard_map.97 = (f32[192,128]{1,0:T(8,128)S(1)}, f32[192,128]{1,0:T(8,128)S(1)}, f32[192,128]{1,0:T(8,128)S(1)}, f32[192,128]{1,0:T(8,128)S(1)}) custom-call(bf16[4,384,1024]{2,1,0:T(8,128)(2,1)S(1)} %get-tuple-element.50.refs_0_, bf16[1024,256]{1,0:T(8,128)(2,1)S(1)} %get-tuple-element.47.refs_1_), custom_call_target="tpu_custom_call" | custom-call | flops 301989888 | bytes 1509949 | tf_op jit(solution)/shard_map/pallas_call | solution.py:318
  42.7 0.4 collective-permute-start.18
  43.2 0.1 collective-permute-start.20
  43.3 0.6 shard_map.96
  43.9 0.4 collective-permute-start.17
  44.4 1.7 %collective-permute-start.23 = (f32[192,128]{1,0:T(8,128)S(1)}, f32[192,128]{1,0:T(8,128)S(1)}, u32[]{:S(2)}, u32[]{:S(2)}) collective-permute-start(f32[192,128]{1,0:T(8,128)S(1)} %add.75), channel_id=1, source_target_pairs={{0,17},{1,16},{2,19},{3,18},{4,21},{5,20},{6,23},{7,22},{8,25},{9,... | collective-permute-start | bytes 294920 | tf_op jit(solution)/shard_map/ppermute | solution.py:46
  46.1 1.5 %collective-permute-start.19 = (f32[192,128]{1,0:T(8,128)S(1)}, f32[192,128]{1,0:T(8,128)S(1)}, u32[]{:S(2)}, u32[]{:S(2)}) collective-permute-start(f32[192,128]{1,0:T(8,128)S(1)} %add.71), channel_id=1, source_target_pairs={{0,1},{1,0},{2,3},{3,2},{4,5},{5,4},{6,7},{7,6},{8,9},{9,8},{10,11... | collective-permute-start | bytes 294920 | tf_op jit(solution)/shard_map/ppermute | solution.py:46
  47.6 0.5 collective-permute-start.21
  48.1 2.9 %collective-permute-done.23 = f32[192,128]{1,0:T(8,128)S(1)} collective-permute-done((f32[192,128]{1,0:T(8,128)S(1)}, f32[192,128]{1,0:T(8,128)S(1)}, u32[]{:S(2)}, u32[]{:S(2)}) %collective-permute-start.23) | collective-permute-done | bytes 98336 | tf_op jit(solution)/shard_map/ppermute | solution.py:46
  51.0 1.4 %collective-permute-done.19 = f32[192,128]{1,0:T(8,128)S(1)} collective-permute-done((f32[192,128]{1,0:T(8,128)S(1)}, f32[192,128]{1,0:T(8,128)S(1)}, u32[]{:S(2)}, u32[]{:S(2)}) %collective-permute-start.19) | collective-permute-done | bytes 98336 | tf_op jit(solution)/shard_map/ppermute | solution.py:46
  52.6 1.7 %collective-permute-start.26 = (f32[192,128]{1,0:T(8,128)S(1)}, f32[192,128]{1,0:T(8,128)S(1)}, u32[]{:S(2)}, u32[]{:S(2)}) collective-permute-start(f32[192,128]{1,0:T(8,128)S(1)} %add_add_fusion), channel_id=1, source_target_pairs={{0,2},{1,3},{2,0},{3,1},{4,6},{5,7},{6,4},{7,5},{8,10},{9,11},{10,... | collective-permute-start | bytes 294920 | tf_op jit(solution)/shard_map/ppermute | solution.py:54
  54.2 1.4 %collective-permute-start.25 = (f32[192,128]{1,0:T(8,128)S(1)}, f32[192,128]{1,0:T(8,128)S(1)}, u32[]{:S(2)}, u32[]{:S(2)}) collective-permute-start(f32[192,128]{1,0:T(8,128)S(1)} %add_add_fusion), channel_id=1, source_target_pairs={{0,4},{1,5},{2,6},{3,7},{4,0},{5,1},{6,2},{7,3},{8,12},{9,13},{10,... | collective-permute-start | bytes 294920 | tf_op jit(solution)/shard_map/ppermute | solution.py:54
  55.6 1.4 %collective-permute-start.24 = (f32[192,128]{1,0:T(8,128)S(1)}, f32[192,128]{1,0:T(8,128)S(1)}, u32[]{:S(2)}, u32[]{:S(2)}) collective-permute-start(f32[192,128]{1,0:T(8,128)S(1)} %add_add_fusion), channel_id=1, source_target_pairs={{0,6},{1,7},{2,4},{3,5},{4,2},{5,3},{6,0},{7,1},{8,14},{9,15},{10,... | collective-permute-start | bytes 294920 | tf_op jit(solution)/shard_map/ppermute | solution.py:54
  57.0 1.2 %collective-permute-done.26 = f32[192,128]{1,0:T(8,128)S(1)} collective-permute-done((f32[192,128]{1,0:T(8,128)S(1)}, f32[192,128]{1,0:T(8,128)S(1)}, u32[]{:S(2)}, u32[]{:S(2)}) %collective-permute-start.26) | collective-permute-done | bytes 98336 | tf_op jit(solution)/shard_map/ppermute | solution.py:54
  58.2 5.9 %collective-permute-done.25 = f32[192,128]{1,0:T(8,128)S(1)} collective-permute-done((f32[192,128]{1,0:T(8,128)S(1)}, f32[192,128]{1,0:T(8,128)S(1)}, u32[]{:S(2)}, u32[]{:S(2)}) %collective-permute-start.25) | collective-permute-done | bytes 98336 | tf_op jit(solution)/shard_map/ppermute | solution.py:54
  64.2 1.7 %collective-permute-start.29 = (f32[192,128]{1,0:T(8,128)S(1)}, f32[192,128]{1,0:T(8,128)S(1)}, u32[]{:S(2)}, u32[]{:S(2)}) collective-permute-start(f32[192,128]{1,0:T(8,128)S(1)} %add_multiply_fusion.refs_0_), channel_id=1, source_target_pairs={{0,17},{1,16},{2,19},{3,18},{4,21},{5,20},{6,23},{7,22},{8,25},{9,... | collective-permute-start | bytes 294920 | tf_op jit(solution)/shard_map/ppermute | solution.py:46
  65.9 1.1 %collective-permute-start.28 = (f32[192,128]{1,0:T(8,128)S(1)}, f32[192,128]{1,0:T(8,128)S(1)}, u32[]{:S(2)}, u32[]{:S(2)}) collective-permute-start(f32[192,128]{1,0:T(8,128)S(1)} %add_multiply_fusion.refs_0_), channel_id=1, source_target_pairs={{0,16},{1,17},{2,18},{3,19},{4,20},{5,21},{6,22},{7,23},{8,24},{9,... | collective-permute-start | bytes 294920 | tf_op jit(solution)/shard_map/ppermute | solution.py:46
  67.0 0.8 collective-permute-start.27
  67.7 2.1 %collective-permute-done.29.refs_3_ = f32[192,128]{1,0:T(8,128)S(1)} collective-permute-done((f32[192,128]{1,0:T(8,128)S(1)}, f32[192,128]{1,0:T(8,128)S(1)}, u32[]{:S(2)}, u32[]{:S(2)}) %collective-permute-start.29) | collective-permute-done | bytes 98336 | tf_op jit(solution)/shard_map/ppermute | solution.py:46
  69.8 1.0 %collective-permute-done.28.refs_2_ = f32[192,128]{1,0:T(8,128)S(1)} collective-permute-done((f32[192,128]{1,0:T(8,128)S(1)}, f32[192,128]{1,0:T(8,128)S(1)}, u32[]{:S(2)}, u32[]{:S(2)}) %collective-permute-start.28) | collective-permute-done | bytes 98336 | tf_op jit(solution)/shard_map/ppermute | solution.py:46
  70.8 0.8 %collective-permute-done.27.refs_1_ = f32[192,128]{1,0:T(8,128)S(1)} collective-permute-done((f32[192,128]{1,0:T(8,128)S(1)}, f32[192,128]{1,0:T(8,128)S(1)}, u32[]{:S(2)}, u32[]{:S(2)}) %collective-permute-start.27) | collective-permute-done | bytes 98336 | tf_op jit(solution)/shard_map/ppermute | solution.py:46
  71.6 0.5 collective-permute-done.32.refs_6_
  72.1 0.8 %collective-permute-done.31.refs_5_ = f32[192,128]{1,0:T(8,128)S(1)} collective-permute-done((f32[192,128]{1,0:T(8,128)S(1)}, f32[192,128]{1,0:T(8,128)S(1)}, u32[]{:S(2)}, u32[]{:S(2)}) %collective-permute-start.31) | collective-permute-done | bytes 98336 | tf_op jit(solution)/shard_map/ppermute | solution.py:46
  72.9 3.5 %shard_map.98 = f32[1024,128]{1,0:T(8,128)} custom-call(f32[192,128]{1,0:T(8,128)S(1)} %add_multiply_fusion.refs_0_, f32[192,128]{1,0:T(8,128)S(1)} %collective-permute-done.27.refs_1_, f32[192,128]{1,0:T(8,128)S(1)} %collective-permute-done.28.refs_2_, f32[192,128]{1,0:T(8,128)S(1)} %collective-permute-done.29.refs_3_, ...), custom_call_target="tpu_custom_call" | custom-call | flops 1207959552 | bytes 6039797 | tf_op jit(solution)/shard_map/pallas_call | solution.py:318
  (56 shorter events, 0.8 us)
Async XLA Ops:
  0.0 21.9 %copy-start.8 = (s32[3,768]{1,0:T(4,128)S(1)}, s32[3,768]{1,0:T(4,128)}, u32[]{:S(2)}) copy-start(s32[3,768]{1,0:T(4,128)} %refs_0_.3) | copy-start | bytes 27652
  0.0 21.9 %copy-start.7 = (s32[3,1024]{1,0:T(4,128)S(1)}, s32[3,1024]{1,0:T(4,128)}, u32[]{:S(2)}) copy-start(s32[3,1024]{1,0:T(4,128)} %refs_1_.3) | copy-start | bytes 36868
  0.0 21.9 %copy-start.6 = (f32[2,768,128]{2,1,0:T(8,128)S(1)}, f32[2,768,128]{2,1,0:T(8,128)}, u32[]{:S(2)}) copy-start(f32[2,768,128]{2,1,0:T(8,128)} %refs_2_.3) | copy-start | bytes 2359300
  2.7 5.3 %collective-permute-start.5 = (f32[192,128]{1,0:T(8,128)S(1)}, f32[192,128]{1,0:T(8,128)S(1)}, u32[]{:S(2)}, u32[]{:S(2)}) collective-permute-start(f32[192,128]{1,0:T(8,128)S(1)} %get-tuple-element.43), channel_id=1, source_target_pairs={{0,8},{1,9},{2,10},{3,11},{4,12},{5,13},{6,14},{7,15},{8,0},{9,1},... | collective-permute-start | bytes 294920 | tf_op jit(solution)/shard_map/ppermute | solution.py:46
  5.8 6.2 %collective-permute-start.1 = (f32[192,128]{1,0:T(8,128)S(1)}, f32[192,128]{1,0:T(8,128)S(1)}, u32[]{:S(2)}, u32[]{:S(2)}) collective-permute-start(f32[192,128]{1,0:T(8,128)S(1)} %get-tuple-element.39), channel_id=1, source_target_pairs={{0,8},{1,9},{2,10},{3,11},{4,12},{5,13},{6,14},{7,15},{8,0},{9,1},... | collective-permute-start | bytes 294920 | tf_op jit(solution)/shard_map/ppermute | solution.py:46
  5.9 6.7 %collective-permute-start.3 = (f32[192,128]{1,0:T(8,128)S(1)}, f32[192,128]{1,0:T(8,128)S(1)}, u32[]{:S(2)}, u32[]{:S(2)}) collective-permute-start(f32[192,128]{1,0:T(8,128)S(1)} %get-tuple-element.41), channel_id=1, source_target_pairs={{0,8},{1,9},{2,10},{3,11},{4,12},{5,13},{6,14},{7,15},{8,0},{9,1},... | collective-permute-start | bytes 294920 | tf_op jit(solution)/shard_map/ppermute | solution.py:46
  7.9 4.9 %collective-permute-start = (f32[192,128]{1,0:T(8,128)S(1)}, f32[192,128]{1,0:T(8,128)S(1)}, u32[]{:S(2)}, u32[]{:S(2)}) collective-permute-start(f32[192,128]{1,0:T(8,128)S(1)} %get-tuple-element.37), channel_id=1, source_target_pairs={{0,8},{1,9},{2,10},{3,11},{4,12},{5,13},{6,14},{7,15},{8,0},{9,1},... | collective-permute-start | bytes 294920 | tf_op jit(solution)/shard_map/ppermute | solution.py:46
  8.0 30.1 %copy-start = (f32[2,128,128]{2,1,0:T(8,128)S(1)}, f32[2,128,128]{2,1,0:T(8,128)}, u32[]{:S(2)}) copy-start(f32[2,128,128]{2,1,0:T(8,128)} %refs_11_.3) | copy-start | bytes 393220
  8.0 30.1 %copy-start.1 = (f32[2,128,128]{2,1,0:T(8,128)S(1)}, f32[2,128,128]{2,1,0:T(8,128)}, u32[]{:S(2)}) copy-start(f32[2,128,128]{2,1,0:T(8,128)} %refs_13_.3) | copy-start | bytes 393220
  8.0 30.1 %copy-start.2 = (f32[1024,128]{1,0:T(8,128)S(1)}, f32[1024,128]{1,0:T(8,128)}, u32[]{:S(2)}) copy-start(f32[1024,128]{1,0:T(8,128)} %refs_9_.1) | copy-start | bytes 1572868
  8.0 30.1 %copy-start.3 = (f32[2,128,128]{2,1,0:T(8,128)S(1)}, f32[2,128,128]{2,1,0:T(8,128)}, u32[]{:S(2)}) copy-start(f32[2,128,128]{2,1,0:T(8,128)} %refs_14_.1) | copy-start | bytes 393220
  8.1 30.1 %copy-start.4 = (f32[2,128]{1,0:T(2,128)S(1)}, f32[2,128]{1,0:T(2,128)}, u32[]{:S(2)}) copy-start(f32[2,128]{1,0:T(2,128)} %refs_10_.3) | copy-start | bytes 3076
  8.1 30.1 %copy-start.5 = (f32[2,128]{1,0:T(2,128)S(1)}, f32[2,128]{1,0:T(2,128)}, u32[]{:S(2)}) copy-start(f32[2,128]{1,0:T(2,128)} %refs_12_.3) | copy-start | bytes 3076
  8.1 7.6 %collective-permute-start.6 = (f32[192,128]{1,0:T(8,128)S(1)}, f32[192,128]{1,0:T(8,128)S(1)}, u32[]{:S(2)}, u32[]{:S(2)}) collective-permute-start(f32[192,128]{1,0:T(8,128)S(1)} %add.65), channel_id=1, source_target_pairs={{0,17},{1,16},{2,19},{3,18},{4,21},{5,20},{6,23},{7,22},{8,25},{9,... | collective-permute-start | bytes 294920 | tf_op jit(solution)/shard_map/ppermute | solution.py:46
  12.0 5.4 %collective-permute-start.2 = (f32[192,128]{1,0:T(8,128)S(1)}, f32[192,128]{1,0:T(8,128)S(1)}, u32[]{:S(2)}, u32[]{:S(2)}) collective-permute-start(f32[192,128]{1,0:T(8,128)S(1)} %add.61), channel_id=1, source_target_pairs={{0,1},{1,0},{2,3},{3,2},{4,5},{5,4},{6,7},{7,6},{8,9},{9,8},{10,11... | collective-permute-start | bytes 294920 | tf_op jit(solution)/shard_map/ppermute | solution.py:46
  12.7 4.7 %collective-permute-start.4 = (f32[192,128]{1,0:T(8,128)S(1)}, f32[192,128]{1,0:T(8,128)S(1)}, u32[]{:S(2)}, u32[]{:S(2)}) collective-permute-start(f32[192,128]{1,0:T(8,128)S(1)} %add.63), channel_id=1, source_target_pairs={{0,16},{1,17},{2,18},{3,19},{4,20},{5,21},{6,22},{7,23},{8,24},{9,... | collective-permute-start | bytes 294920 | tf_op jit(solution)/shard_map/ppermute | solution.py:46
  17.4 8.7 %collective-permute-start.9 = (f32[192,128]{1,0:T(8,128)S(1)}, f32[192,128]{1,0:T(8,128)S(1)}, u32[]{:S(2)}, u32[]{:S(2)}) collective-permute-start(f32[192,128]{1,0:T(8,128)S(1)} %add_add_fusion.1), channel_id=1, source_target_pairs={{0,2},{1,3},{2,0},{3,1},{4,6},{5,7},{6,4},{7,5},{8,10},{9,11},{10,... | collective-permute-start | bytes 294920 | tf_op jit(solution)/shard_map/ppermute | solution.py:54
  19.2 9.8 %collective-permute-start.8 = (f32[192,128]{1,0:T(8,128)S(1)}, f32[192,128]{1,0:T(8,128)S(1)}, u32[]{:S(2)}, u32[]{:S(2)}) collective-permute-start(f32[192,128]{1,0:T(8,128)S(1)} %add_add_fusion.1), channel_id=1, source_target_pairs={{0,4},{1,5},{2,6},{3,7},{4,0},{5,1},{6,2},{7,3},{8,12},{9,13},{10,... | collective-permute-start | bytes 294920 | tf_op jit(solution)/shard_map/ppermute | solution.py:54
  21.8 7.3 %collective-permute-start.7 = (f32[192,128]{1,0:T(8,128)S(1)}, f32[192,128]{1,0:T(8,128)S(1)}, u32[]{:S(2)}, u32[]{:S(2)}) collective-permute-start(f32[192,128]{1,0:T(8,128)S(1)} %add_add_fusion.1), channel_id=1, source_target_pairs={{0,6},{1,7},{2,4},{3,5},{4,2},{5,3},{6,0},{7,1},{8,14},{9,15},{10,... | collective-permute-start | bytes 294920 | tf_op jit(solution)/shard_map/ppermute | solution.py:54
  29.1 6.2 %collective-permute-start.12 = (f32[192,128]{1,0:T(8,128)S(1)}, f32[192,128]{1,0:T(8,128)S(1)}, u32[]{:S(2)}, u32[]{:S(2)}) collective-permute-start(f32[192,128]{1,0:T(8,128)S(1)} %add_multiply_fusion.1.refs_0_), channel_id=1, source_target_pairs={{0,17},{1,16},{2,19},{3,18},{4,21},{5,20},{6,23},{7,22},{8,25},{9,... | collective-permute-start | bytes 294920 | tf_op jit(solution)/shard_map/ppermute | solution.py:46
  31.8 4.6 %collective-permute-start.11 = (f32[192,128]{1,0:T(8,128)S(1)}, f32[192,128]{1,0:T(8,128)S(1)}, u32[]{:S(2)}, u32[]{:S(2)}) collective-permute-start(f32[192,128]{1,0:T(8,128)S(1)} %add_multiply_fusion.1.refs_0_), channel_id=1, source_target_pairs={{0,16},{1,17},{2,18},{3,19},{4,20},{5,21},{6,22},{7,23},{8,24},{9,... | collective-permute-start | bytes 294920 | tf_op jit(solution)/shard_map/ppermute | solution.py:46
  32.2 4.6 %collective-permute-start.10 = (f32[192,128]{1,0:T(8,128)S(1)}, f32[192,128]{1,0:T(8,128)S(1)}, u32[]{:S(2)}, u32[]{:S(2)}) collective-permute-start(f32[192,128]{1,0:T(8,128)S(1)} %add_multiply_fusion.1.refs_0_), channel_id=1, source_target_pairs={{0,1},{1,0},{2,3},{3,2},{4,5},{5,4},{6,7},{7,6},{8,9},{9,8},{10,11... | collective-permute-start | bytes 294920 | tf_op jit(solution)/shard_map/ppermute | solution.py:46
  32.7 4.3 %collective-permute-start.13 = (f32[192,128]{1,0:T(8,128)S(1)}, f32[192,128]{1,0:T(8,128)S(1)}, u32[]{:S(2)}, u32[]{:S(2)}) collective-permute-start(f32[192,128]{1,0:T(8,128)S(1)} %add_multiply_fusion.1.refs_0_), channel_id=1, source_target_pairs={{0,8},{1,9},{2,10},{3,11},{4,12},{5,13},{6,14},{7,15},{8,0},{9,1},... | collective-permute-start | bytes 294920 | tf_op jit(solution)/shard_map/ppermute | solution.py:46
  35.2 1.7 %collective-permute-start.16 = (f32[192,128]{1,0:T(8,128)S(1)}, f32[192,128]{1,0:T(8,128)S(1)}, u32[]{:S(2)}, u32[]{:S(2)}) collective-permute-start(f32[192,128]{1,0:T(8,128)S(1)} %collective-permute-done.12.refs_3_), channel_id=1, source_target_pairs={{0,8},{1,9},{2,10},{3,11},{4,12},{5,13},{6,14},{7,15},{8,0},{9,1},... | collective-permute-start | bytes 294920 | tf_op jit(solution)/shard_map/ppermute | solution.py:46
  36.4 1.3 %collective-permute-start.15 = (f32[192,128]{1,0:T(8,128)S(1)}, f32[192,128]{1,0:T(8,128)S(1)}, u32[]{:S(2)}, u32[]{:S(2)}) collective-permute-start(f32[192,128]{1,0:T(8,128)S(1)} %collective-permute-done.11.refs_2_), channel_id=1, source_target_pairs={{0,8},{1,9},{2,10},{3,11},{4,12},{5,13},{6,14},{7,15},{8,0},{9,1},... | collective-permute-start | bytes 294920 | tf_op jit(solution)/shard_map/ppermute | solution.py:46
  36.8 1.3 %collective-permute-start.14 = (f32[192,128]{1,0:T(8,128)S(1)}, f32[192,128]{1,0:T(8,128)S(1)}, u32[]{:S(2)}, u32[]{:S(2)}) collective-permute-start(f32[192,128]{1,0:T(8,128)S(1)} %collective-permute-done.10.refs_1_), channel_id=1, source_target_pairs={{0,8},{1,9},{2,10},{3,11},{4,12},{5,13},{6,14},{7,15},{8,0},{9,1},... | collective-permute-start | bytes 294920 | tf_op jit(solution)/shard_map/ppermute | solution.py:46
  41.5 2.8 %collective-permute-start.22 = (f32[192,128]{1,0:T(8,128)S(1)}, f32[192,128]{1,0:T(8,128)S(1)}, u32[]{:S(2)}, u32[]{:S(2)}) collective-permute-start(f32[192,128]{1,0:T(8,128)S(1)} %get-tuple-element.56), channel_id=1, source_target_pairs={{0,8},{1,9},{2,10},{3,11},{4,12},{5,13},{6,14},{7,15},{8,0},{9,1},... | collective-permute-start | bytes 294920 | tf_op jit(solution)/shard_map/ppermute | solution.py:46
  42.7 3.3 %collective-permute-start.18 = (f32[192,128]{1,0:T(8,128)S(1)}, f32[192,128]{1,0:T(8,128)S(1)}, u32[]{:S(2)}, u32[]{:S(2)}) collective-permute-start(f32[192,128]{1,0:T(8,128)S(1)} %get-tuple-element.52), channel_id=1, source_target_pairs={{0,8},{1,9},{2,10},{3,11},{4,12},{5,13},{6,14},{7,15},{8,0},{9,1},... | collective-permute-start | bytes 294920 | tf_op jit(solution)/shard_map/ppermute | solution.py:46
  43.2 4.4 %collective-permute-start.20 = (f32[192,128]{1,0:T(8,128)S(1)}, f32[192,128]{1,0:T(8,128)S(1)}, u32[]{:S(2)}, u32[]{:S(2)}) collective-permute-start(f32[192,128]{1,0:T(8,128)S(1)} %get-tuple-element.54), channel_id=1, source_target_pairs={{0,8},{1,9},{2,10},{3,11},{4,12},{5,13},{6,14},{7,15},{8,0},{9,1},... | collective-permute-start | bytes 294920 | tf_op jit(solution)/shard_map/ppermute | solution.py:46
  43.9 4.2 %collective-permute-start.17 = (f32[192,128]{1,0:T(8,128)S(1)}, f32[192,128]{1,0:T(8,128)S(1)}, u32[]{:S(2)}, u32[]{:S(2)}) collective-permute-start(f32[192,128]{1,0:T(8,128)S(1)} %get-tuple-element.49), channel_id=1, source_target_pairs={{0,8},{1,9},{2,10},{3,11},{4,12},{5,13},{6,14},{7,15},{8,0},{9,1},... | collective-permute-start | bytes 294920 | tf_op jit(solution)/shard_map/ppermute | solution.py:46
  44.4 6.6 %collective-permute-start.23 = (f32[192,128]{1,0:T(8,128)S(1)}, f32[192,128]{1,0:T(8,128)S(1)}, u32[]{:S(2)}, u32[]{:S(2)}) collective-permute-start(f32[192,128]{1,0:T(8,128)S(1)} %add.75), channel_id=1, source_target_pairs={{0,17},{1,16},{2,19},{3,18},{4,21},{5,20},{6,23},{7,22},{8,25},{9,... | collective-permute-start | bytes 294920 | tf_op jit(solution)/shard_map/ppermute | solution.py:46
  46.1 6.4 %collective-permute-start.19 = (f32[192,128]{1,0:T(8,128)S(1)}, f32[192,128]{1,0:T(8,128)S(1)}, u32[]{:S(2)}, u32[]{:S(2)}) collective-permute-start(f32[192,128]{1,0:T(8,128)S(1)} %add.71), channel_id=1, source_target_pairs={{0,1},{1,0},{2,3},{3,2},{4,5},{5,4},{6,7},{7,6},{8,9},{9,8},{10,11... | collective-permute-start | bytes 294920 | tf_op jit(solution)/shard_map/ppermute | solution.py:46
  47.6 4.9 %collective-permute-start.21 = (f32[192,128]{1,0:T(8,128)S(1)}, f32[192,128]{1,0:T(8,128)S(1)}, u32[]{:S(2)}, u32[]{:S(2)}) collective-permute-start(f32[192,128]{1,0:T(8,128)S(1)} %add.73), channel_id=1, source_target_pairs={{0,16},{1,17},{2,18},{3,19},{4,20},{5,21},{6,22},{7,23},{8,24},{9,... | collective-permute-start | bytes 294920 | tf_op jit(solution)/shard_map/ppermute | solution.py:46
  52.6 5.6 %collective-permute-start.26 = (f32[192,128]{1,0:T(8,128)S(1)}, f32[192,128]{1,0:T(8,128)S(1)}, u32[]{:S(2)}, u32[]{:S(2)}) collective-permute-start(f32[192,128]{1,0:T(8,128)S(1)} %add_add_fusion), channel_id=1, source_target_pairs={{0,2},{1,3},{2,0},{3,1},{4,6},{5,7},{6,4},{7,5},{8,10},{9,11},{10,... | collective-permute-start | bytes 294920 | tf_op jit(solution)/shard_map/ppermute | solution.py:54
  54.2 9.9 %collective-permute-start.25 = (f32[192,128]{1,0:T(8,128)S(1)}, f32[192,128]{1,0:T(8,128)S(1)}, u32[]{:S(2)}, u32[]{:S(2)}) collective-permute-start(f32[192,128]{1,0:T(8,128)S(1)} %add_add_fusion), channel_id=1, source_target_pairs={{0,4},{1,5},{2,6},{3,7},{4,0},{5,1},{6,2},{7,3},{8,12},{9,13},{10,... | collective-permute-start | bytes 294920 | tf_op jit(solution)/shard_map/ppermute | solution.py:54
  55.6 8.5 %collective-permute-start.24 = (f32[192,128]{1,0:T(8,128)S(1)}, f32[192,128]{1,0:T(8,128)S(1)}, u32[]{:S(2)}, u32[]{:S(2)}) collective-permute-start(f32[192,128]{1,0:T(8,128)S(1)} %add_add_fusion), channel_id=1, source_target_pairs={{0,6},{1,7},{2,4},{3,5},{4,2},{5,3},{6,0},{7,1},{8,14},{9,15},{10,... | collective-permute-start | bytes 294920 | tf_op jit(solution)/shard_map/ppermute | solution.py:54
  64.2 5.6 %collective-permute-start.29 = (f32[192,128]{1,0:T(8,128)S(1)}, f32[192,128]{1,0:T(8,128)S(1)}, u32[]{:S(2)}, u32[]{:S(2)}) collective-permute-start(f32[192,128]{1,0:T(8,128)S(1)} %add_multiply_fusion.refs_0_), channel_id=1, source_target_pairs={{0,17},{1,16},{2,19},{3,18},{4,21},{5,20},{6,23},{7,22},{8,25},{9,... | collective-permute-start | bytes 294920 | tf_op jit(solution)/shard_map/ppermute | solution.py:46
  65.9 4.9 %collective-permute-start.28 = (f32[192,128]{1,0:T(8,128)S(1)}, f32[192,128]{1,0:T(8,128)S(1)}, u32[]{:S(2)}, u32[]{:S(2)}) collective-permute-start(f32[192,128]{1,0:T(8,128)S(1)} %add_multiply_fusion.refs_0_), channel_id=1, source_target_pairs={{0,16},{1,17},{2,18},{3,19},{4,20},{5,21},{6,22},{7,23},{8,24},{9,... | collective-permute-start | bytes 294920 | tf_op jit(solution)/shard_map/ppermute | solution.py:46
  67.0 4.6 %collective-permute-start.27 = (f32[192,128]{1,0:T(8,128)S(1)}, f32[192,128]{1,0:T(8,128)S(1)}, u32[]{:S(2)}, u32[]{:S(2)}) collective-permute-start(f32[192,128]{1,0:T(8,128)S(1)} %add_multiply_fusion.refs_0_), channel_id=1, source_target_pairs={{0,1},{1,0},{2,3},{3,2},{4,5},{5,4},{6,7},{7,6},{8,9},{9,8},{10,11... | collective-permute-start | bytes 294920 | tf_op jit(solution)/shard_map/ppermute | solution.py:46
  67.7 3.9 %collective-permute-start.30 = (f32[192,128]{1,0:T(8,128)S(1)}, f32[192,128]{1,0:T(8,128)S(1)}, u32[]{:S(2)}, u32[]{:S(2)}) collective-permute-start(f32[192,128]{1,0:T(8,128)S(1)} %add_multiply_fusion.refs_0_), channel_id=1, source_target_pairs={{0,8},{1,9},{2,10},{3,11},{4,12},{5,13},{6,14},{7,15},{8,0},{9,1},... | collective-permute-start | bytes 294920 | tf_op jit(solution)/shard_map/ppermute | solution.py:46
  69.8 1.8 %collective-permute-start.33 = (f32[192,128]{1,0:T(8,128)S(1)}, f32[192,128]{1,0:T(8,128)S(1)}, u32[]{:S(2)}, u32[]{:S(2)}) collective-permute-start(f32[192,128]{1,0:T(8,128)S(1)} %collective-permute-done.29.refs_3_), channel_id=1, source_target_pairs={{0,8},{1,9},{2,10},{3,11},{4,12},{5,13},{6,14},{7,15},{8,0},{9,1},... | collective-permute-start | bytes 294920 | tf_op jit(solution)/shard_map/ppermute | solution.py:46
  70.8 1.3 %collective-permute-start.32 = (f32[192,128]{1,0:T(8,128)S(1)}, f32[192,128]{1,0:T(8,128)S(1)}, u32[]{:S(2)}, u32[]{:S(2)}) collective-permute-start(f32[192,128]{1,0:T(8,128)S(1)} %collective-permute-done.28.refs_2_), channel_id=1, source_target_pairs={{0,8},{1,9},{2,10},{3,11},{4,12},{5,13},{6,14},{7,15},{8,0},{9,1},... | collective-permute-start | bytes 294920 | tf_op jit(solution)/shard_map/ppermute | solution.py:46
  71.6 1.3 %collective-permute-start.31 = (f32[192,128]{1,0:T(8,128)S(1)}, f32[192,128]{1,0:T(8,128)S(1)}, u32[]{:S(2)}, u32[]{:S(2)}) collective-permute-start(f32[192,128]{1,0:T(8,128)S(1)} %collective-permute-done.27.refs_1_), channel_id=1, source_target_pairs={{0,8},{1,9},{2,10},{3,11},{4,12},{5,13},{6,14},{7,15},{8,0},{9,1},... | collective-permute-start | bytes 294920 | tf_op jit(solution)/shard_map/ppermute | solution.py:46

commit v3 on v1

--- a/solution.py
+++ b/solution.py
@@ -231,55 +231,86 @@
     project(table[len(chunks) - 1], pair[...], chunks[-1], rows)
 
 
-def atom_table_kernel(layout, rows, waves, positions, freq_filter, table, *refs):
-    scales = refs[:-3]
-    wave_rows, digit_rows, turns = refs[-3:]
+def project_kernel(rows, table, pair, *chunks):
+    for n, chunk in enumerate(chunks):
+        project(table[n], pair[...], chunk, rows)
+
+
+def atom_table_kernel(layout, rows, order, waves, positions, freq_filter, early, late, *refs):
+    scales = refs[:-5]
+    wave_rows, digit_rows, columns, ordered, turns = refs[-5:]
     own = pl.ds(pl.multiple_of(layout.chunk_of(0, 0, 0) * rows, rows), rows)
     for block, scale in enumerate(scales):
         scale[:rows, :] = freq_filter[block, own, :]
         scale[rows:, :] = freq_filter[block, own, :]
     operands(waves, positions, wave_rows, digit_rows)
-    turns[...] = contract_rows(digit_rows[...], wave_rows[...])
-    atoms, count = turns.shape
-    step, width = 32, 256
-    half = table.shape[1] // 2
+    count = wave_rows.shape[0]
+    row, column = (lax.broadcasted_iota(jnp.int32, (count, count), axis) for axis in range(2))
+    columns[...] = contract_rows(wave_rows[...], (row == column).astype(f32))
+    for n, offset in enumerate(order):
+        first = pl.multiple_of(layout.chunk_of(*offset) * rows, rows)
+        ordered[n * rows : (n + 1) * rows, :] = columns[pl.ds(first, rows), :]
+    swapped = lax.dot_general(
+        (row == column).astype(bf16), ordered[...].astype(bf16), (((1,), (1,)), ((), ())), preferred_element_type=f32
+    )
+    turns[...] = contract_rows(digit_rows[...], swapped)
+    atoms, span = turns.shape[0], early.shape[2] // 2
+    step = 16
+    half = early.shape[1] // 2
     per_group = half // step
 
     def body(m, carry):
         here = pl.ds(pl.multiple_of(m * step, step), step)
         group, row = m // per_group, pl.multiple_of((m % per_group) * step, step)
-        for at in range(0, count, width):
+        for n, table in enumerate((early, late)):
             targets = [
-                (table, (group, pl.ds(row + low * half, step), pl.ds(kind * count + at, width)))
+                (table, (group, pl.ds(row + low * half, step), slice(kind * span, (kind + 1) * span)))
                 for low in range(2)
                 for kind in range(2)
             ]
-            fill_tables(turns, here, slice(at, at + width), targets)
+            fill_tables(turns, here, slice(n * span, (n + 1) * span), targets)
         return carry
 
     lax.fori_loop(0, atoms // step, body, 0)
 
 
-def block_kernel(layout, rows, block, last, *refs):
-    chunks_in, refs = refs[: layout.chunks], refs[layout.chunks :]
-    atom_table, current_ref, gain, w_hidden, b_hidden, w_output = refs[:6]
-    refs = refs[6:]
+def gather_factor(rows, chunks, factor):
+    count = len(chunks)
+    for n, chunk in enumerate(chunks):
+        factor[n * rows : (n + 1) * rows, :] = paired(chunk[:rows, :])
+        factor[(count + n) * rows : (count + n + 1) * rows, :] = paired(chunk[rows:, :])
+
+
+def back_product(table, factor):
+    both = matmul(table, factor[...])
+    step, width = table.shape[0] // 2, both.shape[1] // 2
+    return folded(both[:step, :]) + both[step:, :width]
+
+
+def early_kernel(rows, *refs):
+    chunks, (table, part, factor) = refs[:-3], refs[-3:]
+    gather_factor(rows, chunks, factor)
+    step = table.shape[1] // 2
+    for n in range(table.shape[0]):
+        part[n * step : (n + 1) * step, :] = back_product(table[n], factor)
+
+
+def block_kernel(rows, count, block, last, *refs):
+    chunks_in, refs = refs[:count], refs[count:]
+    atom_table, part, current_ref, gain, w_hidden, b_hidden, w_output = refs[:7]
+    refs = refs[7:]
     if not last:
-        w_value, far_table, near_table, refs = refs[0], refs[1], refs[2], refs[3:]
-    current_out, chunks_out, factor = refs[0], refs[1:-1], refs[-1]
-    waves = rows * layout.chunks
-    width = current_ref.shape[1]
-    for offset, chunk in zip(layout.offsets(), chunks_in):
-        row = pl.multiple_of(layout.chunk_of(*offset) * rows, rows)
-        factor[pl.ds(row, rows), :] = paired(chunk[:rows, :])
-        factor[pl.ds(waves + row, rows), :] = paired(chunk[rows:, :])
+        w_value, table, current_out, pair_out = refs[:4]
+        chunks_out, factor = refs[4:-1], refs[-1]
+    else:
+        result, factor, current_out, sent = refs
+    gather_factor(rows, chunks_in, factor)
     hidden_stack, output_stack = stacked(w_hidden[block]), stacked(w_output[block])
     groups = atom_table.shape[0]
     step = atom_table.shape[1] // 2
 
     def back(n):
-        both = matmul(atom_table[n], factor[...])
-        return folded(both[:step, :]) + both[step:, :width]
+        return back_product(atom_table[n], factor) + part[n * step : (n + 1) * step, :]
 
     def update(n, messages):
         here = slice(n * step, (n + 1) * step)
@@ -289,25 +320,27 @@
         hidden = hidden / (1.0 + jnp.exp(-hidden))
         current_out[here, :] = current_ref[here, :] + product(hidden, output_stack)
 
-    messages = back(0)
+    messages, copies = back(0), []
     for n in range(groups):
         coming = back(n + 1) if n + 1 < groups else None
         update(n, messages)
         messages = coming
+        if last:
+            here = pl.ds(n * step, step)
+            copies.append(pltpu.make_async_copy(current_out.at[here], result.at[here], sent.at[n]))
+            copies[-1].start()
     if not last:
-        pair = paired(product(current_out[...], stacked(w_value[block + 1])))
-        far = [n for n, o in enumerate(layout.offsets()) if o[1:] != (0, 0)]
-        near = [n for n, o in enumerate(layout.offsets()) if o[1:] == (0, 0)]
-        for table, members in ((far_table, far), (near_table, near)):
-            for at, n in enumerate(members):
-                project(table[at], pair, chunks_out[n], rows)
-
-
-def call(kernel, outputs, scratch, limit, flops, *inputs, space=pltpu.VMEM):
+        pair_out[...] = paired(product(current_out[...], stacked(w_value[block + 1])))
+        project_kernel(rows, table, pair_out, *chunks_out)
+    for copy in copies:
+        copy.wait()
+
+
+def call(kernel, outputs, scratch, limit, flops, *inputs, space=pltpu.VMEM, out_space=pltpu.VMEM):
     return pl.pallas_call(
         kernel,
         in_specs=[pl.BlockSpec(memory_space=space)] * len(inputs),
-        out_specs=[pl.BlockSpec(memory_space=pltpu.VMEM)] * len(outputs),
+        out_specs=[pl.BlockSpec(memory_space=out_space)] * len(outputs),
         out_shape=outputs,
         scratch_shapes=scratch,
         compiler_params=pltpu.CompilerParams(vmem_limit_bytes=limit),
@@ -330,6 +363,9 @@
     far = [o for o in offsets if o[1:] != (0, 0)]
     near = [o for o in offsets if o[1:] == (0, 0)]
     group = min(256, atoms)
+    squares = sorted({o[1:] for o in offsets})
+    early_order = [o for o in offsets if o[1:] in (squares[0], squares[-1])]
+    late_order = [o for o in offsets if o not in early_order]
     outs = call(
         lambda *refs: first_kernel(layout, rows, *refs),
         [
@@ -361,35 +397,62 @@
     near_table = outs[0]
     parts |= dict(zip(near, outs[1:]))
     outs = call(
-        lambda *refs: atom_table_kernel(layout, rows, *refs),
-        [shape((atoms // group, 2 * group, 2 * waves), bf16)] + [chunk] * blocks,
-        index_scratch + [pltpu.VMEM((atoms, waves), f32)],
+        lambda *refs: atom_table_kernel(layout, rows, early_order + late_order, *refs),
+        [shape((atoms // group, 2 * group, 2 * rows * len(part)), bf16) for part in (early_order, late_order)]
+        + [chunk] * blocks,
+        index_scratch + [pltpu.VMEM((waves, 16), f32)] * 2 + [pltpu.VMEM((atoms, waves), f32)],
         table_limit,
         flops,
         wavevectors,
         positions,
         freq_filter,
     )
-    atom_table, scales = outs[0], outs[1:]
+    early_table, late_table, scales = outs[0], outs[1], outs[2:]
     current = features
     for block in range(blocks):
         last = block == blocks - 1
         gathered = total(layout, parts, scales[block])
-        inputs = [gathered[o] for o in offsets]
-        inputs += [atom_table, current, norm_gain, w_hidden, b_hidden, w_output]
-        if not last:
-            inputs += [w_value, far_table, near_table]
+        part = call(
+            lambda *refs: early_kernel(rows, *refs),
+            [shape((atoms, channels), f32)],
+            [pltpu.VMEM((2 * rows * len(early_order), 2 * channels), bf16)],
+            near_limit,
+            flops // 2,
+            *[gathered[o] for o in early_order],
+            early_table,
+        )
+        inputs = [gathered[o] for o in late_order]
+        inputs += [late_table, part[0], current, norm_gain, w_hidden, b_hidden, w_output]
+        outputs = [shape((atoms, channels), f32)]
+        scratch = [pltpu.VMEM((2 * rows * len(late_order), 2 * channels), bf16)]
+        if last:
+            scratch += [pltpu.VMEM((atoms, channels), f32), pltpu.SemaphoreType.DMA((atoms // group,))]
+        else:
+            inputs += [w_value, far_table]
+            outputs += [shape((atoms, 2 * channels), bf16)] + [chunk] * len(far)
         outs = call(
-            lambda *refs, block=block, last=last: block_kernel(layout, rows, block, last, *refs),
-            [shape((atoms, channels), f32)] + ([] if last else [chunk] * layout.chunks),
-            [pltpu.VMEM((2 * waves, 2 * channels), bf16)],
+            lambda *refs, block=block, last=last: block_kernel(rows, len(late_order), block, last, *refs),
+            outputs,
+            scratch,
             block_limit,
             flops,
             *inputs,
+            out_space=pltpu.HBM if last else pltpu.VMEM,
         )
         current = outs[0]
-        parts = dict(zip(offsets, outs[1:]))
-    return current
+        if last:
+            return current
+        parts = dict(zip(far, outs[2:]))
+        outs = call(
+            lambda *refs: project_kernel(rows, *refs),
+            [chunk] * len(near),
+            [],
+            near_limit,
+            flops // 4,
+            near_table,
+            outs[1],
+        )
+        parts |= dict(zip(near, outs))
 
 
 def solution(mesh):
@@ -409,6 +472,4 @@
     def body(*arguments):
         return local(layout, *arguments)
 
-    return jax.shard_map(
-        body, mesh=mesh, in_specs=placed, out_specs=P(("outer", "atoms"), None), check_vma=False
-    )
+    return jax.shard_map(body, mesh=mesh, in_specs=placed, out_specs=P(("outer", "atoms"), None), check_vma=False)

time: 73.4 us -> 71.7 us (0.977)
  waiting for transfers between devices: 27.6 us -> 24.6 us
  Pallas kernels: 18.2 us -> 19.3 us
    ppermute x28, waiting for transfers between devices: 19 us -> 16.9 us  [send(): lax.ppermute(value, axes, [(i, self.moved(i, **d)) for i in range(count)])]
    pallas_call x5 -> x8, Pallas kernels: 18.2 us -> 19.3 us  [call(): pl.pallas_call(kernel, in_specs=[pl.BlockSpec(memory_space=space)] * len(...]
    ppermute x6, waiting for transfers between devices: 8.61 us -> 7.73 us  [exchange(): return lax.ppermute(value, axes, pairs)]
  transfers between devices with their start and end apart: 34 -> 34, of which waited for: 20 -> 15; matrix products, arithmetic and copies ran while one was open for 0% -> 0% of each run, Pallas kernels for 7% -> 12%
where the time goes in v3:
time: 71.7 us; the launch traced here: 71.6 us
  starting transfers between devices  27 us (38%)
  waiting for transfers between devices  24.6 us (34%)
  Pallas kernels  19.3 us (27%)
    pallas_call x8, Pallas kernels, call(): pl.pallas_call(kernel, in_specs=[pl.BlockSpec(memory_space=space)] * len(...  19.3 us
    ppermute x28, starting transfers between devices, send(): lax.ppermute(value, axes, [(i, self.moved(i, **d)) for i in range(count)])  18.1 us
    ppermute x28, waiting for transfers between devices, send(): lax.ppermute(value, axes, [(i, self.moved(i, **d)) for i in range(count)])  16.9 us
    ppermute x6, starting transfers between devices, exchange(): return lax.ppermute(value, axes, pairs)  8.9 us
    ppermute x6, waiting for transfers between devices, exchange(): return lax.ppermute(value, axes, pairs)  7.73 us
  transfers between devices with their start and end apart: 34, of which 15 were waited for; matrix products, arithmetic and copies ran while one was open for 0% of the time, Pallas kernels for 12%

profile of v3, /device:TPU:0, one launch (start us, length us, event | category | flops | bytes accessed | tf_op | source)
XLA Modules:
  0.0 71.6 jit_solution(15820125883725658075)
XLA Ops:
  0.0 4.7 %shard_map.91 = (bf16[6,384,1024]{2,1,0:T(8,128)(2,1)S(1)}, bf16[1024,256]{1,0:T(8,128)(2,1)S(1)}, f32[192,1024]{1,0:T(8,128)S(1)}, f32[192,128]{1,0:T(8,128)S(1...) custom-call(s32[3,768]{1,0:T(4,128)} %refs_0_.3, ...), custom_call_target="tpu_custom_call" | custom-call | flops 1207959552 | bytes 6039797 | tf_op jit(solution)/shard_map/pallas_call | solution.py:340
  4.7 0.6 collective-permute-start.1
  5.4 0.4 collective-permute-start.5
  5.8 1.1 %shard_map.92 = (bf16[2,384,1024]{2,1,0:T(8,128)(2,1)S(1)}, f32[192,128]{1,0:T(8,128)S(1)}, f32[192,128]{1,0:T(8,128)S(1)}) custom-call(f32[192,1024]{1,0:T(8,128)S(1)} %get-tuple-element.31.refs_0_, bf16[1024,256]{1,0:T(8,128)(2,1)S(1)} %get-tuple-element.32.refs_1_), custom_call_target="tpu_custom_call" | custom-call | flops 301989888 | bytes 1509949 | tf_op jit(solution)/shard_map/pallas_call | solution.py:340
  6.9 0.1 collective-permute-start
  7.0 3.0 %collective-permute-start.2 = (f32[192,128]{1,0:T(8,128)S(1)}, f32[192,128]{1,0:T(8,128)S(1)}, u32[]{:S(2)}, u32[]{:S(2)}) collective-permute-start(f32[192,128]{1,0:T(8,128)S(1)} %add.61), channel_id=1, source_target_pairs={{0,1},{1,0},{2,3},{3,2},{4,5},{5,4},{6,7},{7,6},{8,9},{9,8},{10,11... | collective-permute-start | bytes 294920 | tf_op jit(solution)/shard_map/ppermute | solution.py:46
  10.0 1.6 %collective-permute-start.4 = (f32[192,128]{1,0:T(8,128)S(1)}, f32[192,128]{1,0:T(8,128)S(1)}, u32[]{:S(2)}, u32[]{:S(2)}) collective-permute-start(f32[192,128]{1,0:T(8,128)S(1)} %add.63), channel_id=1, source_target_pairs={{0,16},{1,17},{2,18},{3,19},{4,20},{5,21},{6,22},{7,23},{8,24},{9,... | collective-permute-start | bytes 294920 | tf_op jit(solution)/shard_map/ppermute | solution.py:46
  11.7 1.3 %collective-permute-done.2 = f32[192,128]{1,0:T(8,128)S(1)} collective-permute-done((f32[192,128]{1,0:T(8,128)S(1)}, f32[192,128]{1,0:T(8,128)S(1)}, u32[]{:S(2)}, u32[]{:S(2)}) %collective-permute-start.2) | collective-permute-done | bytes 98336 | tf_op jit(solution)/shard_map/ppermute | solution.py:46
  13.0 2.8 %collective-permute-done.4 = f32[192,128]{1,0:T(8,128)S(1)} collective-permute-done((f32[192,128]{1,0:T(8,128)S(1)}, f32[192,128]{1,0:T(8,128)S(1)}, u32[]{:S(2)}, u32[]{:S(2)}) %collective-permute-start.4) | collective-permute-done | bytes 98336 | tf_op jit(solution)/shard_map/ppermute | solution.py:46
  15.9 1.3 %collective-permute-done.6 = f32[192,128]{1,0:T(8,128)S(1)} collective-permute-done((f32[192,128]{1,0:T(8,128)S(1)}, f32[192,128]{1,0:T(8,128)S(1)}, u32[]{:S(2)}, u32[]{:S(2)}) %collective-permute-start.6) | collective-permute-done | bytes 98336 | tf_op jit(solution)/shard_map/ppermute | solution.py:46
  17.2 1.6 %collective-permute-start.9 = (f32[192,128]{1,0:T(8,128)S(1)}, f32[192,128]{1,0:T(8,128)S(1)}, u32[]{:S(2)}, u32[]{:S(2)}) collective-permute-start(f32[192,128]{1,0:T(8,128)S(1)} %add_add_fusion.1), channel_id=1, source_target_pairs={{0,2},{1,3},{2,0},{3,1},{4,6},{5,7},{6,4},{7,5},{8,10},{9,11},{10,... | collective-permute-start | bytes 294920 | tf_op jit(solution)/shard_map/ppermute | solution.py:54
  18.9 2.6 %collective-permute-start.8 = (f32[192,128]{1,0:T(8,128)S(1)}, f32[192,128]{1,0:T(8,128)S(1)}, u32[]{:S(2)}, u32[]{:S(2)}) collective-permute-start(f32[192,128]{1,0:T(8,128)S(1)} %add_add_fusion.1), channel_id=1, source_target_pairs={{0,4},{1,5},{2,6},{3,7},{4,0},{5,1},{6,2},{7,3},{8,12},{9,13},{10,... | collective-permute-start | bytes 294920 | tf_op jit(solution)/shard_map/ppermute | solution.py:54
  21.5 0.2 collective-permute-start.7
  21.7 5.0 %shard_map.93 = (bf16[4,512,768]{2,1,0:T(8,128)(2,1)S(1)}, bf16[4,512,768]{2,1,0:T(8,128)(2,1)S(1)}, f32[192,128]{1,0:T(8,128)S(1)}, f32[192,128]{1,0:T(8,128)S(1)}) custom-call(s32[3,768]{1,0:T(4,128)S(1)} %copy-done.8, s32[3,1024]{1,0:T(4,128)S(1)} %copy-done.7, f32[2,768,128]{2,1,0:T(8,128)S(1)} %copy-done.6), custom_call_target="tpu_custom_call" | custom-call | flops 1207959552 | bytes 6039797 | tf_op jit(solution)/shard_map/pallas_call | solution.py:340
  26.8 1.2 %collective-permute-done.7 = f32[192,128]{1,0:T(8,128)S(1)} collective-permute-done((f32[192,128]{1,0:T(8,128)S(1)}, f32[192,128]{1,0:T(8,128)S(1)}, u32[]{:S(2)}, u32[]{:S(2)}) %collective-permute-start.7) | collective-permute-done | bytes 98336 | tf_op jit(solution)/shard_map/ppermute | solution.py:54
  28.0 1.3 %collective-permute-start.14 = (f32[192,128]{1,0:T(8,128)S(1)}, f32[192,128]{1,0:T(8,128)S(1)}, u32[]{:S(2)}, u32[]{:S(2)}) collective-permute-start(f32[192,128]{1,0:T(8,128)S(1)} %add_multiply_fusion.1.refs_0_), channel_id=1, source_target_pairs={{0,17},{1,16},{2,19},{3,18},{4,21},{5,20},{6,23},{7,22},{8,25},{9,... | collective-permute-start | bytes 294920 | tf_op jit(solution)/shard_map/ppermute | solution.py:46
  29.3 1.5 %collective-permute-start.11 = (f32[192,128]{1,0:T(8,128)S(1)}, f32[192,128]{1,0:T(8,128)S(1)}, u32[]{:S(2)}, u32[]{:S(2)}) collective-permute-start(f32[192,128]{1,0:T(8,128)S(1)} %add_multiply_fusion.1.refs_0_), channel_id=1, source_target_pairs={{0,16},{1,17},{2,18},{3,19},{4,20},{5,21},{6,22},{7,23},{8,24},{9,... | collective-permute-start | bytes 294920 | tf_op jit(solution)/shard_map/ppermute | solution.py:46
  30.8 0.8 %collective-permute-start.10 = (f32[192,128]{1,0:T(8,128)S(1)}, f32[192,128]{1,0:T(8,128)S(1)}, u32[]{:S(2)}, u32[]{:S(2)}) collective-permute-start(f32[192,128]{1,0:T(8,128)S(1)} %add_multiply_fusion.1.refs_0_), channel_id=1, source_target_pairs={{0,1},{1,0},{2,3},{3,2},{4,5},{5,4},{6,7},{7,6},{8,9},{9,8},{10,11... | collective-permute-start | bytes 294920 | tf_op jit(solution)/shard_map/ppermute | solution.py:46
  31.6 2.1 %collective-permute-done.14.refs_1_ = f32[192,128]{1,0:T(8,128)S(1)} collective-permute-done((f32[192,128]{1,0:T(8,128)S(1)}, f32[192,128]{1,0:T(8,128)S(1)}, u32[]{:S(2)}, u32[]{:S(2)}) %collective-permute-start.14) | collective-permute-done | bytes 98336 | tf_op jit(solution)/shard_map/ppermute | solution.py:46
  33.7 1.0 %collective-permute-done.11.refs_1_ = f32[192,128]{1,0:T(8,128)S(1)} collective-permute-done((f32[192,128]{1,0:T(8,128)S(1)}, f32[192,128]{1,0:T(8,128)S(1)}, u32[]{:S(2)}, u32[]{:S(2)}) %collective-permute-start.11) | collective-permute-done | bytes 98336 | tf_op jit(solution)/shard_map/ppermute | solution.py:46
  34.6 0.8 %collective-permute-done.10.refs_0_ = f32[192,128]{1,0:T(8,128)S(1)} collective-permute-done((f32[192,128]{1,0:T(8,128)S(1)}, f32[192,128]{1,0:T(8,128)S(1)}, u32[]{:S(2)}, u32[]{:S(2)}) %collective-permute-start.10) | collective-permute-done | bytes 98336 | tf_op jit(solution)/shard_map/ppermute | solution.py:46
  35.4 1.0 %shard_map.94.refs_5_ = f32[1024,128]{1,0:T(8,128)S(1)} custom-call(f32[192,128]{1,0:T(8,128)S(1)} %add_multiply_fusion.1.refs_0_, f32[192,128]{1,0:T(8,128)S(1)} %collective-permute-done.14.refs_1_, f32[192,128]{1,0:T(8,128)S(1)} %collective-permute-done.15.refs_2_, f32[192,128]{1,0:T(8,128)S(1)} %collective-permute-done.16.refs_3_, ...), custom_call_target="tpu_custom_call" | custom-call | flops 603979776 | bytes 3019898 | tf_op jit(solution)/shard_map/pallas_call | solution.py:340
  36.5 0.3 collective-permute-done.12.refs_2_
  36.7 3.3 %shard_map.95 = (f32[1024,128]{1,0:T(8,128)S(1)}, bf16[1024,256]{1,0:T(8,128)(2,1)S(1)}, f32[192,128]{1,0:T(8,128)S(1)}, f32[192,128]{1,0:T(8,128)S(1)}, f32[192...) custom-call(f32[192,128]{1,0:T(8,128)S(1)} %collective-permute-done.10.refs_0_, ...), custom_call_target="tpu_custom_call" | custom-call | flops 1207959552 | bytes 6039797 | tf_op jit(solution)/shard_map/pallas_call | solution.py:340
  40.0 0.3 collective-permute-start.18
  40.4 0.2 collective-permute-start.20
  40.6 0.3 collective-permute-start.22
  40.9 0.6 shard_map.96
  41.5 0.3 collective-permute-start.17
  41.8 0.8 %collective-permute-start.19 = (f32[192,128]{1,0:T(8,128)S(1)}, f32[192,128]{1,0:T(8,128)S(1)}, u32[]{:S(2)}, u32[]{:S(2)}) collective-permute-start(f32[192,128]{1,0:T(8,128)S(1)} %add.71), channel_id=1, source_target_pairs={{0,1},{1,0},{2,3},{3,2},{4,5},{5,4},{6,7},{7,6},{8,9},{9,8},{10,11... | collective-permute-start | bytes 294920 | tf_op jit(solution)/shard_map/ppermute | solution.py:46
  42.6 1.2 %collective-permute-start.21 = (f32[192,128]{1,0:T(8,128)S(1)}, f32[192,128]{1,0:T(8,128)S(1)}, u32[]{:S(2)}, u32[]{:S(2)}) collective-permute-start(f32[192,128]{1,0:T(8,128)S(1)} %add.73), channel_id=1, source_target_pairs={{0,16},{1,17},{2,18},{3,19},{4,20},{5,21},{6,22},{7,23},{8,24},{9,... | collective-permute-start | bytes 294920 | tf_op jit(solution)/shard_map/ppermute | solution.py:46
  43.8 1.7 %collective-permute-start.23 = (f32[192,128]{1,0:T(8,128)S(1)}, f32[192,128]{1,0:T(8,128)S(1)}, u32[]{:S(2)}, u32[]{:S(2)}) collective-permute-start(f32[192,128]{1,0:T(8,128)S(1)} %add.75), channel_id=1, source_target_pairs={{0,17},{1,16},{2,19},{3,18},{4,21},{5,20},{6,23},{7,22},{8,25},{9,... | collective-permute-start | bytes 294920 | tf_op jit(solution)/shard_map/ppermute | solution.py:46
  45.5 1.6 %collective-permute-done.19 = f32[192,128]{1,0:T(8,128)S(1)} collective-permute-done((f32[192,128]{1,0:T(8,128)S(1)}, f32[192,128]{1,0:T(8,128)S(1)}, u32[]{:S(2)}, u32[]{:S(2)}) %collective-permute-start.19) | collective-permute-done | bytes 98336 | tf_op jit(solution)/shard_map/ppermute | solution.py:46
  47.1 2.4 %collective-permute-done.21 = f32[192,128]{1,0:T(8,128)S(1)} collective-permute-done((f32[192,128]{1,0:T(8,128)S(1)}, f32[192,128]{1,0:T(8,128)S(1)}, u32[]{:S(2)}, u32[]{:S(2)}) %collective-permute-start.21) | collective-permute-done | bytes 98336 | tf_op jit(solution)/shard_map/ppermute | solution.py:46
  49.5 1.5 %collective-permute-start.26 = (f32[192,128]{1,0:T(8,128)S(1)}, f32[192,128]{1,0:T(8,128)S(1)}, u32[]{:S(2)}, u32[]{:S(2)}) collective-permute-start(f32[192,128]{1,0:T(8,128)S(1)} %add_add_fusion), channel_id=1, source_target_pairs={{0,2},{1,3},{2,0},{3,1},{4,6},{5,7},{6,4},{7,5},{8,10},{9,11},{10,... | collective-permute-start | bytes 294920 | tf_op jit(solution)/shard_map/ppermute | solution.py:54
  51.1 1.6 %collective-permute-start.25 = (f32[192,128]{1,0:T(8,128)S(1)}, f32[192,128]{1,0:T(8,128)S(1)}, u32[]{:S(2)}, u32[]{:S(2)}) collective-permute-start(f32[192,128]{1,0:T(8,128)S(1)} %add_add_fusion), channel_id=1, source_target_pairs={{0,4},{1,5},{2,6},{3,7},{4,0},{5,1},{6,2},{7,3},{8,12},{9,13},{10,... | collective-permute-start | bytes 294920 | tf_op jit(solution)/shard_map/ppermute | solution.py:54
  52.6 1.3 %collective-permute-start.24 = (f32[192,128]{1,0:T(8,128)S(1)}, f32[192,128]{1,0:T(8,128)S(1)}, u32[]{:S(2)}, u32[]{:S(2)}) collective-permute-start(f32[192,128]{1,0:T(8,128)S(1)} %add_add_fusion), channel_id=1, source_target_pairs={{0,6},{1,7},{2,4},{3,5},{4,2},{5,3},{6,0},{7,1},{8,14},{9,15},{10,... | collective-permute-start | bytes 294920 | tf_op jit(solution)/shard_map/ppermute | solution.py:54
  54.0 0.9 %collective-permute-done.26 = f32[192,128]{1,0:T(8,128)S(1)} collective-permute-done((f32[192,128]{1,0:T(8,128)S(1)}, f32[192,128]{1,0:T(8,128)S(1)}, u32[]{:S(2)}, u32[]{:S(2)}) %collective-permute-start.26) | collective-permute-done | bytes 98336 | tf_op jit(solution)/shard_map/ppermute | solution.py:54
  54.9 5.7 %collective-permute-done.25 = f32[192,128]{1,0:T(8,128)S(1)} collective-permute-done((f32[192,128]{1,0:T(8,128)S(1)}, f32[192,128]{1,0:T(8,128)S(1)}, u32[]{:S(2)}, u32[]{:S(2)}) %collective-permute-start.25) | collective-permute-done | bytes 98336 | tf_op jit(solution)/shard_map/ppermute | solution.py:54
  60.6 1.5 %collective-permute-start.31 = (f32[192,128]{1,0:T(8,128)S(1)}, f32[192,128]{1,0:T(8,128)S(1)}, u32[]{:S(2)}, u32[]{:S(2)}) collective-permute-start(f32[192,128]{1,0:T(8,128)S(1)} %add_multiply_fusion.refs_0_), channel_id=1, source_target_pairs={{0,17},{1,16},{2,19},{3,18},{4,21},{5,20},{6,23},{7,22},{8,25},{9,... | collective-permute-start | bytes 294920 | tf_op jit(solution)/shard_map/ppermute | solution.py:46
  62.1 0.7 %collective-permute-start.28 = (f32[192,128]{1,0:T(8,128)S(1)}, f32[192,128]{1,0:T(8,128)S(1)}, u32[]{:S(2)}, u32[]{:S(2)}) collective-permute-start(f32[192,128]{1,0:T(8,128)S(1)} %add_multiply_fusion.refs_0_), channel_id=1, source_target_pairs={{0,16},{1,17},{2,18},{3,19},{4,20},{5,21},{6,22},{7,23},{8,24},{9,... | collective-permute-start | bytes 294920 | tf_op jit(solution)/shard_map/ppermute | solution.py:46
  62.8 1.3 %collective-permute-start.27 = (f32[192,128]{1,0:T(8,128)S(1)}, f32[192,128]{1,0:T(8,128)S(1)}, u32[]{:S(2)}, u32[]{:S(2)}) collective-permute-start(f32[192,128]{1,0:T(8,128)S(1)} %add_multiply_fusion.refs_0_), channel_id=1, source_target_pairs={{0,1},{1,0},{2,3},{3,2},{4,5},{5,4},{6,7},{7,6},{8,9},{9,8},{10,11... | collective-permute-start | bytes 294920 | tf_op jit(solution)/shard_map/ppermute | solution.py:46
  64.2 2.1 %collective-permute-done.31.refs_1_ = f32[192,128]{1,0:T(8,128)S(1)} collective-permute-done((f32[192,128]{1,0:T(8,128)S(1)}, f32[192,128]{1,0:T(8,128)S(1)}, u32[]{:S(2)}, u32[]{:S(2)}) %collective-permute-start.31) | collective-permute-done | bytes 98336 | tf_op jit(solution)/shard_map/ppermute | solution.py:46
  66.2 1.0 %collective-permute-done.28.refs_1_ = f32[192,128]{1,0:T(8,128)S(1)} collective-permute-done((f32[192,128]{1,0:T(8,128)S(1)}, f32[192,128]{1,0:T(8,128)S(1)}, u32[]{:S(2)}, u32[]{:S(2)}) %collective-permute-start.28) | collective-permute-done | bytes 98336 | tf_op jit(solution)/shard_map/ppermute | solution.py:46
  67.2 0.2 collective-permute-done.27.refs_0_
  67.4 0.3 collective-permute-start.29
  67.7 1.0 %shard_map.97.refs_5_ = f32[1024,128]{1,0:T(8,128)S(1)} custom-call(f32[192,128]{1,0:T(8,128)S(1)} %add_multiply_fusion.refs_0_, f32[192,128]{1,0:T(8,128)S(1)} %collective-permute-done.31.refs_1_, f32[192,128]{1,0:T(8,128)S(1)} %collective-permute-done.32.refs_2_, f32[192,128]{1,0:T(8,128)S(1)} %collective-permute-done.33.refs_3_, ...), custom_call_target="tpu_custom_call" | custom-call | flops 603979776 | bytes 3019898 | tf_op jit(solution)/shard_map/pallas_call | solution.py:340
  68.8 2.6 %shard_map.98 = f32[1024,128]{1,0:T(8,128)} custom-call(f32[192,128]{1,0:T(8,128)S(1)} %collective-permute-done.27.refs_0_, f32[192,128]{1,0:T(8,128)S(1)} %collective-permute-done.28.refs_1_, f32[192,128]{1,0:T(8,128)S(1)} %collective-permute-done.29.refs_2_, f32[192,128]{1,0:T(8,128)S(1)} %collective-permute-done.30.refs_3_, ...), custom_call_target="tpu_custom_call" | custom-call | flops 1207959552 | bytes 6039797 | tf_op jit(solution)/shard_map/pallas_call | solution.py:340
  (56 shorter events, 0.5 us)
Async XLA Ops:
  0.0 21.7 %copy-start.8 = (s32[3,768]{1,0:T(4,128)S(1)}, s32[3,768]{1,0:T(4,128)}, u32[]{:S(2)}) copy-start(s32[3,768]{1,0:T(4,128)} %refs_0_.3) | copy-start | bytes 27652
  0.0 21.7 %copy-start.7 = (s32[3,1024]{1,0:T(4,128)S(1)}, s32[3,1024]{1,0:T(4,128)}, u32[]{:S(2)}) copy-start(s32[3,1024]{1,0:T(4,128)} %refs_1_.3) | copy-start | bytes 36868
  0.0 21.7 %copy-start.6 = (f32[2,768,128]{2,1,0:T(8,128)S(1)}, f32[2,768,128]{2,1,0:T(8,128)}, u32[]{:S(2)}) copy-start(f32[2,768,128]{2,1,0:T(8,128)} %refs_2_.3) | copy-start | bytes 2359300
  4.7 2.3 %collective-permute-start.1 = (f32[192,128]{1,0:T(8,128)S(1)}, f32[192,128]{1,0:T(8,128)S(1)}, u32[]{:S(2)}, u32[]{:S(2)}) collective-permute-start(f32[192,128]{1,0:T(8,128)S(1)} %get-tuple-element.37), channel_id=1, source_target_pairs={{0,8},{1,9},{2,10},{3,11},{4,12},{5,13},{6,14},{7,15},{8,0},{9,1},... | collective-permute-start | bytes 294920 | tf_op jit(solution)/shard_map/ppermute | solution.py:46
  5.3 4.7 %collective-permute-start.3 = (f32[192,128]{1,0:T(8,128)S(1)}, f32[192,128]{1,0:T(8,128)S(1)}, u32[]{:S(2)}, u32[]{:S(2)}) collective-permute-start(f32[192,128]{1,0:T(8,128)S(1)} %get-tuple-element.39), channel_id=1, source_target_pairs={{0,8},{1,9},{2,10},{3,11},{4,12},{5,13},{6,14},{7,15},{8,0},{9,1},... | collective-permute-start | bytes 294920 | tf_op jit(solution)/shard_map/ppermute | solution.py:46
  5.4 6.2 %collective-permute-start.5 = (f32[192,128]{1,0:T(8,128)S(1)}, f32[192,128]{1,0:T(8,128)S(1)}, u32[]{:S(2)}, u32[]{:S(2)}) collective-permute-start(f32[192,128]{1,0:T(8,128)S(1)} %get-tuple-element.41), channel_id=1, source_target_pairs={{0,8},{1,9},{2,10},{3,11},{4,12},{5,13},{6,14},{7,15},{8,0},{9,1},... | collective-permute-start | bytes 294920 | tf_op jit(solution)/shard_map/ppermute | solution.py:46
  6.9 4.8 %collective-permute-start = (f32[192,128]{1,0:T(8,128)S(1)}, f32[192,128]{1,0:T(8,128)S(1)}, u32[]{:S(2)}, u32[]{:S(2)}) collective-permute-start(f32[192,128]{1,0:T(8,128)S(1)} %get-tuple-element.35), channel_id=1, source_target_pairs={{0,8},{1,9},{2,10},{3,11},{4,12},{5,13},{6,14},{7,15},{8,0},{9,1},... | collective-permute-start | bytes 294920 | tf_op jit(solution)/shard_map/ppermute | solution.py:46
  7.0 6.0 %collective-permute-start.2 = (f32[192,128]{1,0:T(8,128)S(1)}, f32[192,128]{1,0:T(8,128)S(1)}, u32[]{:S(2)}, u32[]{:S(2)}) collective-permute-start(f32[192,128]{1,0:T(8,128)S(1)} %add.61), channel_id=1, source_target_pairs={{0,1},{1,0},{2,3},{3,2},{4,5},{5,4},{6,7},{7,6},{8,9},{9,8},{10,11... | collective-permute-start | bytes 294920 | tf_op jit(solution)/shard_map/ppermute | solution.py:46
  10.0 5.9 %collective-permute-start.4 = (f32[192,128]{1,0:T(8,128)S(1)}, f32[192,128]{1,0:T(8,128)S(1)}, u32[]{:S(2)}, u32[]{:S(2)}) collective-permute-start(f32[192,128]{1,0:T(8,128)S(1)} %add.63), channel_id=1, source_target_pairs={{0,16},{1,17},{2,18},{3,19},{4,20},{5,21},{6,22},{7,23},{8,24},{9,... | collective-permute-start | bytes 294920 | tf_op jit(solution)/shard_map/ppermute | solution.py:46
  11.6 5.6 %collective-permute-start.6 = (f32[192,128]{1,0:T(8,128)S(1)}, f32[192,128]{1,0:T(8,128)S(1)}, u32[]{:S(2)}, u32[]{:S(2)}) collective-permute-start(f32[192,128]{1,0:T(8,128)S(1)} %add.65), channel_id=1, source_target_pairs={{0,17},{1,16},{2,19},{3,18},{4,21},{5,20},{6,23},{7,22},{8,25},{9,... | collective-permute-start | bytes 294920 | tf_op jit(solution)/shard_map/ppermute | solution.py:46
  17.2 9.6 %collective-permute-start.9 = (f32[192,128]{1,0:T(8,128)S(1)}, f32[192,128]{1,0:T(8,128)S(1)}, u32[]{:S(2)}, u32[]{:S(2)}) collective-permute-start(f32[192,128]{1,0:T(8,128)S(1)} %add_add_fusion.1), channel_id=1, source_target_pairs={{0,2},{1,3},{2,0},{3,1},{4,6},{5,7},{6,4},{7,5},{8,10},{9,11},{10,... | collective-permute-start | bytes 294920 | tf_op jit(solution)/shard_map/ppermute | solution.py:54
  18.9 8.0 %collective-permute-start.8 = (f32[192,128]{1,0:T(8,128)S(1)}, f32[192,128]{1,0:T(8,128)S(1)}, u32[]{:S(2)}, u32[]{:S(2)}) collective-permute-start(f32[192,128]{1,0:T(8,128)S(1)} %add_add_fusion.1), channel_id=1, source_target_pairs={{0,4},{1,5},{2,6},{3,7},{4,0},{5,1},{6,2},{7,3},{8,12},{9,13},{10,... | collective-permute-start | bytes 294920 | tf_op jit(solution)/shard_map/ppermute | solution.py:54
  21.5 6.5 %collective-permute-start.7 = (f32[192,128]{1,0:T(8,128)S(1)}, f32[192,128]{1,0:T(8,128)S(1)}, u32[]{:S(2)}, u32[]{:S(2)}) collective-permute-start(f32[192,128]{1,0:T(8,128)S(1)} %add_add_fusion.1), channel_id=1, source_target_pairs={{0,6},{1,7},{2,4},{3,5},{4,2},{5,3},{6,0},{7,1},{8,14},{9,15},{10,... | collective-permute-start | bytes 294920 | tf_op jit(solution)/shard_map/ppermute | solution.py:54
  26.7 10.0 %copy-start = (f32[2,128,128]{2,1,0:T(8,128)S(1)}, f32[2,128,128]{2,1,0:T(8,128)}, u32[]{:S(2)}) copy-start(f32[2,128,128]{2,1,0:T(8,128)} %refs_8_.3) | copy-start | bytes 393220
  26.7 10.0 %copy-start.1 = (f32[2,128,128]{2,1,0:T(8,128)S(1)}, f32[2,128,128]{2,1,0:T(8,128)}, u32[]{:S(2)}) copy-start(f32[2,128,128]{2,1,0:T(8,128)} %refs_10_.3) | copy-start | bytes 393220
  26.7 10.0 %copy-start.2 = (f32[1024,128]{1,0:T(8,128)S(1)}, f32[1024,128]{1,0:T(8,128)}, u32[]{:S(2)}) copy-start(f32[1024,128]{1,0:T(8,128)} %refs_6_.1) | copy-start | bytes 1572868
  26.8 10.0 %copy-start.3 = (f32[2,128,128]{2,1,0:T(8,128)S(1)}, f32[2,128,128]{2,1,0:T(8,128)}, u32[]{:S(2)}) copy-start(f32[2,128,128]{2,1,0:T(8,128)} %refs_11_.1) | copy-start | bytes 393220
  26.8 10.0 %copy-start.4 = (f32[2,128]{1,0:T(2,128)S(1)}, f32[2,128]{1,0:T(2,128)}, u32[]{:S(2)}) copy-start(f32[2,128]{1,0:T(2,128)} %refs_7_.3) | copy-start | bytes 3076
  26.8 10.0 %copy-start.5 = (f32[2,128]{1,0:T(2,128)S(1)}, f32[2,128]{1,0:T(2,128)}, u32[]{:S(2)}) copy-start(f32[2,128]{1,0:T(2,128)} %refs_9_.3) | copy-start | bytes 3076
  28.0 5.7 %collective-permute-start.14 = (f32[192,128]{1,0:T(8,128)S(1)}, f32[192,128]{1,0:T(8,128)S(1)}, u32[]{:S(2)}, u32[]{:S(2)}) collective-permute-start(f32[192,128]{1,0:T(8,128)S(1)} %add_multiply_fusion.1.refs_0_), channel_id=1, source_target_pairs={{0,17},{1,16},{2,19},{3,18},{4,21},{5,20},{6,23},{7,22},{8,25},{9,... | collective-permute-start | bytes 294920 | tf_op jit(solution)/shard_map/ppermute | solution.py:46
  29.3 5.4 %collective-permute-start.11 = (f32[192,128]{1,0:T(8,128)S(1)}, f32[192,128]{1,0:T(8,128)S(1)}, u32[]{:S(2)}, u32[]{:S(2)}) collective-permute-start(f32[192,128]{1,0:T(8,128)S(1)} %add_multiply_fusion.1.refs_0_), channel_id=1, source_target_pairs={{0,16},{1,17},{2,18},{3,19},{4,20},{5,21},{6,22},{7,23},{8,24},{9,... | collective-permute-start | bytes 294920 | tf_op jit(solution)/shard_map/ppermute | solution.py:46
  30.8 4.6 %collective-permute-start.10 = (f32[192,128]{1,0:T(8,128)S(1)}, f32[192,128]{1,0:T(8,128)S(1)}, u32[]{:S(2)}, u32[]{:S(2)}) collective-permute-start(f32[192,128]{1,0:T(8,128)S(1)} %add_multiply_fusion.1.refs_0_), channel_id=1, source_target_pairs={{0,1},{1,0},{2,3},{3,2},{4,5},{5,4},{6,7},{7,6},{8,9},{9,8},{10,11... | collective-permute-start | bytes 294920 | tf_op jit(solution)/shard_map/ppermute | solution.py:46
  31.6 3.9 %collective-permute-start.15 = (f32[192,128]{1,0:T(8,128)S(1)}, f32[192,128]{1,0:T(8,128)S(1)}, u32[]{:S(2)}, u32[]{:S(2)}) collective-permute-start(f32[192,128]{1,0:T(8,128)S(1)} %add_multiply_fusion.1.refs_0_), channel_id=1, source_target_pairs={{0,8},{1,9},{2,10},{3,11},{4,12},{5,13},{6,14},{7,15},{8,0},{9,1},... | collective-permute-start | bytes 294920 | tf_op jit(solution)/shard_map/ppermute | solution.py:46
  33.7 1.7 %collective-permute-start.16 = (f32[192,128]{1,0:T(8,128)S(1)}, f32[192,128]{1,0:T(8,128)S(1)}, u32[]{:S(2)}, u32[]{:S(2)}) collective-permute-start(f32[192,128]{1,0:T(8,128)S(1)} %collective-permute-done.14.refs_1_), channel_id=1, source_target_pairs={{0,8},{1,9},{2,10},{3,11},{4,12},{5,13},{6,14},{7,15},{8,0},{9,1},... | collective-permute-start | bytes 294920 | tf_op jit(solution)/shard_map/ppermute | solution.py:46
  34.6 1.8 %collective-permute-start.13 = (f32[192,128]{1,0:T(8,128)S(1)}, f32[192,128]{1,0:T(8,128)S(1)}, u32[]{:S(2)}, u32[]{:S(2)}) collective-permute-start(f32[192,128]{1,0:T(8,128)S(1)} %collective-permute-done.11.refs_1_), channel_id=1, source_target_pairs={{0,8},{1,9},{2,10},{3,11},{4,12},{5,13},{6,14},{7,15},{8,0},{9,1},... | collective-permute-start | bytes 294920 | tf_op jit(solution)/shard_map/ppermute | solution.py:46
  35.4 1.3 %collective-permute-start.12 = (f32[192,128]{1,0:T(8,128)S(1)}, f32[192,128]{1,0:T(8,128)S(1)}, u32[]{:S(2)}, u32[]{:S(2)}) collective-permute-start(f32[192,128]{1,0:T(8,128)S(1)} %collective-permute-done.10.refs_0_), channel_id=1, source_target_pairs={{0,8},{1,9},{2,10},{3,11},{4,12},{5,13},{6,14},{7,15},{8,0},{9,1},... | collective-permute-start | bytes 294920 | tf_op jit(solution)/shard_map/ppermute | solution.py:46
  40.0 1.7 %collective-permute-start.18 = (f32[192,128]{1,0:T(8,128)S(1)}, f32[192,128]{1,0:T(8,128)S(1)}, u32[]{:S(2)}, u32[]{:S(2)}) collective-permute-start(f32[192,128]{1,0:T(8,128)S(1)} %get-tuple-element.50), channel_id=1, source_target_pairs={{0,8},{1,9},{2,10},{3,11},{4,12},{5,13},{6,14},{7,15},{8,0},{9,1},... | collective-permute-start | bytes 294920 | tf_op jit(solution)/shard_map/ppermute | solution.py:46
  40.4 2.3 %collective-permute-start.20 = (f32[192,128]{1,0:T(8,128)S(1)}, f32[192,128]{1,0:T(8,128)S(1)}, u32[]{:S(2)}, u32[]{:S(2)}) collective-permute-start(f32[192,128]{1,0:T(8,128)S(1)} %get-tuple-element.52), channel_id=1, source_target_pairs={{0,8},{1,9},{2,10},{3,11},{4,12},{5,13},{6,14},{7,15},{8,0},{9,1},... | collective-permute-start | bytes 294920 | tf_op jit(solution)/shard_map/ppermute | solution.py:46
  40.6 3.2 %collective-permute-start.22 = (f32[192,128]{1,0:T(8,128)S(1)}, f32[192,128]{1,0:T(8,128)S(1)}, u32[]{:S(2)}, u32[]{:S(2)}) collective-permute-start(f32[192,128]{1,0:T(8,128)S(1)} %get-tuple-element.54), channel_id=1, source_target_pairs={{0,8},{1,9},{2,10},{3,11},{4,12},{5,13},{6,14},{7,15},{8,0},{9,1},... | collective-permute-start | bytes 294920 | tf_op jit(solution)/shard_map/ppermute | solution.py:46
  41.5 4.0 %collective-permute-start.17 = (f32[192,128]{1,0:T(8,128)S(1)}, f32[192,128]{1,0:T(8,128)S(1)}, u32[]{:S(2)}, u32[]{:S(2)}) collective-permute-start(f32[192,128]{1,0:T(8,128)S(1)} %get-tuple-element.48), channel_id=1, source_target_pairs={{0,8},{1,9},{2,10},{3,11},{4,12},{5,13},{6,14},{7,15},{8,0},{9,1},... | collective-permute-start | bytes 294920 | tf_op jit(solution)/shard_map/ppermute | solution.py:46
  41.8 5.3 %collective-permute-start.19 = (f32[192,128]{1,0:T(8,128)S(1)}, f32[192,128]{1,0:T(8,128)S(1)}, u32[]{:S(2)}, u32[]{:S(2)}) collective-permute-start(f32[192,128]{1,0:T(8,128)S(1)} %add.71), channel_id=1, source_target_pairs={{0,1},{1,0},{2,3},{3,2},{4,5},{5,4},{6,7},{7,6},{8,9},{9,8},{10,11... | collective-permute-start | bytes 294920 | tf_op jit(solution)/shard_map/ppermute | solution.py:46
  42.6 6.9 %collective-permute-start.21 = (f32[192,128]{1,0:T(8,128)S(1)}, f32[192,128]{1,0:T(8,128)S(1)}, u32[]{:S(2)}, u32[]{:S(2)}) collective-permute-start(f32[192,128]{1,0:T(8,128)S(1)} %add.73), channel_id=1, source_target_pairs={{0,16},{1,17},{2,18},{3,19},{4,20},{5,21},{6,22},{7,23},{8,24},{9,... | collective-permute-start | bytes 294920 | tf_op jit(solution)/shard_map/ppermute | solution.py:46
  43.8 5.7 %collective-permute-start.23 = (f32[192,128]{1,0:T(8,128)S(1)}, f32[192,128]{1,0:T(8,128)S(1)}, u32[]{:S(2)}, u32[]{:S(2)}) collective-permute-start(f32[192,128]{1,0:T(8,128)S(1)} %add.75), channel_id=1, source_target_pairs={{0,17},{1,16},{2,19},{3,18},{4,21},{5,20},{6,23},{7,22},{8,25},{9,... | collective-permute-start | bytes 294920 | tf_op jit(solution)/shard_map/ppermute | solution.py:46
  49.5 5.3 %collective-permute-start.26 = (f32[192,128]{1,0:T(8,128)S(1)}, f32[192,128]{1,0:T(8,128)S(1)}, u32[]{:S(2)}, u32[]{:S(2)}) collective-permute-start(f32[192,128]{1,0:T(8,128)S(1)} %add_add_fusion), channel_id=1, source_target_pairs={{0,2},{1,3},{2,0},{3,1},{4,6},{5,7},{6,4},{7,5},{8,10},{9,11},{10,... | collective-permute-start | bytes 294920 | tf_op jit(solution)/shard_map/ppermute | solution.py:54
  51.1 9.5 %collective-permute-start.25 = (f32[192,128]{1,0:T(8,128)S(1)}, f32[192,128]{1,0:T(8,128)S(1)}, u32[]{:S(2)}, u32[]{:S(2)}) collective-permute-start(f32[192,128]{1,0:T(8,128)S(1)} %add_add_fusion), channel_id=1, source_target_pairs={{0,4},{1,5},{2,6},{3,7},{4,0},{5,1},{6,2},{7,3},{8,12},{9,13},{10,... | collective-permute-start | bytes 294920 | tf_op jit(solution)/shard_map/ppermute | solution.py:54
  52.6 7.9 %collective-permute-start.24 = (f32[192,128]{1,0:T(8,128)S(1)}, f32[192,128]{1,0:T(8,128)S(1)}, u32[]{:S(2)}, u32[]{:S(2)}) collective-permute-start(f32[192,128]{1,0:T(8,128)S(1)} %add_add_fusion), channel_id=1, source_target_pairs={{0,6},{1,7},{2,4},{3,5},{4,2},{5,3},{6,0},{7,1},{8,14},{9,15},{10,... | collective-permute-start | bytes 294920 | tf_op jit(solution)/shard_map/ppermute | solution.py:54
  60.6 5.6 %collective-permute-start.31 = (f32[192,128]{1,0:T(8,128)S(1)}, f32[192,128]{1,0:T(8,128)S(1)}, u32[]{:S(2)}, u32[]{:S(2)}) collective-permute-start(f32[192,128]{1,0:T(8,128)S(1)} %add_multiply_fusion.refs_0_), channel_id=1, source_target_pairs={{0,17},{1,16},{2,19},{3,18},{4,21},{5,20},{6,23},{7,22},{8,25},{9,... | collective-permute-start | bytes 294920 | tf_op jit(solution)/shard_map/ppermute | solution.py:46
  62.1 5.1 %collective-permute-start.28 = (f32[192,128]{1,0:T(8,128)S(1)}, f32[192,128]{1,0:T(8,128)S(1)}, u32[]{:S(2)}, u32[]{:S(2)}) collective-permute-start(f32[192,128]{1,0:T(8,128)S(1)} %add_multiply_fusion.refs_0_), channel_id=1, source_target_pairs={{0,16},{1,17},{2,18},{3,19},{4,20},{5,21},{6,22},{7,23},{8,24},{9,... | collective-permute-start | bytes 294920 | tf_op jit(solution)/shard_map/ppermute | solution.py:46
  62.8 4.6 %collective-permute-start.27 = (f32[192,128]{1,0:T(8,128)S(1)}, f32[192,128]{1,0:T(8,128)S(1)}, u32[]{:S(2)}, u32[]{:S(2)}) collective-permute-start(f32[192,128]{1,0:T(8,128)S(1)} %add_multiply_fusion.refs_0_), channel_id=1, source_target_pairs={{0,1},{1,0},{2,3},{3,2},{4,5},{5,4},{6,7},{7,6},{8,9},{9,8},{10,11... | collective-permute-start | bytes 294920 | tf_op jit(solution)/shard_map/ppermute | solution.py:46
  64.1 3.6 %collective-permute-start.32 = (f32[192,128]{1,0:T(8,128)S(1)}, f32[192,128]{1,0:T(8,128)S(1)}, u32[]{:S(2)}, u32[]{:S(2)}) collective-permute-start(f32[192,128]{1,0:T(8,128)S(1)} %add_multiply_fusion.refs_0_), channel_id=1, source_target_pairs={{0,8},{1,9},{2,10},{3,11},{4,12},{5,13},{6,14},{7,15},{8,0},{9,1},... | collective-permute-start | bytes 294920 | tf_op jit(solution)/shard_map/ppermute | solution.py:46
  66.2 1.5 %collective-permute-start.33 = (f32[192,128]{1,0:T(8,128)S(1)}, f32[192,128]{1,0:T(8,128)S(1)}, u32[]{:S(2)}, u32[]{:S(2)}) collective-permute-start(f32[192,128]{1,0:T(8,128)S(1)} %collective-permute-done.31.refs_1_), channel_id=1, source_target_pairs={{0,8},{1,9},{2,10},{3,11},{4,12},{5,13},{6,14},{7,15},{8,0},{9,1},... | collective-permute-start | bytes 294920 | tf_op jit(solution)/shard_map/ppermute | solution.py:46
  67.2 1.5 %collective-permute-start.30 = (f32[192,128]{1,0:T(8,128)S(1)}, f32[192,128]{1,0:T(8,128)S(1)}, u32[]{:S(2)}, u32[]{:S(2)}) collective-permute-start(f32[192,128]{1,0:T(8,128)S(1)} %collective-permute-done.28.refs_1_), channel_id=1, source_target_pairs={{0,8},{1,9},{2,10},{3,11},{4,12},{5,13},{6,14},{7,15},{8,0},{9,1},... | collective-permute-start | bytes 294920 | tf_op jit(solution)/shard_map/ppermute | solution.py:46
  67.4 1.3 %collective-permute-start.29 = (f32[192,128]{1,0:T(8,128)S(1)}, f32[192,128]{1,0:T(8,128)S(1)}, u32[]{:S(2)}, u32[]{:S(2)}) collective-permute-start(f32[192,128]{1,0:T(8,128)S(1)} %collective-permute-done.27.refs_0_), channel_id=1, source_target_pairs={{0,8},{1,9},{2,10},{3,11},{4,12},{5,13},{6,14},{7,15},{8,0},{9,1},... | collective-permute-start | bytes 294920 | tf_op jit(solution)/shard_map/ppermute | solution.py:46
